TPU v7x, 256 devices: a whole 4x4x8 slice. The times are simulated.
256 devices in a mesh: group: 4 (over x), member: 64 (over z, y, core).
Axes of the slice: x: 4, y: 4, z: 8, core: 2. Of those that a mesh axis runs over, the one named last changes fastest.
Arguments:
- a_band: bfloat16 [49152, 3, 64, 64], P(('group', 'member')), as said below
- p_tent: bfloat16 [49152, 6, 64], P(('group', 'member')), may hold values from -0.8984375 to 0.8984375
- new_owner: int32 [49152], P(('group', 'member')), may hold values from 0 to 63, as said below
Outputs:
- p_smooth: bfloat16 [49152, 3, 6, 64], P(('group', 'member'))
- coarse: float32 [49152, 252], P(('group', 'member'))
Inputs may be any that keep to these rules, and one draw needn't show every extreme that they name: `new_owner`: within each group, every device sends between 1 and 6 of its block rows to every member of its group, exactly 6 to at least one member, and every member receives exactly 192 block rows. a_band[n, 1, i, i] lies between 2 and 6.
All inputs are finite; a program needn't handle non-finite values.
Results may differ from a plain program's by a relative error of at most 0.0027.
The roundings to bfloat16 on the way count: a program that leaves them out, or rounds other values in their place, can miss the bound.
Values may be sent and summed in bfloat16 or wider, within the bound.
No kernel may reach another device: no remote copies, remote signals or barrier semaphores. Data moves between devices by JAX's collectives and lax.ppermute only.
A program may use at most 128 MiB of HBM per device.

v0:
```python
import jax
import jax.numpy as jnp
from jax import lax
from jax.sharding import PartitionSpec as P


def extended(cells, sides, width):
    for axis, dim in sides:
        count = lax.axis_size(axis)
        ends = count - 1
        head = lax.slice_in_dim(cells, 0, width, axis=dim)
        tail = lax.slice_in_dim(cells, cells.shape[dim] - width, cells.shape[dim], axis=dim)
        cells = jnp.concatenate(
            [
                lax.ppermute(tail, axis, [(i, (i + 1) % count) for i in range(ends)]),
                cells,
                lax.ppermute(head, axis, [((i + 1) % count, i) for i in range(ends)]),
            ],
            axis=dim,
        )
    return cells


def slot_sources(flat_slot, rows, members, slots):
    spots = jnp.arange(members * slots, dtype=jnp.int32)
    match = (flat_slot[:, None] == spots[None, :]).astype(jnp.int32)
    return jnp.sum(jnp.arange(rows, dtype=jnp.int32)[:, None] * match, 0)


def to_slots(values, source, members, slots):
    return values[source].reshape((members, slots) + values.shape[1:])


def from_slots(received, take):
    flat = received.reshape((-1,) + received.shape[2:])
    return flat[take]


def placing(got, rows, slots):
    starts = jnp.cumsum(got) - got
    within = jnp.arange(slots, dtype=jnp.int32)
    spots = starts[:, None] + within[None, :]
    landing = jnp.where(within[None, :] < got[:, None], spots, rows).reshape(-1)
    match = (landing[None, :] == jnp.arange(rows, dtype=jnp.int32)[:, None]).astype(jnp.int32)
    take = jnp.sum(jnp.arange(landing.shape[0], dtype=jnp.int32)[None, :] * match, 1)
    pick = jnp.minimum(spots, rows - 1).reshape(-1)
    return (take, pick)


def rim_of_tent(p_rows):
    return extended(p_rows, ((("group", "member"), 0),), 1)


def rim_of_smooth(s_rows):
    return extended(s_rows, ((("group", "member"), 0),), 1)


def smooth_rows(a_rows, earlier, own, later):
    dinv = 1.0 / jnp.diagonal(a_rows[:, 1], axis1=1, axis2=2).astype(jnp.float32)
    own_wide = own.astype(jnp.float32)
    tiles = []
    for k, other in enumerate((earlier, own, later)):
        prod = jnp.einsum("nij,ncj->nci", a_rows[:, k], other, preferred_element_type=jnp.float32)
        base = own_wide if k == 1 else jnp.zeros_like(own_wide)
        tiles.append(base - 0.6 * dinv[:, None, :] * prod)
    return jnp.stack(tiles, 1).astype(jnp.bfloat16)


def product_rows(a_rows, earlier, own, later):
    total = jnp.zeros((own.shape[0], 5) + own.shape[2:], jnp.float32)
    for k, other in enumerate((earlier, own, later)):
        prod = jnp.einsum("nij,ntcj->ntci", a_rows[:, k], other, preferred_element_type=jnp.float32)
        total = total + jnp.pad(prod, ((0, 0), (k, 2 - k), (0, 0), (0, 0)))
    return total.astype(jnp.bfloat16)


def per_device(a_band, p_tent, new_owner):
    members = lax.axis_size("member")
    rows = a_band.shape[0]
    slots = 2 * rows // members
    modes = p_tent.shape[1]
    onehot = (new_owner[:, None] == jnp.arange(members, dtype=jnp.int32)[None, :]).astype(jnp.int32)
    before = jnp.cumsum(onehot, 0) - onehot
    place = jnp.sum(before * onehot, 1)
    counts = jnp.sum(onehot, 0)
    flat_slot = new_owner * slots + place
    source = slot_sources(flat_slot, rows, members, slots)
    a_recv, p_recv, got = (
        lax.all_to_all(
            to_slots(a_band, source, members, slots),
            "member",
            split_axis=0,
            concat_axis=0,
            tiled=True,
        ),
        lax.all_to_all(
            to_slots(p_tent, source, members, slots),
            "member",
            split_axis=0,
            concat_axis=0,
            tiled=True,
        ),
        lax.all_to_all(counts, "member", split_axis=0, concat_axis=0, tiled=True),
    )
    take, pick = placing(got, rows, slots)
    a_new = from_slots(a_recv, take)
    p_new = from_slots(p_recv, take)
    p_rim = rim_of_tent(p_new)
    p_smooth = smooth_rows(a_new, p_rim[:-2], p_new, p_rim[2:])
    s_rim = rim_of_smooth(p_smooth)
    ap_tiles = product_rows(a_new, s_rim[:-2], p_smooth, s_rim[2:])
    stacked = jnp.concatenate([p_smooth, ap_tiles], 1)
    b_rim = extended(stacked, ((("group", "member"), 0),), 1)
    coarse = jnp.zeros((rows, 7, modes, modes), jnp.float32)
    for shift_n in (-1, 0, 1):
        near = b_rim[1 + shift_n : 1 + shift_n + rows]
        term = jnp.einsum(
            "nci,nedi->necd", near[:, 1 - shift_n], near[:, 3:8], preferred_element_type=jnp.float32
        )
        coarse = coarse + jnp.pad(term, ((0, 0), (1 + shift_n, 1 - shift_n), (0, 0), (0, 0)))
    return (p_smooth, coarse.reshape(rows, 7 * modes * modes))


def solution(mesh):
    in_specs = (
        P(("group", "member"), None, None, None),
        P(("group", "member"), None, None),
        P(("group", "member")),
    )
    out_specs = (P(("group", "member"), None, None, None), P(("group", "member"), None))
    return jax.shard_map(
        per_device, mesh=mesh, in_specs=in_specs, out_specs=out_specs, check_vma=False
    )
```

profile of v0, /device:TPU:3, one launch (start us, length us, event | category | flops | bytes accessed | tf_op | source)
XLA Modules:
  0.0 415.4 jit_solution(16825038865556496266)
XLA Ops:
  3.8 12.3 %all-to-all-start.1 = ((s32[64,1,1]{2,1,0:T(1,128)}), s32[64,1,1]{2,1,0:T(1,128)S(1)}, u32[]{:S(2)}, u32[]{:S(2)}) async-start(s32[64,1,1]{2,1,0:T(1,128)} %copy.123), calls=%async_computation.1 | async-start | bytes 65536 | tf_op jit(solution)/shard_map/all_to_all | solution.py:103
  18.2 1.7 gather_fusion.3
  21.3 4.2 %all-to-all-done.1 = s32[64,1,1]{2,1,0:T(1,128)S(1)} async-done(((s32[64,1,1]{2,1,0:T(1,128)}), s32[64,1,1]{2,1,0:T(1,128)S(1)}, u32[]{:S(2)}, u32[]{:S(2)}) %all-to-all-start.1) | async-done | bytes 288 | tf_op jit(solution)/shard_map/all_to_all | solution.py:103
  25.5 6.1 %all-to-all-start.2 = ((bf16[64,2,1152]{2,1,0:T(2,128)(2,1)}), bf16[64,2,1152]{2,1,0:T(2,128)(2,1)S(1)}, u32[]{:S(2)}, u32[]{:S(2)}) async-start(bf16[64,2,1152]{2,1,0:T(2,128)(2,1)} %reshape.189), calls=%async_computation.2 | async-start | bytes 589824 | tf_op jit(solution)/shard_map/all_to_all | solution.py:96
  31.6 13.1 %copy.122 = bf16[192,3,64,64]{3,2,1,0:T(8,128)(2,1)} copy(bf16[192,3,64,64]{0,3,2,1:T(8,128)(2,1)} %param.3) | data formatting | bytes 9437184 | tf_op args[0]
  44.7 17.2 %gather_fusion = bf16[384,3,64,64]{3,2,1,0:T(8,128)(2,1)} fusion(bf16[192,3,64,64]{3,2,1,0:T(8,128)(2,1)} %copy.122, s32[1024]{0:T(1024)S(1)} %pad_clamp_fusion.1), kind=kCustom, calls=%fused_computation | custom fusion | bytes 18875904 | tf_op jit(solution)/shard_map/gather | solution.py:31
  61.9 27.8 %reshape.187 = bf16[64,2,36864]{2,1,0:T(2,128)(2,1)} reshape(bf16[64,6,3,64,64]{4,3,2,1,0:T(8,128)(2,1)} %bitcast.133) | data formatting | bytes 18874368
  89.7 10.5 %all-to-all-start = ((bf16[64,2,36864]{2,1,0:T(2,128)(2,1)}), bf16[64,2,36864]{2,1,0:T(2,128)(2,1)}, u32[]{:S(2)}, u32[]{:S(2)}) async-start(bf16[64,2,36864]{2,1,0:T(2,128)(2,1)} %reshape.187), calls=%async_computation | async-start | bytes 18874368 | tf_op jit(solution)/shard_map/all_to_all | solution.py:89
  103.4 2.4 collective-permute-start.1
  105.8 3.3 collective-permute-start
  109.1 25.0 %collective-permute-done.1 = bf16[1,6,64]{2,1,0:T(8,128)(2,1)S(1)} collective-permute-done((bf16[1,6,64]{2,1,0:T(8,128)(2,1)S(1)}, bf16[1,6,64]{2,1,0:T(8,128)(2,1)S(1)}, u32[]{:S(2)}, u32[]{:S(2)}) %collective-permute-start.1) | collective-permute-done | bytes 800 | tf_op jit(solution)/shard_map/ppermute | solution.py:17
  135.9 169.4 %all-to-all-done = bf16[64,2,36864]{2,1,0:T(2,128)(2,1)} async-done(((bf16[64,2,36864]{2,1,0:T(2,128)(2,1)}), bf16[64,2,36864]{2,1,0:T(2,128)(2,1)}, u32[]{:S(2)}, u32[]{:S(2)}) %all-to-all-start) | async-done | bytes 9437216 | tf_op jit(solution)/shard_map/all_to_all | solution.py:89
  305.3 27.3 %reshape.188 = bf16[64,6,3,64,64]{4,3,2,1,0:T(8,128)(2,1)} reshape(bf16[64,2,36864]{2,1,0:T(2,128)(2,1)} %all-to-all-done) | data formatting | bytes 18874368
  332.6 16.1 %gather_fusion.1 = bf16[192,3,64,64]{3,2,1,0:T(8,128)(2,1)} fusion(bf16[384,3,64,64]{3,2,1,0:T(8,128)(2,1)} %bitcast.136, s32[1024]{0:T(1024)S(1)} %pad_clamp_fusion), kind=kCustom, calls=%fused_computation.1 | custom fusion | bytes 9437952 | tf_op jit(solution)/shard_map/gather | solution.py:36
  348.7 2.6 slice_bitcast_fusion
  351.3 3.8 copy.126
  356.8 3.8 fusion.56
  360.7 3.8 fusion.60
  366.7 5.9 %collective-permute-start.3 = (bf16[1,3,6,64]{3,2,0,1:T(8,128)(2,1)S(1)}, bf16[1,3,6,64]{3,2,0,1:T(8,128)(2,1)S(1)}, u32[]{:S(2)}, u32[]{:S(2)}) collective-permute-start(bf16[1,3,6,64]{3,2,0,1:T(8,128)(2,1)S(1)} %get-tuple-element.18), channel_id=1, source_target_pairs={{1,0},{2,1},{3,2},{4,3},{5,4},{6,5},{7,6},{8,7},{9,8},{10,9},{11,1... | collective-permute-start | bytes 6920 | tf_op jit(solution)/shard_map/ppermute | solution.py:17
  372.5 2.1 collective-permute-start.2
  374.7 3.6 fusion.22
  378.3 1.8 copy.142
  380.5 3.8 fusion.24
  384.4 3.8 add_convert_fusion
  388.8 3.5 collective-permute-start.5
  392.3 2.7 convolution_bitcast_fusion
  395.0 2.0 collective-permute-start.4
  397.2 3.3 fusion.35
  400.5 1.8 collective-permute-done.4
  403.1 2.2 fusion.38
  406.4 3.3 pad_add_fusion
  409.7 4.8 %copy.141 = f32[192,7,6,6]{0,3,2,1:T(8,128)S(1)} copy(f32[192,7,6,6]{2,3,1,0:T(8,128)} %pad_add_fusion) | data formatting | bytes 387072 | tf_op jit(solution)/shard_map/add | solution.py:120
  (66 shorter events, 19.2 us)
Async XLA Ops:
  3.8 21.6 %all-to-all-start.1 = ((s32[64,1,1]{2,1,0:T(1,128)}), s32[64,1,1]{2,1,0:T(1,128)S(1)}, u32[]{:S(2)}, u32[]{:S(2)}) async-start(s32[64,1,1]{2,1,0:T(1,128)} %copy.123), calls=%async_computation.1 | async-start | bytes 65536 | tf_op jit(solution)/shard_map/all_to_all | solution.py:103
  25.5 64.2 %all-to-all-start.2 = ((bf16[64,2,1152]{2,1,0:T(2,128)(2,1)}), bf16[64,2,1152]{2,1,0:T(2,128)(2,1)S(1)}, u32[]{:S(2)}, u32[]{:S(2)}) async-start(bf16[64,2,1152]{2,1,0:T(2,128)(2,1)} %reshape.189), calls=%async_computation.2 | async-start | bytes 589824 | tf_op jit(solution)/shard_map/all_to_all | solution.py:96
  89.7 215.6 %all-to-all-start = ((bf16[64,2,36864]{2,1,0:T(2,128)(2,1)}), bf16[64,2,36864]{2,1,0:T(2,128)(2,1)}, u32[]{:S(2)}, u32[]{:S(2)}) async-start(bf16[64,2,36864]{2,1,0:T(2,128)(2,1)} %reshape.187), calls=%async_computation | async-start | bytes 18874368 | tf_op jit(solution)/shard_map/all_to_all | solution.py:89
  103.4 30.8 %collective-permute-start.1 = (bf16[1,6,64]{2,1,0:T(8,128)(2,1)S(1)}, bf16[1,6,64]{2,1,0:T(8,128)(2,1)S(1)}, u32[]{:S(2)}, u32[]{:S(2)}) collective-permute-start(bf16[1,6,64]{2,1,0:T(8,128)(2,1)S(1)} %get-tuple-element.21), channel_id=1, source_target_pairs={{1,0},{2,1},{3,2},{4,3},{5,4},{6,5},{7,6},{8,7},{9,8},{10,9},{11,1... | collective-permute-start | bytes 2312 | tf_op jit(solution)/shard_map/ppermute | solution.py:17
  105.8 29.2 %collective-permute-start = (bf16[1,6,64]{2,1,0:T(8,128)(2,1)S(1)}, bf16[1,6,64]{2,1,0:T(8,128)(2,1)S(1)}, u32[]{:S(2)}, u32[]{:S(2)}) collective-permute-start(bf16[1,6,64]{2,1,0:T(8,128)(2,1)S(1)} %get-tuple-element.20), channel_id=1, source_target_pairs={{0,1},{1,2},{2,3},{3,4},{4,5},{5,6},{6,7},{7,8},{8,9},{9,10},{10,1... | collective-permute-start | bytes 2312 | tf_op jit(solution)/shard_map/ppermute | solution.py:15
  355.1 5.5 %copy-start.3 = (bf16[193,6,64]{2,1,0:T(8,128)(2,1)S(1)}, bf16[193,6,64]{2,1,0:T(8,128)(2,1)}, u32[]{:S(2)}) copy-start(bf16[193,6,64]{2,1,0:T(8,128)(2,1)} %fusion.122) | copy-start | bytes 444676
  356.8 7.6 %slice-start = ((s8[9437184]{0:T(1024)(128)(4,1)}), s8[4194304]{0:T(1024)(128)(4,1)S(1)}, s32[]{:S(2)}) async-start(s8[9437184]{0:T(1024)(128)(4,1)} %bitcast.134), calls=%async_computation.3 | async-start | bytes 8388608
  360.6 3.8 slice-start.1
  360.6 3.8 slice-start.2
  360.6 3.8 copy-start.4
  366.7 13.4 %collective-permute-start.3 = (bf16[1,3,6,64]{3,2,0,1:T(8,128)(2,1)S(1)}, bf16[1,3,6,64]{3,2,0,1:T(8,128)(2,1)S(1)}, u32[]{:S(2)}, u32[]{:S(2)}) collective-permute-start(bf16[1,3,6,64]{3,2,0,1:T(8,128)(2,1)S(1)} %get-tuple-element.18), channel_id=1, source_target_pairs={{1,0},{2,1},{3,2},{4,3},{5,4},{6,5},{7,6},{8,7},{9,8},{10,9},{11,1... | collective-permute-start | bytes 6920 | tf_op jit(solution)/shard_map/ppermute | solution.py:17
  372.5 7.6 %collective-permute-start.2 = (bf16[1,3,6,64]{3,2,0,1:T(8,128)(2,1)S(1)}, bf16[1,3,6,64]{3,2,0,1:T(8,128)(2,1)S(1)}, u32[]{:S(2)}, u32[]{:S(2)}) collective-permute-start(bf16[1,3,6,64]{3,2,0,1:T(8,128)(2,1)S(1)} %get-tuple-element.19), channel_id=1, source_target_pairs={{0,1},{1,2},{2,3},{3,4},{4,5},{5,6},{6,7},{7,8},{8,9},{9,10},{10,1... | collective-permute-start | bytes 6920 | tf_op jit(solution)/shard_map/ppermute | solution.py:15
  380.5 3.8 copy-start.1
  388.8 8.3 %collective-permute-start.5 = (bf16[1,8,6,64]{3,2,1,0:T(8,128)(2,1)S(1)}, bf16[1,8,6,64]{3,2,1,0:T(8,128)(2,1)S(1)}, u32[]{:S(2)}, u32[]{:S(2)}) collective-permute-start(bf16[1,8,6,64]{3,2,1,0:T(8,128)(2,1)S(1)} %get-tuple-element.15), channel_id=1, source_target_pairs={{1,0},{2,1},{3,2},{4,3},{5,4},{6,5},{7,6},{8,7},{9,8},{10,9},{11,1... | collective-permute-start | bytes 18440 | tf_op jit(solution)/shard_map/ppermute | solution.py:17
  395.0 7.3 %collective-permute-start.4 = (bf16[1,8,6,64]{3,2,1,0:T(8,128)(2,1)}, bf16[1,8,6,64]{3,2,1,0:T(8,128)(2,1)}, u32[]{:S(2)}, u32[]{:S(2)}) collective-permute-start(bf16[1,8,6,64]{3,2,1,0:T(8,128)(2,1)} %get-tuple-element.14), channel_id=1, source_target_pairs={{0,1},{1,2},{2,3},{3,4},{4,5},{5,6},{6,7},{7,8},{8,9},{9,10},{10,1... | collective-permute-start | bytes 18440 | tf_op jit(solution)/shard_map/ppermute | solution.py:15
  403.1 2.2 copy-start
  403.1 3.3 copy-start.2
where the time goes:
time: 424 us; the launch traced here: 415 us
  waiting for transfers between devices  200 us (47%)
  local copies, waits for them, and re-layouts  125 us (29%)
  starting transfers between devices  48.3 us (11%)
  matrix products  28.8 us (7%)
  other arithmetic  12.2 us (3%)
    all_to_all x1, waiting for transfers between devices, per_device(): lax.all_to_all(to_slots(a_band, source, members, slots), 'member', split_...  169 us
    unnamed x24, local copies, waits for them, and re-layouts  74.7 us
    ppermute x3, waiting for transfers between devices, extended(): lax.ppermute(head, axis, [((i + 1) % count, i) for i in range(ends)])  25 us
    gather x2, local copies, waits for them, and re-layouts, to_slots(): return values[source].reshape((members, slots) + values.shape[1:])  18.9 us
    gather x2, local copies, waits for them, and re-layouts, from_slots(): return flat[take]  16.9 us
    all_to_all x1, starting transfers between devices, per_device(): lax.all_to_all(counts, 'member', split_axis=0, concat_axis=0, tiled=True)  12.3 us
    ppermute x3, starting transfers between devices, extended(): lax.ppermute(head, axis, [((i + 1) % count, i) for i in range(ends)])  11.8 us
    all_to_all x1, starting transfers between devices, per_device(): lax.all_to_all(to_slots(a_band, source, members, slots), 'member', split_...  10.5 us
  transfers between devices with their start and end apart: 9, of which 4 were waited for; matrix products, arithmetic and copies ran while one was open for 19% of the time, Pallas kernels for 0%

commit v1 on v0

v1 whole, which is shorter than its diff:
```python
import functools

import jax
import jax.numpy as jnp
from jax import lax
from jax.experimental import pallas as pl
from jax.experimental.pallas import tpu as pltpu
from jax.sharding import PartitionSpec as P

ROWS = 192
WIDE = 256
TILE = 64
MODES = 6
MEMBERS = 64
SLOTS = 8
COLS = 3 * MODES * TILE
F32 = jnp.float32
BF16 = jnp.bfloat16
NT = (((1,), (1,)), ((), ()))
TN = (((0,), (0,)), ((), ()))
VMEM_BYTES = 56 * 1024 * 1024


def iota(shape, axis):
    return lax.broadcasted_iota(jnp.int32, shape, axis)


def ones_where(mask):
    return jnp.where(mask, 1.0, 0.0).astype(BF16)


def dot(a, b):
    return jnp.dot(a, b, preferred_element_type=F32)


def parts_of(x):
    high = x.astype(BF16)
    rest = x - high.astype(F32)
    mid = rest.astype(BF16)
    low = (rest - mid.astype(F32)).astype(BF16)
    return high, mid, low


def exact_dot(pick, x, dims, pick_first):
    total = None
    for part in parts_of(x):
        ab = (pick, part) if pick_first else (part, pick)
        prod = lax.dot_general(*ab, dims, preferred_element_type=F32)
        total = prod if total is None else total + prod
    return total


def ranks(owner_row):
    wide = jnp.broadcast_to(owner_row.astype(F32), (WIDE, WIDE))
    tall = wide.T[:ROWS]
    wide = wide[:ROWS]
    lane = iota((ROWS, WIDE), 1)
    row_l = jnp.where(lane < ROWS, lane, lane - TILE)
    row_s = iota((ROWS, WIDE), 0)
    same = wide == tall
    one = jnp.where(same, 1.0, 0.0)
    less, more = row_s < row_l, row_s > row_l
    rank_l = jnp.sum(jnp.where(less, one, 0.0), 0, keepdims=True)
    after_l = jnp.sum(jnp.where(more, one, 0.0), 0, keepdims=True)
    once = jnp.where(lane < ROWS, one, 0.0)
    rank_s = jnp.sum(jnp.where(more, once, 0.0), 1, keepdims=True)
    after_s = jnp.sum(jnp.where(less, once, 0.0), 1, keepdims=True)
    return dict(
        wide=wide[:1], tall=tall[:, :128], same=same, row_l=row_l, row_s=row_s,
        rank_l=rank_l, after_l=after_l, rank_s=rank_s, after_s=after_s,
    )


def rim_picks(r, me):
    lane = iota((ROWS, 128), 1)
    first, last = r["rank_s"] == 0.0, r["after_s"] == 0.0
    picks = []
    for half in (0, 1):
        slot = lane - TILE * half
        inside = (slot >= 0) & (slot < TILE)
        to_left = jnp.where(inside, slot + jnp.where(me == 0, 1, 0), -1).astype(F32)
        to_right = jnp.where(inside, slot - jnp.where(me == MEMBERS - 1, 1, 0), -1).astype(F32)
        left = ones_where((r["tall"] == to_left) & first)
        right = ones_where((r["tall"] == to_right) & last)
        far_first = (slot == TILE - 1) & (me == 0) & (r["tall"] == 0.0) & first
        far_last = (slot == 0) & (me == MEMBERS - 1) & (r["tall"] == MEMBERS - 1.0) & last
        far = ones_where(far_first | far_last)
        picks.append((left, right, far))
    return picks


def rims_of(rows, r, me):
    half = rows.shape[0] // 2
    top, bottom = rim_picks(r, me)
    return [
        (dot(rows[:half], a) + dot(rows[half:], b)).astype(BF16) for a, b in zip(top, bottom)
    ]


def neighbours(rows, from_left, from_right, far, r, me):
    half = rows.shape[0] // 2
    zero = jnp.zeros_like(far)
    from_left = from_left + jnp.where(me == MEMBERS - 1, zero, far)
    from_right = from_right + jnp.where(me == 0, zero, far)
    before = ones_where(r["same"] & (r["rank_s"] + 1.0 == r["rank_l"]))
    after = ones_where(r["same"] & (r["rank_s"] == r["rank_l"] + 1.0))
    here = ones_where(r["row_s"] == r["row_l"])
    bucket = iota((128, WIDE), 0)
    result = []
    for local, rim, edge in ((before, from_left, "rank_l"), (here, None, None), (after, from_right, "after_l")):
        own = dot(rows, local)
        if rim is not None:
            ends = []
            for side in (0, 1):
                want = bucket - TILE * side
                want = jnp.where((want >= 0) & (want < TILE), want, -1).astype(F32)
                ends.append(dot(rim, ones_where((want == r["wide"]) & (r[edge] == 0.0))))
            own = own + jnp.concatenate(ends, 0)
        result.append(own)
    return result


def set_wide(ref, k, value):
    for tile in (0, 1):
        part = value[:, 128 * tile : 128 * (tile + 1)]
        ref[tile, k] = part.reshape(-1, TILE, 128)


def set_groups(a_ref, group_ref):
    for k in range(3):
        for i in range(8):
            low, high = a_ref[k, i].astype(F32), a_ref[k, i + 8].astype(F32)
            group_ref[0, k, i] = low[:, :128]
            group_ref[1, k, i] = high[:, :128]
            group_ref[2, k, i] = jnp.concatenate([low[:, 128:], high[:, 128:]], 1)


def folded(terms):
    sub = iota((8, 128), 0)
    for shift in (1, 2, 4):
        keep = (sub & shift) == 0
        terms = [
            jnp.where(keep, x, y) + pltpu.roll(jnp.where(keep, y, x), shift, 0)
            for x, y in zip(terms[::2], terms[1::2])
        ]
    return terms[0]


def contracted(group_ref, wide_ref, g, tile, pairs, columns):
    totals = [[None] * 8 for _ in columns]
    for jb in range(TILE // 8):
        j = pl.ds(8 * jb, 8)
        for k, base in pairs:
            a = [group_ref[g, k, i, j, :] for i in range(8)]
            for n, column in enumerate(columns):
                x = wide_ref[tile, k, base + column, j, :]
                for i in range(8):
                    term = a[i] * x
                    totals[n][i] = term if totals[n][i] is None else totals[n][i] + term
    return [folded(t) for t in totals]


def ungrouped(out_ref, index):
    low, high, both = out_ref[0, index], out_ref[1, index], out_ref[2, index]
    top = jnp.concatenate([low, both[:, :TILE]], 1)
    bottom = jnp.concatenate([high, both[:, TILE:]], 1)
    return jnp.concatenate([top, bottom], 0)


def first_kernel(me_ref, owner_ref, p_ref, left_ref, right_ref, far_ref):
    r = ranks(owner_ref[...])
    me = me_ref[0]
    for ref, rim in zip((left_ref, right_ref, far_ref), rims_of(p_ref[...], r, me)):
        ref[...] = rim


def smooth_kernel(
    me_ref, owner_ref, a_ref, p_ref, from_left_ref, from_right_ref, far_ref,
    s_ref, left_out, right_out, far_out, group_ref, wide_ref, out_ref,
):
    ib = pl.program_id(0)
    me = me_ref[0]

    @pl.when(ib == 0)
    def _():
        r = ranks(owner_ref[...])
        near = neighbours(p_ref[...], from_left_ref[...], from_right_ref[...], far_ref[...], r, me)
        for k, value in enumerate(near):
            set_wide(wide_ref, k, value)

    set_groups(a_ref, group_ref)
    sub, lane = iota((8, 128), 0), iota((8, 128), 1)

    def one_group(g, carry):
        tile = jnp.where(g == 2, 1, 0)
        second = (g == 1) | ((g == 2) & (lane >= TILE))
        lower, upper = pl.ds(pl.multiple_of(16 * ib, 8), 8), pl.ds(pl.multiple_of(16 * ib + 8, 8), 8)
        diag = jnp.zeros((8, 128), F32)
        for i in range(8):
            entry = jnp.where(second, group_ref[g, 1, i, upper, :], group_ref[g, 1, i, lower, :])
            diag = jnp.where(sub == i, entry, diag)
        scale = 0.6 * (1.0 / diag)
        for k in range(3):
            for half in (0, 1):
                columns = [3 * half + c for c in range(3)]
                sums = contracted(group_ref, wide_ref, g, tile, [(k, 0)], columns)
                for c, total in zip(columns, sums):
                    value = scale * total
                    if k == 1:
                        own = jnp.where(second, wide_ref[tile, 1, c, upper, :], wide_ref[tile, 1, c, lower, :])
                        value = own - value
                    else:
                        value = 0.0 - value
                    out_ref[g, 6 * k + c] = value
        return carry

    lax.fori_loop(0, 3, one_group, 0)
    rows = pl.ds(pl.multiple_of(16 * ib, 16), 16)
    for index in range(18):
        s_ref[index, rows, :] = ungrouped(out_ref, index).astype(BF16)

    @pl.when(ib == pl.num_programs(0) - 1)
    def _():
        r = ranks(owner_ref[...])
        flat = s_ref[...].reshape(COLS, ROWS)
        for ref, rim in zip((left_out, right_out, far_out), rims_of(flat, r, me)):
            ref[...] = rim


def slot_grid(width):
    spot = iota((MEMBERS * SLOTS, width), 0)
    return (spot // SLOTS).astype(F32), (spot % SLOTS).astype(F32)


def pack_kernel(owner_ref, s_ref, out_ref):
    r = ranks(owner_ref[...])
    member, slot = slot_grid(ROWS)
    owner, rank = r["wide"][:, :ROWS], r["rank_l"][:, :ROWS]
    mine = owner == member
    pick = ones_where(mine & (rank == slot))
    count = jnp.sum(jnp.where(mine, 1.0, 0.0), 1, keepdims=True)
    spot, lane = iota((MEMBERS * SLOTS, 128), 0) % SLOTS, iota((MEMBERS * SLOTS, 128), 1)
    for block in range(COLS // 128):
        value = lax.dot_general(
            pick, s_ref[128 * block : 128 * (block + 1), :], NT, preferred_element_type=F32
        )
        if block == 0:
            value = jnp.where((spot == 6) & (lane == 0), count, value)
        out_ref[:, 128 * block : 128 * (block + 1)] = value.astype(BF16)


OFFSETS = [[(k, 6 * (e - k)) for k in range(3) if 0 <= e - k <= 2] for e in range(5)]


def product_kernel(
    me_ref, owner_ref, a_ref, s_ref, from_left_ref, from_right_ref, far_ref,
    out_ref, far_out, group_ref, wide_ref, ap_ref, own_ref, term_ref,
):
    ib = pl.program_id(0)
    me = me_ref[0]

    @pl.when(ib == 0)
    def _():
        r = ranks(owner_ref[...])
        near = neighbours(s_ref[...], from_left_ref[...], from_right_ref[...], far_ref[...], r, me)
        for k, value in enumerate(near):
            set_wide(wide_ref, k, value)
        term_ref[...] = jnp.zeros_like(term_ref)

    set_groups(a_ref, group_ref)
    lane = iota((8, 128), 1)

    def one_group(step, carry):
        g, half = step // 2, step % 2
        tile = jnp.where(g == 2, 1, 0)
        for e in range(5):
            columns = [3 * half + c for c in range(3)]
            sums = contracted(group_ref, wide_ref, g, tile, OFFSETS[e], columns)
            for c, total in zip(columns, sums):
                ap_ref[g, ib, 6 * e + c] = total.astype(BF16).astype(F32)
        second = (g == 1) | ((g == 2) & (lane >= TILE))
        lower, upper = pl.ds(pl.multiple_of(16 * ib, 8), 8), pl.ds(pl.multiple_of(16 * ib + 8, 8), 8)
        for c in range(9):
            column = 9 * half + c
            own_ref[g, ib, column] = jnp.where(
                second, wide_ref[tile, 1, column, upper, :], wide_ref[tile, 1, column, lower, :]
            )
        return carry

    lax.fori_loop(0, 6, one_group, 0)

    @pl.when(ib == pl.num_programs(0) - 1)
    def _():
        def one_pair(step, carry):
            k, e = step // 5, step % 5
            for c in range(6):
                near, far = [None] * 6, [None] * 6
                for block in range(TILE // 16):
                    for g in range(3):
                        x = own_ref[g, block, 6 * k + c]
                        for d in range(6):
                            term = x * ap_ref[g, block, 6 * e + d]
                            sums = far if g == 2 else near
                            sums[d] = term if sums[d] is None else sums[d] + term
                for d in range(6):
                    row = slice(6 * c + d, 6 * c + d + 1)
                    tail = jnp.sum(far[d], 0, keepdims=True)
                    term_ref[step, row, 0:128] = jnp.sum(near[d], 0, keepdims=True)
                    term_ref[step, row, 128:ROWS] = tail[:, :TILE] + tail[:, TILE:]
            return carry

        lax.fori_loop(0, 15, one_pair, 0)
        r = ranks(owner_ref[...])
        owner, rank, after = (r[n][:, :ROWS] for n in ("wide", "rank_l", "after_l"))
        member, slot = slot_grid(ROWS)
        mine, row_slot = owner == member, slot < 6.0
        here = ones_where(mine & (rank == slot))
        back_to = member + jnp.where(me == 0, 1.0, 0.0)
        on_to = member - jnp.where(me == MEMBERS - 1, 1.0, 0.0)
        back = (mine & row_slot & (rank == slot + 1.0)) | ((slot == 6.0) & (owner == back_to) & (rank == 0.0))
        on = (mine & row_slot & (rank == slot - 1.0) & (after > 0.0)) | (
            (slot == 7.0) & (owner == on_to) & (after == 0.0)
        )
        picks = [ones_where(back), here, ones_where(on)]
        terms = []
        for k in range(3):
            pieces = [term_ref[5 * k + e][:36, :ROWS] for e in range(5)]
            pieces.append(jnp.zeros((4 + 36 * k, ROWS), F32))
            if k < 2:
                pieces.insert(0, jnp.zeros((72 - 36 * k, ROWS), F32))
            terms.append(jnp.concatenate(pieces, 0))
        total = None
        for k in range(3):
            prod = exact_dot(picks[k], terms[k], NT, True)
            total = prod if total is None else total + prod
        out_ref[...] = total
        top = iota((8, ROWS), 0) == 0
        far_back = ones_where(top & (me == 0) & (owner == 0.0) & (rank == 0.0))
        far_on = ones_where(top & (me == MEMBERS - 1) & (owner == MEMBERS - 1.0) & (after == 0.0))
        far_out[...] = exact_dot(far_back, terms[0], NT, True) + exact_dot(
            far_on, terms[2], NT, True
        )


def arrivals(counts):
    size = MEMBERS * SLOTS
    spot, lane = iota((size, 128), 0) % SLOTS, iota((size, 128), 1)
    marked = jnp.where((spot == 6) & (lane == 0), counts.astype(F32), 0.0).astype(BF16)
    source, other = iota((size, size), 0) // SLOTS, iota((size, size), 1) // SLOTS
    start = dot(ones_where(other < source), marked)[:, :1]
    count = dot(ones_where(other == source), marked)[:, :1]
    slot = (iota((size, 1), 0) % SLOTS).astype(F32)
    return slot, start, count


def unpack_smooth_kernel(recv_ref, out_ref):
    slot, start, count = arrivals(recv_ref[:, :128])
    place = jnp.where(slot < count, start + slot, -1.0)
    pick = ones_where(place == iota((MEMBERS * SLOTS, ROWS), 1).astype(F32))
    for block in range(COLS // 128):
        at = slice(128 * block, 128 * (block + 1))
        value = lax.dot_general(recv_ref[:, at], pick, TN, preferred_element_type=F32)
        out_ref[at, :] = value.astype(BF16)


def unpack_coarse_kernel(me_ref, recv_ref, sums_ref, far_ref, out_ref):
    me = me_ref[0]
    slot, start, count = arrivals(recv_ref[...])
    place = jnp.where(slot < count, start + slot, -1.0)
    place = jnp.where(slot == 6.0, jnp.where(start == 0.0, ROWS - 1.0, start - 1.0), place)
    stop = start + count
    place = jnp.where(slot == 7.0, jnp.where(stop == float(ROWS), 0.0, stop), place)
    pick = ones_where(place == iota((MEMBERS * SLOTS, ROWS), 1).astype(F32))
    total = exact_dot(pick, sums_ref[...], TN, True)
    row = iota((ROWS, WIDE), 0)
    edge = jnp.where(me == 0, 0, ROWS - 1)
    far = jnp.broadcast_to(far_ref[0:1, :], (ROWS, WIDE))
    total = total + jnp.where(row == edge, far, 0.0)
    out_ref[...] = total[:, :252]


def call(kernel, outs, args, grid=None, in_specs=None, scratch=(), flops=0, name=None):
    whole = lambda shape: pl.BlockSpec(shape, lambda *_: (0,) * len(shape))
    specs = []
    for n, arg in enumerate(args):
        spec = None if in_specs is None else in_specs.get(n)
        if spec is None:
            spec = pl.BlockSpec(memory_space=pltpu.SMEM) if arg.shape == (1,) else whole(arg.shape)
        specs.append(spec)
    moved = sum(a.size * a.dtype.itemsize for a in args) + sum(o.size * o.dtype.itemsize for o in outs)
    return pl.pallas_call(
        kernel,
        grid=(1,) if grid is None else grid,
        in_specs=specs,
        out_specs=[whole(o.shape) for o in outs],
        out_shape=outs,
        scratch_shapes=list(scratch),
        compiler_params=pltpu.CompilerParams(vmem_limit_bytes=VMEM_BYTES),
        cost_estimate=pl.CostEstimate(flops=flops, bytes_accessed=moved, transcendentals=0),
        name=name,
    )(*args)


def shaped(shape, dtype=BF16):
    return jax.ShapeDtypeStruct(shape, dtype)


def exchanged(left, right, far, groups):
    ring = MEMBERS
    axes = ("group", "member")
    to_left = [(g * ring + i, g * ring + (i - 1) % ring) for g in range(groups) for i in range(ring)]
    to_right = [(b, a) for a, b in to_left]
    across = []
    for g in range(groups - 1):
        across += [(g * ring + ring - 1, (g + 1) * ring), ((g + 1) * ring, g * ring + ring - 1)]
    from_right = lax.ppermute(left, axes, to_left)
    from_left = lax.ppermute(right, axes, to_right)
    return from_left, from_right, lax.ppermute(far, axes, across), across


def per_device(a_band, p_tent, new_owner):
    groups = lax.axis_size("group")
    me = lax.axis_index("member").astype(jnp.int32).reshape(1)
    owner = jnp.concatenate([new_owner, new_owner[128:]]).reshape(1, WIDE)
    a = a_band.transpose(1, 2, 3, 0)
    p = p_tent.transpose(1, 2, 0).reshape(MODES * TILE, ROWS)
    a_spec = pl.BlockSpec((3, 16, TILE, ROWS), lambda i: (0, i, 0, 0))
    grid = (TILE // 16,)
    group_scratch = pltpu.VMEM((3, 3, 8, TILE, 128), F32)

    rim = shaped((MODES * TILE // 2, 128))
    left, right, far = call(first_kernel, [rim] * 3, (me, owner, p), name="rims")
    from_left, from_right, from_far, across = exchanged(left, right, far, groups)

    rim = shaped((COLS // 2, 128))
    s, left, right, far = call(
        smooth_kernel,
        [shaped((18, TILE, ROWS)), rim, rim, rim],
        (me, owner, a, p, from_left, from_right, from_far),
        grid=grid,
        in_specs={2: a_spec},
        scratch=[
            group_scratch,
            pltpu.VMEM((2, 3, MODES, TILE, 128), F32),
            pltpu.VMEM((3, 18, 8, 128), F32),
        ],
        flops=10**9,
        name="smooth",
    )
    from_left, from_right, from_far, _ = exchanged(left, right, far, groups)
    s = s.reshape(COLS, ROWS)
    (packed,) = call(pack_kernel, [shaped((MEMBERS * SLOTS, COLS))], (owner, s), name="pack")
    packed, from_left, from_right, from_far = lax.optimization_barrier(
        (packed, from_left, from_right, from_far)
    )
    recv = lax.all_to_all(
        packed.reshape(MEMBERS, SLOTS, COLS), "member", split_axis=0, concat_axis=0, tiled=True
    ).reshape(MEMBERS * SLOTS, COLS)

    sums, far = call(
        product_kernel,
        [shaped((MEMBERS * SLOTS, WIDE), F32), shaped((8, WIDE), F32)],
        (me, owner, a, s, from_left, from_right, from_far),
        grid=grid,
        in_specs={2: a_spec},
        scratch=[
            group_scratch,
            pltpu.VMEM((2, 3, 18, TILE, 128), F32),
            pltpu.VMEM((3, TILE // 16, 30, 8, 128), F32),
            pltpu.VMEM((3, TILE // 16, 18, 8, 128), F32),
            pltpu.VMEM((15, 40, WIDE), F32),
        ],
        flops=10**10,
        name="product",
    )
    far = lax.ppermute(far, ("group", "member"), across)
    sums = lax.all_to_all(
        sums.reshape(MEMBERS, SLOTS, WIDE), "member", split_axis=0, concat_axis=0, tiled=True
    ).reshape(MEMBERS * SLOTS, WIDE)
    (smooth,) = call(unpack_smooth_kernel, [shaped((COLS, ROWS))], (recv,), name="unpack_smooth")
    (coarse,) = call(
        unpack_coarse_kernel,
        [shaped((ROWS, 252), F32)],
        (me, recv, sums, far),
        in_specs={1: pl.BlockSpec((MEMBERS * SLOTS, 128), lambda i: (0, 0))},
        name="unpack_coarse",
    )
    return smooth.reshape(3, MODES, TILE, ROWS).transpose(3, 0, 1, 2), coarse


def solution(mesh):
    in_specs = (
        P(("group", "member"), None, None, None),
        P(("group", "member"), None, None),
        P(("group", "member")),
    )
    out_specs = (P(("group", "member"), None, None, None), P(("group", "member"), None))
    return jax.shard_map(
        per_device, mesh=mesh, in_specs=in_specs, out_specs=out_specs, check_vma=False
    )
```

time: 424 us -> 113 us (0.27); the launches traced: 415 us -> 113 us
  waiting for transfers between devices: 200 us -> 24.3 us
  local copies, waits for them, and re-layouts: 125 us -> 2.86 us
  Pallas kernels: 0 us -> 44 us
  matrix products: 28.8 us -> 0 us
  other arithmetic: 12.2 us -> 1.34 us
  starting transfers between devices: 48.3 us -> 39.3 us
    all_to_all x3 -> x2, waiting for transfers between devices: 174 us -> 21.2 us  [the longest x1 13.8 us: per_device(): lax.all_to_all(sums.reshape(MEMBERS, SLOTS, WIDE), 'member', split_axis=0...]
    unnamed x24 -> x18, local copies, waits for them, and re-layouts: 74.7 us -> 2.18 us
    pallas_call x0 -> x6, Pallas kernels: none -> 44 us  [call(): pl.pallas_call(kernel, grid=(1,) if grid is None else grid, in_specs=spec...]
    gather x5 -> x0, local copies, waits for them, and re-layouts: 37.4 us -> none  [the longest x2 18.9 us: to_slots(): return values[source].reshape((members, slots) + values.shape[1:])]
    ppermute x6 -> x7, waiting for transfers between devices: 26.8 us -> 3.07 us  [the longest x2 2.23 us: exchanged(): from_right = lax.ppermute(left, axes, to_left)]
    dot_general x7 -> x0, matrix products: 21.4 us -> none  [the longest x3 9.34 us: smooth_rows(): jnp.einsum('nij,ncj->nci', a_rows[:, k], other, preferred_element_type=jn...]
    pad x2 -> x0, matrix products: 7.42 us -> none  [product_rows(): total = total + jnp.pad(prod, ((0, 0), (k, 2 - k), (0, 0), (0, 0)))]
    squeeze x2 -> x0, local copies, waits for them, and re-layouts: 6.37 us -> none  [smooth_rows(): a_rows[:, 1]]
  transfers between devices with their start and end apart: 9 -> 9, of which waited for: 4 -> 4; matrix products, arithmetic and copies ran while one was open for 19% -> 0% of each run, Pallas kernels for 0% -> 26%
where the time goes in v1:
time: 113 us
  Pallas kernels  44 us (39%)
  starting transfers between devices  39.3 us (35%)
  waiting for transfers between devices  24.3 us (22%)
  local copies, waits for them, and re-layouts  2.86 us (3%)
  other arithmetic  1.34 us (1%)
    pallas_call x6, Pallas kernels, call(): pl.pallas_call(kernel, grid=(1,) if grid is None else grid, in_specs=spec...  44 us
    all_to_all x1, starting transfers between devices, per_device(): lax.all_to_all(packed.reshape(MEMBERS, SLOTS, COLS), 'member', split_axis...  16.2 us
    all_to_all x1, waiting for transfers between devices, per_device(): lax.all_to_all(sums.reshape(MEMBERS, SLOTS, WIDE), 'member', split_axis=0...  13.8 us
    ppermute x2, starting transfers between devices, exchanged(): from_right = lax.ppermute(left, axes, to_left)  12.6 us
    all_to_all x1, waiting for transfers between devices, per_device(): lax.all_to_all(packed.reshape(MEMBERS, SLOTS, COLS), 'member', split_axis...  7.41 us
    all_to_all x1, starting transfers between devices, per_device(): lax.all_to_all(sums.reshape(MEMBERS, SLOTS, WIDE), 'member', split_axis=0...  6.63 us
  transfers between devices with their start and end apart: 9, of which 4 were waited for; matrix products, arithmetic and copies ran while one was open for 0% of the time, Pallas kernels for 26%

profile of v1, /device:TPU:3, one launch (start us, length us, event | category | flops | bytes accessed | tf_op | source)
XLA Modules:
  0.0 112.6 jit_solution(2546575333665301730)
XLA Ops:
  0.6 0.7 slice.3
  1.3 1.3 %pad_add_fusion = s32[256]{0:T(256)} fusion(s32[64]{0:T(128)S(1)} %slice.3, s32[192]{0:T(256)} %param.5), kind=kLoop, calls=%fused_computation | loop fusion | flops 256 | bytes 2048 | tf_op jit(solution)/shard_map/concatenate | solution.py:424
  2.7 2.1 %rims.1 = (bf16[192,128]{1,0:T(8,128)(2,1)}, bf16[192,128]{1,0:T(8,128)(2,1)}, bf16[192,128]{1,0:T(8,128)(2,1)}) custom-call(s32[1]{0:T(128)} %bitcast.1.me_ref, s32[1,256]{1,0:T(1,128)} %bitcast.26, bf16[384,192]{1,0:T(8,128)(2,1)} %bitcast.20), custom_call_target="tpu_custom_call" | custom-call | bytes 295940 | tf_op jit(solution)/shard_map/rims/pallas_call | solution.py:391
  4.7 1.9 %collective-permute-start = (bf16[192,128]{1,0:T(8,128)(2,1)}, bf16[192,128]{1,0:T(8,128)(2,1)S(1)}, u32[]{:S(2)}, u32[]{:S(2)}) collective-permute-start(bf16[192,128]{1,0:T(8,128)(2,1)} %get-tuple-element.15), channel_id=1, source_target_pairs={{63,0},{0,1},{1,2},{2,3},{3,4},{4,5},{5,6},{6,7},{7,8},{8,9},{9,10... | collective-permute-start | bytes 147464 | tf_op jit(solution)/shard_map/ppermute | solution.py:417
  6.6 0.0 collective-permute-start.1
  6.6 0.7 collective-permute-start.2
  7.2 0.8 collective-permute-done.from_left_ref
  8.1 2.2 %collective-permute-done.1.from_right_ref = bf16[192,128]{1,0:T(8,128)(2,1)S(1)} collective-permute-done((bf16[192,128]{1,0:T(8,128)(2,1)}, bf16[192,128]{1,0:T(8,128)(2,1)S(1)}, u32[]{:S(2)}, u32[]{:S(2)}) %collective-permute-start.1) | collective-permute-done | bytes 49184 | tf_op jit(solution)/shard_map/ppermute | solution.py:416
  10.3 0.0 collective-permute-done.2.far_ref
  10.3 0.6 copy-done.3
  10.9 0.0 copy-done.4
  10.9 9.5 %smooth.1 = (bf16[18,64,192]{2,1,0:T(8,128)(2,1)}, bf16[576,128]{1,0:T(8,128)(2,1)}, bf16[576,128]{1,0:T(8,128)(2,1)}, bf16[576,128]{1,0:T(8,128)(2,1)}) custom-call(s32[1]{0:T(128)} %bitcast.1.me_ref, s32[1,256]{1,0:T(1,128)} %bitcast.27, bf16[3,64,64,192]{3,2,1,0:T(8,128)(2,1)} %bitcast.16, bf16[384,192]{1,0:T(8,128)(2,1)} %bitcast.21, ...), custom_call_target="tpu_custom_call" | custom-call | flops 1000000000 | bytes 5899268 | tf_op jit(solution)/shard_map/smooth/pallas_call | solution.py:391
  20.5 0.1 collective-permute-start.3
  20.6 12.6 %collective-permute-start.4 = (bf16[576,128]{1,0:T(8,128)(2,1)}, bf16[576,128]{1,0:T(8,128)(2,1)S(1)}, u32[]{:S(2)}, u32[]{:S(2)}) collective-permute-start(bf16[576,128]{1,0:T(8,128)(2,1)} %get-tuple-element.20), channel_id=1, source_target_pairs={{0,63},{1,0},{2,1},{3,2},{4,3},{5,4},{6,5},{7,6},{8,7},{9,8},{10,9... | collective-permute-start | bytes 442376 | tf_op jit(solution)/shard_map/ppermute | solution.py:416
  33.2 0.7 collective-permute-start.5
  33.9 3.0 %pack.1 = bf16[512,1152]{1,0:T(8,128)(2,1)} custom-call(s32[1,256]{1,0:T(1,128)} %bitcast.28, bf16[1152,192]{1,0:T(8,128)(2,1)} %bitcast.22), custom_call_target="tpu_custom_call" | custom-call | bytes 1623040 | tf_op jit(solution)/shard_map/pack/pallas_call | solution.py:391
  36.9 0.0 collective-permute-done.3.from_left_ref
  36.9 0.0 collective-permute-done.4.from_right_ref
  36.9 0.0 copy-start.7
  36.9 0.0 collective-permute-done.5.far_ref
  37.0 0.6 copy-done.6
  37.6 0.0 copy-done.7
  37.6 0.1 copy-done.8
  37.7 16.2 %all-to-all-start = ((bf16[64,8,1152]{2,1,0:T(8,128)(2,1)}), bf16[64,8,1152]{2,1,0:T(8,128)(2,1)S(1)}, u32[]{:S(2)}, u32[]{:S(2)}) async-start(bf16[64,8,1152]{2,1,0:T(8,128)(2,1)} %bitcast.18), calls=%async_computation | async-start | bytes 2359296 | tf_op jit(solution)/shard_map/all_to_all | solution.py:456
  53.9 23.3 %product.1 = (f32[512,256]{1,0:T(8,128)}, f32[8,256]{1,0:T(8,128)}) custom-call(s32[1]{0:T(128)} %bitcast.1.me_ref, s32[1,256]{1,0:T(1,128)} %bitcast.29, bf16[3,64,64,192]{3,2,1,0:T(8,128)(2,1)} %bitcast.17, bf16[1152,192]{1,0:T(8,128)(2,1)} %bitcast.23, bf16[576,128]{1,0:T(8,128)(2,1)} %copy-done.6, bf16[576,128]{1,0:T(8,128)(2,1)} %copy-done.7, ...), custom_call_target="tpu_custom_call" | custom-call | flops 10000000000 | bytes 6136836 | tf_op jit(solution)/shard_map/product/pallas_call | solution.py:391
  77.2 7.4 %all-to-all-done = bf16[64,8,1152]{2,1,0:T(8,128)(2,1)S(1)} async-done(((bf16[64,8,1152]{2,1,0:T(8,128)(2,1)}), bf16[64,8,1152]{2,1,0:T(8,128)(2,1)S(1)}, u32[]{:S(2)}, u32[]{:S(2)}) %all-to-all-start) | async-done | bytes 1179680 | tf_op jit(solution)/shard_map/all_to_all | solution.py:456
  84.6 6.6 %all-to-all-start.1 = ((f32[64,8,256]{2,1,0:T(8,128)}), f32[64,8,256]{2,1,0:T(8,128)S(1)}, u32[]{:S(2)}, u32[]{:S(2)}) async-start(f32[64,8,256]{2,1,0:T(8,128)} %bitcast.25), calls=%async_computation.1 | async-start | bytes 1048576 | tf_op jit(solution)/shard_map/all_to_all | solution.py:477
  91.3 0.7 collective-permute-start.6
  91.9 3.2 %unpack_smooth.1 = bf16[1152,192]{1,0:T(8,128)(2,1)} custom-call(bf16[512,1152]{1,0:T(8,128)(2,1)} %bitcast.14), custom_call_target="tpu_custom_call" | custom-call | bytes 1622016 | tf_op jit(solution)/shard_map/unpack_smooth/pallas_call | solution.py:391
  95.1 13.8 %all-to-all-done.1 = f32[64,8,256]{2,1,0:T(8,128)S(1)} async-done(((f32[64,8,256]{2,1,0:T(8,128)}), f32[64,8,256]{2,1,0:T(8,128)S(1)}, u32[]{:S(2)}, u32[]{:S(2)}) %all-to-all-start.1) | async-done | bytes 524320 | tf_op jit(solution)/shard_map/all_to_all | solution.py:477
  109.0 0.8 copy-done.1
  109.8 2.8 %unpack_coarse.1 = f32[192,252]{1,0:T(8,128)} custom-call(s32[1]{0:T(128)} %bitcast.1.me_ref, bf16[512,1152]{1,0:T(8,128)(2,1)} %bitcast.15, f32[512,256]{1,0:T(8,128)} %bitcast.19, f32[8,256]{1,0:T(8,128)} %copy-done.5), custom_call_target="tpu_custom_call" | custom-call | bytes 1905668 | tf_op jit(solution)/shard_map/unpack_coarse/pallas_call | solution.py:391
  (12 shorter events, 0.0 us)
Async XLA Ops:
  4.7 3.4 %collective-permute-start = (bf16[192,128]{1,0:T(8,128)(2,1)}, bf16[192,128]{1,0:T(8,128)(2,1)S(1)}, u32[]{:S(2)}, u32[]{:S(2)}) collective-permute-start(bf16[192,128]{1,0:T(8,128)(2,1)} %get-tuple-element.15), channel_id=1, source_target_pairs={{63,0},{0,1},{1,2},{2,3},{3,4},{4,5},{5,6},{6,7},{7,8},{8,9},{9,10... | collective-permute-start | bytes 147464 | tf_op jit(solution)/shard_map/ppermute | solution.py:417
  6.6 3.7 %collective-permute-start.1 = (bf16[192,128]{1,0:T(8,128)(2,1)}, bf16[192,128]{1,0:T(8,128)(2,1)S(1)}, u32[]{:S(2)}, u32[]{:S(2)}) collective-permute-start(bf16[192,128]{1,0:T(8,128)(2,1)} %get-tuple-element.16), channel_id=1, source_target_pairs={{0,63},{1,0},{2,1},{3,2},{4,3},{5,4},{6,5},{7,6},{8,7},{9,8},{10,9... | collective-permute-start | bytes 147464 | tf_op jit(solution)/shard_map/ppermute | solution.py:416
  6.6 3.7 %collective-permute-start.2 = (bf16[192,128]{1,0:T(8,128)(2,1)}, bf16[192,128]{1,0:T(8,128)(2,1)S(1)}, u32[]{:S(2)}, u32[]{:S(2)}) collective-permute-start(bf16[192,128]{1,0:T(8,128)(2,1)} %get-tuple-element.17), channel_id=1, source_target_pairs={{63,64},{64,63},{127,128},{128,127},{191,192},{192,191}} | collective-permute-start | bytes 147464 | tf_op jit(solution)/shard_map/ppermute | solution.py:418
  8.1 2.2 %copy-start.2 = (bf16[192,128]{1,0:T(8,128)(2,1)}, bf16[192,128]{1,0:T(8,128)(2,1)S(1)}, u32[]{:S(2)}) copy-start(bf16[192,128]{1,0:T(8,128)(2,1)S(1)} %collective-permute-done.from_left_ref) | copy-start | bytes 147460
  10.3 0.6 copy-start.3
  10.3 0.6 copy-start.4
  20.5 16.4 %collective-permute-start.3 = (bf16[576,128]{1,0:T(8,128)(2,1)}, bf16[576,128]{1,0:T(8,128)(2,1)S(1)}, u32[]{:S(2)}, u32[]{:S(2)}) collective-permute-start(bf16[576,128]{1,0:T(8,128)(2,1)} %get-tuple-element.19), channel_id=1, source_target_pairs={{63,0},{0,1},{1,2},{2,3},{3,4},{4,5},{5,6},{6,7},{7,8},{8,9},{9,10... | collective-permute-start | bytes 442376 | tf_op jit(solution)/shard_map/ppermute | solution.py:417
  20.6 16.3 %collective-permute-start.4 = (bf16[576,128]{1,0:T(8,128)(2,1)}, bf16[576,128]{1,0:T(8,128)(2,1)S(1)}, u32[]{:S(2)}, u32[]{:S(2)}) collective-permute-start(bf16[576,128]{1,0:T(8,128)(2,1)} %get-tuple-element.20), channel_id=1, source_target_pairs={{0,63},{1,0},{2,1},{3,2},{4,3},{5,4},{6,5},{7,6},{8,7},{9,8},{10,9... | collective-permute-start | bytes 442376 | tf_op jit(solution)/shard_map/ppermute | solution.py:416
  33.2 3.7 %collective-permute-start.5 = (bf16[576,128]{1,0:T(8,128)(2,1)}, bf16[576,128]{1,0:T(8,128)(2,1)S(1)}, u32[]{:S(2)}, u32[]{:S(2)}) collective-permute-start(bf16[576,128]{1,0:T(8,128)(2,1)} %get-tuple-element.21), channel_id=1, source_target_pairs={{63,64},{64,63},{127,128},{128,127},{191,192},{192,191}} | collective-permute-start | bytes 442376 | tf_op jit(solution)/shard_map/ppermute | solution.py:418
  36.9 0.7 copy-start.6
  36.9 0.7 copy-start.7
  37.0 0.7 copy-start.8
  37.7 46.9 %all-to-all-start = ((bf16[64,8,1152]{2,1,0:T(8,128)(2,1)}), bf16[64,8,1152]{2,1,0:T(8,128)(2,1)S(1)}, u32[]{:S(2)}, u32[]{:S(2)}) async-start(bf16[64,8,1152]{2,1,0:T(8,128)(2,1)} %bitcast.18), calls=%async_computation | async-start | bytes 2359296 | tf_op jit(solution)/shard_map/all_to_all | solution.py:456
  84.6 7.3 %copy-start = (bf16[64,8,1152]{2,1,0:T(8,128)(2,1)}, bf16[64,8,1152]{2,1,0:T(8,128)(2,1)S(1)}, u32[]{:S(2)}) copy-start(bf16[64,8,1152]{2,1,0:T(8,128)(2,1)S(1)} %all-to-all-done) | copy-start | bytes 3538948
  84.6 24.4 %all-to-all-start.1 = ((f32[64,8,256]{2,1,0:T(8,128)}), f32[64,8,256]{2,1,0:T(8,128)S(1)}, u32[]{:S(2)}, u32[]{:S(2)}) async-start(f32[64,8,256]{2,1,0:T(8,128)} %bitcast.25), calls=%async_computation.1 | async-start | bytes 1048576 | tf_op jit(solution)/shard_map/all_to_all | solution.py:477
  91.3 3.9 %collective-permute-start.6 = (f32[8,256]{1,0:T(8,128)}, f32[8,256]{1,0:T(8,128)S(1)}, u32[]{:S(2)}, u32[]{:S(2)}) collective-permute-start(f32[8,256]{1,0:T(8,128)} %get-tuple-element.27), channel_id=1, source_target_pairs={{63,64},{64,63},{127,128},{128,127},{191,192},{192,191}} | collective-permute-start | bytes 24584 | tf_op jit(solution)/shard_map/ppermute | solution.py:476
  95.1 13.8 %copy-start.5 = (f32[8,256]{1,0:T(8,128)}, f32[8,256]{1,0:T(8,128)S(1)}, u32[]{:S(2)}) copy-start(f32[8,256]{1,0:T(8,128)S(1)} %collective-permute-done.6.far_ref) | copy-start | bytes 24580
  109.0 0.8 copy-start.1

commit v2 on v1

v2 whole, which is shorter than its diff:
```python
import jax
import jax.numpy as jnp
from jax import lax
from jax.experimental import pallas as pl
from jax.experimental.pallas import tpu as pltpu
from jax.sharding import PartitionSpec as P

ROWS = 192
WIDE = 256
TILE = 64
MODES = 6
MEMBERS = 64
SLOTS = 8
COLS = 3 * MODES * TILE
F32 = jnp.float32
BF16 = jnp.bfloat16
NT = (((1,), (1,)), ((), ()))
TN = (((0,), (0,)), ((), ()))
MIB = 1024 * 1024
PACKED = 56


def iota(shape, axis):
    return lax.broadcasted_iota(jnp.int32, shape, axis)


def ones_where(mask):
    return jnp.where(mask, 1.0, 0.0).astype(BF16)


def dot(a, b):
    return jnp.dot(a, b, preferred_element_type=F32)


def parts_of(x):
    high = x.astype(BF16)
    rest = x - high.astype(F32)
    mid = rest.astype(BF16)
    low = (rest - mid.astype(F32)).astype(BF16)
    return high, mid, low


def exact_dot(pick, x, dims, pick_first):
    total = None
    for part in parts_of(x):
        ab = (pick, part) if pick_first else (part, pick)
        prod = lax.dot_general(*ab, dims, preferred_element_type=F32)
        total = prod if total is None else total + prod
    return total


def rank_arrays(owner_row):
    owner_row = owner_row.astype(F32)
    owner_row = jnp.concatenate([owner_row, owner_row[:, 128:]], 1)
    wide = jnp.broadcast_to(owner_row, (WIDE, WIDE))
    tall = wide.T[:ROWS]
    wide = wide[:ROWS]
    lane = iota((ROWS, WIDE), 1)
    row_l = jnp.where(lane < ROWS, lane, lane - TILE)
    row_s = iota((ROWS, WIDE), 0)
    one = jnp.where(wide == tall, 1.0, 0.0)
    less, more = row_s < row_l, row_s > row_l
    rank_l = jnp.sum(jnp.where(less, one, 0.0), 0, keepdims=True)
    after_l = jnp.sum(jnp.where(more, one, 0.0), 0, keepdims=True)
    once = jnp.where(lane < ROWS, one, 0.0)
    rank_s = jnp.sum(jnp.where(more, once, 0.0), 1, keepdims=True)
    after_s = jnp.sum(jnp.where(less, once, 0.0), 1, keepdims=True)
    return (wide[:1], rank_l, after_l), (tall[:, :1], rank_s, after_s)


class Order:
    def __init__(self, wide_ref, tall_ref):
        self.owner_l, self.rank_l, self.after_l = (wide_ref[n : n + 1, :] for n in range(3))
        self.owner_s, self.rank_s, self.after_s = (tall_ref[:, n : n + 1] for n in range(3))


def rim_picks(r, me):
    lane = iota((ROWS, 128), 1)
    first, last = r.rank_s == 0.0, r.after_s == 0.0
    even = me % 2 == 0
    picks = []
    for half in (0, 1):
        slot = lane - TILE * half
        inside = (slot >= 0) & (slot < TILE)
        to_left = jnp.where(inside, slot + jnp.where(me == 0, 1, 0), -1).astype(F32)
        to_right = jnp.where(inside, slot - jnp.where(me == MEMBERS - 1, 1, 0), -1).astype(F32)
        left = jnp.where((r.owner_s == to_left) & first, 1.0, 0.0)
        right = jnp.where((r.owner_s == to_right) & last, 1.0, 0.0)
        near = jnp.where(even, right, left).astype(BF16)
        far = jnp.where(even, left, right).astype(BF16)
        picks.append((near, far))
    return picks


def far_pick(r, me, width):
    top = iota((8, width), 0) == 0
    owner, rank, after = r.owner_l[:, :width], r.rank_l[:, :width], r.after_l[:, :width]
    head = top & (me == 0) & (owner == 0.0) & (rank == 0.0)
    tail = top & (me == MEMBERS - 1) & (owner == MEMBERS - 1.0) & (after == 0.0)
    return ones_where(head), ones_where(tail)


def rims_of(rows, r, me):
    half = rows.shape[0] // 2
    top, bottom = rim_picks(r, me)
    rims = [(dot(rows[:half], a) + dot(rows[half:], b)).astype(BF16) for a, b in zip(top, bottom)]
    head, tail = far_pick(r, me, ROWS)
    far = lax.dot_general(head + tail, rows, NT, preferred_element_type=F32).astype(BF16)
    return [far] + rims[::-1]


def neighbours(rows, near, away, far, r, me):
    lane = iota((ROWS, WIDE), 1)
    row_l = jnp.where(lane < ROWS, lane, lane - TILE)
    same = r.owner_l == r.owner_s
    before = ones_where(same & (r.rank_s + 1.0 == r.rank_l))
    after = ones_where(same & (r.rank_s == r.rank_l + 1.0))
    here = ones_where(iota((ROWS, WIDE), 0) == row_l)
    bucket = iota((128, WIDE), 0)
    even = me % 2 == 0
    from_left = jnp.where(even, away, near)
    from_right = jnp.where(even, near, away)
    head, tail = far_pick(r, me, WIDE)
    result = []
    for local, rim, edge, end in (
        (before, from_left, r.rank_l, head), (here, None, None, None), (after, from_right, r.after_l, tail)
    ):
        own = dot(rows, local)
        if rim is not None:
            ends = []
            for side in (0, 1):
                want = bucket - TILE * side
                want = jnp.where((want >= 0) & (want < TILE), want, -1).astype(F32)
                ends.append(dot(rim, ones_where((want == r.owner_l) & (edge == 0.0))))
            own = own + jnp.concatenate(ends, 0)
            own = own + lax.dot_general(far, end, TN, preferred_element_type=F32)
        result.append(own)
    return result


def set_wide(ref, k, value):
    for tile in (0, 1):
        part = value[:, 128 * tile : 128 * (tile + 1)]
        ref[tile, k] = part.reshape(-1, TILE, 128)


def chunk_copy(a_hbm, a_ref, sems, n):
    return pltpu.make_async_copy(a_hbm.at[:, pl.ds(16 * n, 16)], a_ref.at[:, pl.ds(16 * n, 16)], sems.at[n])


def start_copies(a_hbm, a_ref, sems):
    for n in range(TILE // 16):
        chunk_copy(a_hbm, a_ref, sems, n).start()


def set_groups(a_ref, ib, group_ref):
    for k in range(3):
        for i in range(8):
            low, high = (a_ref[k, 16 * ib + i + n].astype(F32) for n in (0, 8))
            group_ref[0, k, i] = low[:, :128]
            group_ref[1, k, i] = high[:, :128]
            group_ref[2, k, i] = jnp.concatenate([low[:, 128:], high[:, 128:]], 1)


def folded(terms):
    sub = iota((8, 128), 0)
    for shift in (1, 2, 4):
        keep = (sub & shift) == 0
        terms = [
            jnp.where(keep, x, y) + pltpu.roll(jnp.where(keep, y, x), shift, 0)
            for x, y in zip(terms[::2], terms[1::2])
        ]
    return terms[0]


def contracted(group_ref, wide_ref, g, tile, pairs, columns):
    totals = [[None] * 8 for _ in columns]
    for jb in range(TILE // 8):
        j = pl.ds(8 * jb, 8)
        for k, base in pairs:
            a = [group_ref[g, k, i, j, :] for i in range(8)]
            for n, column in enumerate(columns):
                x = wide_ref[tile, k, base + column, j, :]
                for i in range(8):
                    term = a[i] * x
                    totals[n][i] = term if totals[n][i] is None else totals[n][i] + term
    return [folded(t) for t in totals]


def ungrouped(out_ref, index):
    low, high, both = out_ref[0, index], out_ref[1, index], out_ref[2, index]
    top = jnp.concatenate([low, both[:, :TILE]], 1)
    bottom = jnp.concatenate([high, both[:, TILE:]], 1)
    return jnp.concatenate([top, bottom], 0)


def first_kernel(me_ref, owner_ref, p_ref, wide_ref, tall_ref, far_out, away_out, near_out):
    rows, columns = rank_arrays(owner_ref[...])
    wide_ref[...] = jnp.zeros_like(wide_ref)
    for n in range(3):
        wide_ref[n : n + 1, :] = rows[n]
    lane = iota((ROWS, 128), 1)
    tall_ref[...] = jnp.where(lane == 0, columns[0], jnp.where(lane == 1, columns[1], columns[2]))
    r = Order(wide_ref, tall_ref)
    for ref, rim in zip((far_out, away_out, near_out), rims_of(p_ref[...], r, me_ref[0])):
        ref[...] = rim


def smooth_kernel(
    me_ref, order_l_ref, order_s_ref, a_hbm, p_ref, far_ref, away_ref, near_ref,
    s_ref, far_out, away_out, near_out, a_ref, sems, group_ref, wide_ref, out_ref,
):
    ib = pl.program_id(0)
    me = me_ref[0]

    @pl.when(ib == 0)
    def _():
        start_copies(a_hbm, a_ref, sems)
        r = Order(order_l_ref, order_s_ref)
        near = neighbours(p_ref[...], near_ref[...], away_ref[...], far_ref[...], r, me)
        for k, value in enumerate(near):
            set_wide(wide_ref, k, value)

    chunk_copy(a_hbm, a_ref, sems, ib).wait()
    set_groups(a_ref, ib, group_ref)
    sub, lane = iota((8, 128), 0), iota((8, 128), 1)

    def one_group(g, carry):
        tile = jnp.where(g == 2, 1, 0)
        second = (g == 1) | ((g == 2) & (lane >= TILE))
        lower, upper = pl.ds(pl.multiple_of(16 * ib, 8), 8), pl.ds(pl.multiple_of(16 * ib + 8, 8), 8)
        diag = jnp.zeros((8, 128), F32)
        for i in range(8):
            entry = jnp.where(second, group_ref[g, 1, i, upper, :], group_ref[g, 1, i, lower, :])
            diag = jnp.where(sub == i, entry, diag)
        scale = 0.6 * (1.0 / diag)
        for k in range(3):
            for half in (0, 1):
                columns = [3 * half + c for c in range(3)]
                sums = contracted(group_ref, wide_ref, g, tile, [(k, 0)], columns)
                for c, total in zip(columns, sums):
                    value = scale * total
                    if k == 1:
                        own = jnp.where(second, wide_ref[tile, 1, c, upper, :], wide_ref[tile, 1, c, lower, :])
                        value = own - value
                    else:
                        value = 0.0 - value
                    out_ref[g, 6 * k + c] = value
        return carry

    lax.fori_loop(0, 3, one_group, 0)
    rows = pl.ds(pl.multiple_of(16 * ib, 16), 16)
    for index in range(18):
        s_ref[index, rows, :] = ungrouped(out_ref, index).astype(BF16)

    @pl.when(ib == pl.num_programs(0) - 1)
    def _():
        r = Order(order_l_ref, order_s_ref)
        flat = s_ref[...].reshape(COLS, ROWS)
        for ref, rim in zip((far_out, away_out, near_out), rims_of(flat, r, me)):
            ref[...] = rim


def slot_grid(width):
    spot = iota((MEMBERS * SLOTS, width), 0)
    return (spot // SLOTS).astype(F32), (spot % SLOTS).astype(F32)


def pack_kernel(order_l_ref, s_ref, out_ref):
    member, slot = slot_grid(ROWS)
    owner, rank = order_l_ref[0:1, :ROWS], order_l_ref[1:2, :ROWS]
    mine = owner == member
    pick = ones_where(mine & (rank == slot))
    count = jnp.sum(jnp.where(mine, 1.0, 0.0), 1, keepdims=True)
    for block in range(COLS // 128):
        value = lax.dot_general(
            pick, s_ref[128 * block : 128 * (block + 1), :], NT, preferred_element_type=F32
        ).reshape(MEMBERS, SLOTS, 128)
        out_ref[:, 6 * block : 6 * block + 6, :] = value[:, :6, :].astype(BF16)
    counts = jnp.broadcast_to(count, (MEMBERS * SLOTS, 128)).reshape(MEMBERS, SLOTS, 128)
    out_ref[:, 54:56, :] = counts[:, :2, :].astype(BF16)


OFFSETS = [[(k, 6 * (e - k)) for k in range(3) if 0 <= e - k <= 2] for e in range(5)]


def product_kernel(
    me_ref, order_l_ref, order_s_ref, a_hbm, s_ref, far_ref, away_ref, near_ref,
    out_ref, far_out, a_ref, sems, group_ref, wide_ref, ap_ref, own_ref, term_ref,
):
    ib = pl.program_id(0)
    me = me_ref[0]

    @pl.when(ib == 0)
    def _():
        start_copies(a_hbm, a_ref, sems)
        r = Order(order_l_ref, order_s_ref)
        near = neighbours(s_ref[...], near_ref[...], away_ref[...], far_ref[...], r, me)
        for k, value in enumerate(near):
            set_wide(wide_ref, k, value)
        term_ref[...] = jnp.zeros_like(term_ref)

    chunk_copy(a_hbm, a_ref, sems, ib).wait()
    set_groups(a_ref, ib, group_ref)
    lane = iota((8, 128), 1)

    def one_group(step, carry):
        g, half = step // 2, step % 2
        tile = jnp.where(g == 2, 1, 0)
        for e in range(5):
            columns = [3 * half + c for c in range(3)]
            sums = contracted(group_ref, wide_ref, g, tile, OFFSETS[e], columns)
            for c, total in zip(columns, sums):
                ap_ref[g, ib, 6 * e + c] = total.astype(BF16).astype(F32)
        second = (g == 1) | ((g == 2) & (lane >= TILE))
        lower, upper = pl.ds(pl.multiple_of(16 * ib, 8), 8), pl.ds(pl.multiple_of(16 * ib + 8, 8), 8)
        for c in range(9):
            column = 9 * half + c
            own_ref[g, ib, column] = jnp.where(
                second, wide_ref[tile, 1, column, upper, :], wide_ref[tile, 1, column, lower, :]
            )
        return carry

    lax.fori_loop(0, 6, one_group, 0)

    @pl.when(ib == pl.num_programs(0) - 1)
    def _():
        def one_pair(step, carry):
            k, e = step // 5, step % 5
            for c in range(6):
                near, far = [None] * 6, [None] * 6
                for block in range(TILE // 16):
                    for g in range(3):
                        x = own_ref[g, block, 6 * k + c]
                        for d in range(6):
                            term = x * ap_ref[g, block, 6 * e + d]
                            sums = far if g == 2 else near
                            sums[d] = term if sums[d] is None else sums[d] + term
                for d in range(6):
                    row = slice(6 * c + d, 6 * c + d + 1)
                    tail = jnp.sum(far[d], 0, keepdims=True)
                    term_ref[step, row, 0:128] = jnp.sum(near[d], 0, keepdims=True)
                    term_ref[step, row, 128:ROWS] = tail[:, :TILE] + tail[:, TILE:]
            return carry

        lax.fori_loop(0, 15, one_pair, 0)
        r = Order(order_l_ref, order_s_ref)
        owner, rank, after = (x[:, :ROWS] for x in (r.owner_l, r.rank_l, r.after_l))
        member, slot = slot_grid(ROWS)
        mine, row_slot = owner == member, slot < 6.0
        here = ones_where(mine & (rank == slot))
        back_to = member + jnp.where(me == 0, 1.0, 0.0)
        on_to = member - jnp.where(me == MEMBERS - 1, 1.0, 0.0)
        back = (mine & row_slot & (rank == slot + 1.0)) | ((slot == 6.0) & (owner == back_to) & (rank == 0.0))
        on = (mine & row_slot & (rank == slot - 1.0) & (after > 0.0)) | (
            (slot == 7.0) & (owner == on_to) & (after == 0.0)
        )
        picks = [ones_where(back), here, ones_where(on)]
        terms = []
        for k in range(3):
            pieces = [term_ref[5 * k + e][:36, :ROWS] for e in range(5)]
            pieces.append(jnp.zeros((4 + 36 * k, ROWS), F32))
            if k < 2:
                pieces.insert(0, jnp.zeros((72 - 36 * k, ROWS), F32))
            terms.append(jnp.concatenate(pieces, 0))
        total = None
        for k in range(3):
            prod = exact_dot(picks[k], terms[k], NT, True)
            total = prod if total is None else total + prod
        out_ref[...] = total
        head, tail = far_pick(r, me, ROWS)
        far_out[...] = exact_dot(head, terms[0], NT, True) + exact_dot(tail, terms[2], NT, True)


def unpack_smooth_kernel(recv_ref, out_ref, pick_out):
    size = MEMBERS * SLOTS
    count = jnp.broadcast_to(recv_ref[:, 54:55, :].astype(F32), (MEMBERS, SLOTS, 128)).reshape(size, 128)
    source, other = iota((size, size), 0) // SLOTS, iota((size, size), 1) // SLOTS
    first_slot = iota((size, size), 1) % SLOTS == 0
    earlier = ones_where((other < source) & first_slot)
    start = dot(earlier, count.astype(BF16))[:, :1]
    count = count[:, :1]
    slot = (iota((size, 1), 0) % SLOTS).astype(F32)
    place = jnp.where(slot < count, start + slot, -1.0)
    column = iota((size, ROWS), 1).astype(F32)
    pick = ones_where(place == column)
    for block in range(COLS // 128):
        rows = recv_ref[:, 6 * block : 6 * block + 6, :].astype(F32)
        rows = jnp.concatenate([rows, jnp.zeros((MEMBERS, 2, 128), F32)], 1).reshape(size, 128)
        value = lax.dot_general(rows.astype(BF16), pick, TN, preferred_element_type=F32)
        out_ref[128 * block : 128 * (block + 1), :] = value.astype(BF16)
    place = jnp.where(slot == 6.0, jnp.where(start == 0.0, ROWS - 1.0, start - 1.0), place)
    stop = start + count
    place = jnp.where(slot == 7.0, jnp.where(stop == float(ROWS), 0.0, stop), place)
    column = iota((size, WIDE), 1).astype(F32)
    pick_out[...] = jnp.where(place == column, 1.0, 0.0).T[:ROWS].astype(BF16)


def unpack_coarse_kernel(me_ref, pick_ref, sums_ref, far_ref, out_ref):
    me = me_ref[0]
    total = exact_dot(pick_ref[...], sums_ref[...], (((1,), (0,)), ((), ())), True)
    row = iota((ROWS, WIDE), 0)
    edge = jnp.where(me == 0, 0, ROWS - 1)
    far = jnp.broadcast_to(far_ref[0:1, :], (ROWS, WIDE))
    total = total + jnp.where(row == edge, far, 0.0)
    out_ref[...] = total[:, :252]


def call(kernel, outs, args, grid=None, in_specs=None, scratch=(), flops=0, mib=16, name=None):
    whole = lambda shape: pl.BlockSpec(shape, lambda *_: (0,) * len(shape))
    specs = []
    for n, arg in enumerate(args):
        spec = None if in_specs is None else in_specs.get(n)
        if spec is None:
            spec = pl.BlockSpec(memory_space=pltpu.SMEM) if arg.shape == (1,) else whole(arg.shape)
        specs.append(spec)
    moved = sum(a.size * a.dtype.itemsize for a in args) + sum(o.size * o.dtype.itemsize for o in outs)
    return pl.pallas_call(
        kernel,
        grid=(1,) if grid is None else grid,
        in_specs=specs,
        out_specs=[whole(o.shape) for o in outs],
        out_shape=outs,
        scratch_shapes=list(scratch),
        compiler_params=pltpu.CompilerParams(vmem_limit_bytes=mib * MIB),
        cost_estimate=pl.CostEstimate(flops=flops, bytes_accessed=moved, transcendentals=0),
        name=name,
    )(*args)


def shaped(shape, dtype=BF16):
    return jax.ShapeDtypeStruct(shape, dtype)


def swaps(groups):
    ring, axes = MEMBERS, range(groups)
    both = lambda pairs: [q for a, b in pairs for q in ((a, b), (b, a))]
    across = both([(g * ring - 1, g * ring) for g in range(1, groups)])
    away = both([(g * ring + i, g * ring + (i + 1) % ring) for g in axes for i in range(1, ring, 2)])
    near = both([(g * ring + i, g * ring + i + 1) for g in axes for i in range(0, ring, 2)])
    return across, away, near


def per_device(a_band, p_tent, new_owner):
    axes = ("group", "member")
    across, away_pairs, near_pairs = swaps(lax.axis_size("group"))
    me = lax.axis_index("member").astype(jnp.int32).reshape(1)
    a = a_band.transpose(1, 2, 3, 0)
    p = p_tent.transpose(1, 2, 0).reshape(MODES * TILE, ROWS)
    a_spec = pl.BlockSpec(memory_space=pltpu.HBM)
    grid = (TILE // 16,)
    a_scratch = [
        pltpu.VMEM((3, TILE, TILE, ROWS), BF16),
        pltpu.SemaphoreType.DMA((TILE // 16,)),
        pltpu.VMEM((3, 3, 8, TILE, 128), F32),
    ]

    def exchanged(far, away, near):
        far = lax.ppermute(far, axes, across)
        away = lax.ppermute(away, axes, away_pairs)
        return far, away, lax.ppermute(near, axes, near_pairs)

    def rims(length):
        return [shaped((8, length)), shaped((length // 2, 128)), shaped((length // 2, 128))]

    order_l, order_s, *sent = call(
        first_kernel,
        [shaped((8, WIDE), F32), shaped((ROWS, 128), F32)] + rims(MODES * TILE),
        (me, new_owner.reshape(1, ROWS), p),
        name="rims",
    )
    got = exchanged(*sent)

    s, *sent = call(
        smooth_kernel,
        [shaped((18, TILE, ROWS))] + rims(COLS),
        (me, order_l, order_s, a, p, *got),
        grid=grid,
        in_specs={3: a_spec},
        scratch=[
            *a_scratch,
            pltpu.VMEM((2, 3, MODES, TILE, 128), F32),
            pltpu.VMEM((3, 18, 8, 128), F32),
        ],
        flops=10**9,
        mib=50,
        name="smooth",
    )
    got = exchanged(*sent)
    s = s.reshape(COLS, ROWS)
    (packed,) = call(pack_kernel, [shaped((MEMBERS, PACKED, 128))], (order_l, s), name="pack")
    packed, *got = lax.optimization_barrier((packed, *got))
    recv = lax.all_to_all(packed, "member", split_axis=0, concat_axis=0, tiled=True)

    sums, far = call(
        product_kernel,
        [shaped((MEMBERS * SLOTS, WIDE), F32), shaped((8, WIDE), F32)],
        (me, order_l, order_s, a, s, *got),
        grid=grid,
        in_specs={3: a_spec},
        scratch=[
            *a_scratch,
            pltpu.VMEM((2, 3, 18, TILE, 128), F32),
            pltpu.VMEM((3, TILE // 16, 30, 8, 128), F32),
            pltpu.VMEM((3, TILE // 16, 18, 8, 128), F32),
            pltpu.VMEM((15, 40, WIDE), F32),
        ],
        flops=10**10,
        mib=50,
        name="product",
    )
    far = lax.ppermute(far, axes, across)
    sums = lax.all_to_all(
        sums.reshape(MEMBERS, SLOTS, WIDE), "member", split_axis=0, concat_axis=0, tiled=True
    ).reshape(MEMBERS * SLOTS, WIDE)
    smooth, pick = call(
        unpack_smooth_kernel,
        [shaped((COLS, ROWS)), shaped((ROWS, MEMBERS * SLOTS))],
        (recv,),
        flops=10**9,
        name="unpack_smooth",
    )
    (coarse,) = call(
        unpack_coarse_kernel, [shaped((ROWS, 252), F32)], (me, pick, sums, far), name="unpack_coarse"
    )
    return smooth.reshape(3, MODES, TILE, ROWS).transpose(3, 0, 1, 2), coarse


def solution(mesh):
    in_specs = (
        P(("group", "member"), None, None, None),
        P(("group", "member"), None, None),
        P(("group", "member")),
    )
    out_specs = (P(("group", "member"), None, None, None), P(("group", "member"), None))
    return jax.shard_map(
        per_device, mesh=mesh, in_specs=in_specs, out_specs=out_specs, check_vma=False
    )
```

time: 113 us -> 97.4 us (0.86)
  Pallas kernels: 44 us -> 35.5 us
  waiting for transfers between devices: 24.3 us -> 18.5 us
  other arithmetic: 1.34 us -> 0 us
    pallas_call x6, Pallas kernels: 44 us -> 35.5 us  [call(): pl.pallas_call(kernel, grid=(1,) if grid is None else grid, in_specs=spec...]
    all_to_all x1, waiting for transfers between devices: 7.41 us -> 3.15 us  [per_device(): lax.all_to_all(packed, 'member', split_axis=0, concat_axis=0, tiled=True)]
    all_to_all x1, starting transfers between devices: 16.2 us -> 12.9 us  [per_device(): lax.all_to_all(packed, 'member', split_axis=0, concat_axis=0, tiled=True)]
    ppermute x7, starting transfers between devices: 16.5 us -> 19.7 us  [the longest x2 15.7 us: exchanged(): return (far, away, lax.ppermute(near, axes, near_pairs))]
    ppermute x7, waiting for transfers between devices: 3.07 us -> 0.22 us  [the longest x2 0.21 us: exchanged(): return (far, away, lax.ppermute(near, axes, near_pairs))]
    concatenate x1 -> x0, other arithmetic: 1.34 us -> none  [per_device(): owner = jnp.concatenate([new_owner, new_owner[128:]]).reshape(1, WIDE)]
    all_to_all x1, waiting for transfers between devices: 13.8 us -> 15.2 us  [per_device(): lax.all_to_all(sums.reshape(MEMBERS, SLOTS, WIDE), 'member', split_axis=0...]
    unnamed x18 -> x6, local copies, waits for them, and re-layouts: 2.18 us -> 2.53 us
  transfers between devices with their start and end apart: 9 -> 9, of which waited for: 4 -> 3; matrix products, arithmetic and copies ran while one was open for 0% -> 0% of each run, Pallas kernels for 26% -> 27%
where the time goes in v2:
time: 97.4 us; the launch traced here: 97 us
  starting transfers between devices  39.8 us (41%)
  Pallas kernels  35.5 us (36%)
  waiting for transfers between devices  18.5 us (19%)
  local copies, waits for them, and re-layouts  2.53 us (3%)
    pallas_call x6, Pallas kernels, call(): pl.pallas_call(kernel, grid=(1,) if grid is None else grid, in_specs=spec...  35.5 us
    ppermute x2, starting transfers between devices, exchanged(): return (far, away, lax.ppermute(near, axes, near_pairs))  15.7 us
    all_to_all x1, waiting for transfers between devices, per_device(): lax.all_to_all(sums.reshape(MEMBERS, SLOTS, WIDE), 'member', split_axis=0...  15.2 us
    all_to_all x1, starting transfers between devices, per_device(): lax.all_to_all(packed, 'member', split_axis=0, concat_axis=0, tiled=True)  12.9 us
    all_to_all x1, starting transfers between devices, per_device(): lax.all_to_all(sums.reshape(MEMBERS, SLOTS, WIDE), 'member', split_axis=0...  7.17 us
    all_to_all x1, waiting for transfers between devices, per_device(): lax.all_to_all(packed, 'member', split_axis=0, concat_axis=0, tiled=True)  3.15 us
    unnamed x6, local copies, waits for them, and re-layouts  2.53 us
    ppermute x2, starting transfers between devices, exchanged(): away = lax.ppermute(away, axes, away_pairs)  2.03 us
  transfers between devices with their start and end apart: 9, of which 3 were waited for; matrix products, arithmetic and copies ran while one was open for 0% of the time, Pallas kernels for 27%

profile of v2, /device:TPU:3, one launch (start us, length us, event | category | flops | bytes accessed | tf_op | source)
XLA Modules:
  0.0 97.0 jit_solution(5433224447517005191)
XLA Ops:
  0.6 0.0 copy-start
  0.6 0.9 copy-done
  1.6 0.0 copy-start.2
  1.6 0.7 copy-done.2
  2.2 0.8 rims.1
  3.0 1.9 %collective-permute-start.1 = (bf16[192,128]{1,0:T(8,128)(2,1)S(1)}, bf16[192,128]{1,0:T(8,128)(2,1)S(1)}, u32[]{:S(2)}, u32[]{:S(2)}) collective-permute-start(bf16[192,128]{1,0:T(8,128)(2,1)S(1)} %get-tuple-element.22), channel_id=1, source_target_pairs={{1,2},{2,1},{3,4},{4,3},{5,6},{6,5},{7,8},{8,7},{9,10},{10,9},{11,... | collective-permute-start | bytes 147464 | tf_op jit(solution)/shard_map/ppermute | solution.py:460
  5.0 6.6 %collective-permute-start.2 = (bf16[192,128]{1,0:T(8,128)(2,1)S(1)}, bf16[192,128]{1,0:T(8,128)(2,1)S(1)}, u32[]{:S(2)}, u32[]{:S(2)}) collective-permute-start(bf16[192,128]{1,0:T(8,128)(2,1)S(1)} %get-tuple-element.23), channel_id=1, source_target_pairs={{0,1},{1,0},{2,3},{3,2},{4,5},{5,4},{6,7},{7,6},{8,9},{9,8},{10,11... | collective-permute-start | bytes 147464 | tf_op jit(solution)/shard_map/ppermute | solution.py:461
  11.5 0.6 collective-permute-start
  12.2 0.0 collective-permute-done.far_ref
  12.2 0.0 collective-permute-done.1.away_ref
  12.2 0.2 collective-permute-done.2.near_ref
  12.4 0.0 copy-start.1
  12.4 0.9 copy-done.1
  13.4 7.9 %smooth.1 = (bf16[18,64,192]{2,1,0:T(8,128)(2,1)S(1)}, bf16[8,1152]{1,0:T(8,128)(2,1)S(1)}, bf16[576,128]{1,0:T(8,128)(2,1)S(1)}, bf16[576,128]{1,0:T(8,128)(2,1)S(1)}) custom-call(s32[1]{0:T(128)} %bitcast.me_ref, f32[8,256]{1,0:T(8,128)S(1)} %get-tuple-element.19.order_l_ref, f32[192,128]{1,0:T(8,128)S(1)} %get-tuple-element.20.order_s_ref, ...), custom_call_target="tpu_custom_call" | custom-call | flops 1000000000 | bytes 5832708 | tf_op jit(solution)/shard_map/smooth/pallas_call | solution.py:418
  21.3 0.1 collective-permute-start.4
  21.4 9.1 %collective-permute-start.5 = (bf16[576,128]{1,0:T(8,128)(2,1)S(1)}, bf16[576,128]{1,0:T(8,128)(2,1)S(1)}, u32[]{:S(2)}, u32[]{:S(2)}) collective-permute-start(bf16[576,128]{1,0:T(8,128)(2,1)S(1)} %get-tuple-element.27), channel_id=1, source_target_pairs={{0,1},{1,0},{2,3},{3,2},{4,5},{5,4},{6,7},{7,6},{8,9},{9,8},{10,11... | collective-permute-start | bytes 442376 | tf_op jit(solution)/shard_map/ppermute | solution.py:461
  30.5 0.7 collective-permute-start.3
  31.1 1.8 %pack.1 = bf16[64,56,128]{2,1,0:T(8,128)(2,1)} custom-call(f32[8,256]{1,0:T(8,128)S(1)} %get-tuple-element.19.order_l_ref, bf16[1152,192]{1,0:T(8,128)(2,1)S(1)} %bitcast.15), custom_call_target="tpu_custom_call" | custom-call | bytes 1368064 | tf_op jit(solution)/shard_map/pack/pallas_call | solution.py:418
  32.9 0.0 collective-permute-done.3.far_ref
  32.9 0.0 collective-permute-done.4.away_ref
  32.9 0.0 collective-permute-done.5.near_ref
  32.9 12.9 %all-to-all-start = ((bf16[64,56,128]{2,1,0:T(8,128)(2,1)}), bf16[64,56,128]{2,1,0:T(8,128)(2,1)S(1)}, u32[]{:S(2)}, u32[]{:S(2)}) async-start(bf16[64,56,128]{2,1,0:T(8,128)(2,1)} %pack.1), calls=%async_computation | async-start | bytes 1835008 | tf_op jit(solution)/shard_map/all_to_all | solution.py:493
  45.8 22.1 %product.1 = (f32[512,256]{1,0:T(8,128)}, f32[8,256]{1,0:T(8,128)S(1)}) custom-call(s32[1]{0:T(128)} %bitcast.me_ref, f32[8,256]{1,0:T(8,128)S(1)} %get-tuple-element.19.order_l_ref, f32[192,128]{1,0:T(8,128)S(1)} %get-tuple-element.20.order_s_ref, bf16[3,64,64,192]{3,2,1,0:T(8,128)(2,1)} %bitcast.19, bf16[1152,192]{1,0:T(8,128)(2,1)S(1)} %bitcast.16, ...), custom_call_target="tpu_custom_call" | custom-call | flops 10000000000 | bytes 6113284 | tf_op jit(solution)/shard_map/product/pallas_call | solution.py:418
  68.0 3.1 %all-to-all-done.recv_ref = bf16[64,56,128]{2,1,0:T(8,128)(2,1)S(1)} async-done(((bf16[64,56,128]{2,1,0:T(8,128)(2,1)}), bf16[64,56,128]{2,1,0:T(8,128)(2,1)S(1)}, u32[]{:S(2)}, u32[]{:S(2)}) %all-to-all-start) | async-done | bytes 917536 | tf_op jit(solution)/shard_map/all_to_all | solution.py:493
  71.1 7.2 %all-to-all-start.1 = ((f32[64,8,256]{2,1,0:T(8,128)}), f32[64,8,256]{2,1,0:T(8,128)S(1)}, u32[]{:S(2)}, u32[]{:S(2)}) async-start(f32[64,8,256]{2,1,0:T(8,128)} %bitcast.9), calls=%async_computation.1 | async-start | bytes 1048576 | tf_op jit(solution)/shard_map/all_to_all | solution.py:513
  78.3 0.7 collective-permute-start.6
  79.0 1.9 %unpack_smooth.1 = (bf16[1152,192]{1,0:T(8,128)(2,1)}, bf16[192,512]{1,0:T(8,128)(2,1)S(1)}) custom-call(bf16[64,56,128]{2,1,0:T(8,128)(2,1)S(1)} %all-to-all-done.recv_ref), custom_call_target="tpu_custom_call" | custom-call | flops 1000000000 | bytes 1556480 | tf_op jit(solution)/shard_map/unpack_smooth/pallas_call | solution.py:418
  80.9 0.0 collective-permute-done.6.far_ref
  80.9 15.2 %all-to-all-done.1 = f32[64,8,256]{2,1,0:T(8,128)S(1)} async-done(((f32[64,8,256]{2,1,0:T(8,128)}), f32[64,8,256]{2,1,0:T(8,128)S(1)}, u32[]{:S(2)}, u32[]{:S(2)}) %all-to-all-start.1) | async-done | bytes 524320 | tf_op jit(solution)/shard_map/all_to_all | solution.py:513
  96.0 1.0 %unpack_coarse.1 = f32[192,252]{1,0:T(8,128)} custom-call(s32[1]{0:T(128)} %bitcast.me_ref, bf16[192,512]{1,0:T(8,128)(2,1)S(1)} %get-tuple-element.30.pick_ref, f32[512,256]{1,0:T(8,128)S(1)} %bitcast.12, f32[8,256]{1,0:T(8,128)S(1)} %collective-permute-done.6.far_ref), custom_call_target="tpu_custom_call" | custom-call | bytes 922628 | tf_op jit(solution)/shard_map/unpack_coarse/pallas_call | solution.py:418
Async XLA Ops:
  0.6 0.9 copy-start
  1.6 0.7 copy-start.2
  3.0 9.2 %collective-permute-start.1 = (bf16[192,128]{1,0:T(8,128)(2,1)S(1)}, bf16[192,128]{1,0:T(8,128)(2,1)S(1)}, u32[]{:S(2)}, u32[]{:S(2)}) collective-permute-start(bf16[192,128]{1,0:T(8,128)(2,1)S(1)} %get-tuple-element.22), channel_id=1, source_target_pairs={{1,2},{2,1},{3,4},{4,3},{5,6},{6,5},{7,8},{8,7},{9,10},{10,9},{11,... | collective-permute-start | bytes 147464 | tf_op jit(solution)/shard_map/ppermute | solution.py:460
  5.0 7.4 %collective-permute-start.2 = (bf16[192,128]{1,0:T(8,128)(2,1)S(1)}, bf16[192,128]{1,0:T(8,128)(2,1)S(1)}, u32[]{:S(2)}, u32[]{:S(2)}) collective-permute-start(bf16[192,128]{1,0:T(8,128)(2,1)S(1)} %get-tuple-element.23), channel_id=1, source_target_pairs={{0,1},{1,0},{2,3},{3,2},{4,5},{5,4},{6,7},{7,6},{8,9},{9,8},{10,11... | collective-permute-start | bytes 147464 | tf_op jit(solution)/shard_map/ppermute | solution.py:461
  11.5 0.7 collective-permute-start
  12.4 0.9 copy-start.1
  21.3 11.7 %collective-permute-start.4 = (bf16[576,128]{1,0:T(8,128)(2,1)S(1)}, bf16[576,128]{1,0:T(8,128)(2,1)S(1)}, u32[]{:S(2)}, u32[]{:S(2)}) collective-permute-start(bf16[576,128]{1,0:T(8,128)(2,1)S(1)} %get-tuple-element.26), channel_id=1, source_target_pairs={{1,2},{2,1},{3,4},{4,3},{5,6},{6,5},{7,8},{8,7},{9,10},{10,9},{11,... | collective-permute-start | bytes 442376 | tf_op jit(solution)/shard_map/ppermute | solution.py:460
  21.4 11.6 %collective-permute-start.5 = (bf16[576,128]{1,0:T(8,128)(2,1)S(1)}, bf16[576,128]{1,0:T(8,128)(2,1)S(1)}, u32[]{:S(2)}, u32[]{:S(2)}) collective-permute-start(bf16[576,128]{1,0:T(8,128)(2,1)S(1)} %get-tuple-element.27), channel_id=1, source_target_pairs={{0,1},{1,0},{2,3},{3,2},{4,5},{5,4},{6,7},{7,6},{8,9},{9,8},{10,11... | collective-permute-start | bytes 442376 | tf_op jit(solution)/shard_map/ppermute | solution.py:461
  30.5 2.4 %collective-permute-start.3 = (bf16[8,1152]{1,0:T(8,128)(2,1)S(1)}, bf16[8,1152]{1,0:T(8,128)(2,1)S(1)}, u32[]{:S(2)}, u32[]{:S(2)}) collective-permute-start(bf16[8,1152]{1,0:T(8,128)(2,1)S(1)} %get-tuple-element.25), channel_id=1, source_target_pairs={{63,64},{64,63},{127,128},{128,127},{191,192},{192,191}} | collective-permute-start | bytes 55304 | tf_op jit(solution)/shard_map/ppermute | solution.py:459
  32.9 38.2 %all-to-all-start = ((bf16[64,56,128]{2,1,0:T(8,128)(2,1)}), bf16[64,56,128]{2,1,0:T(8,128)(2,1)S(1)}, u32[]{:S(2)}, u32[]{:S(2)}) async-start(bf16[64,56,128]{2,1,0:T(8,128)(2,1)} %pack.1), calls=%async_computation | async-start | bytes 1835008 | tf_op jit(solution)/shard_map/all_to_all | solution.py:493
  71.1 24.9 %all-to-all-start.1 = ((f32[64,8,256]{2,1,0:T(8,128)}), f32[64,8,256]{2,1,0:T(8,128)S(1)}, u32[]{:S(2)}, u32[]{:S(2)}) async-start(f32[64,8,256]{2,1,0:T(8,128)} %bitcast.9), calls=%async_computation.1 | async-start | bytes 1048576 | tf_op jit(solution)/shard_map/all_to_all | solution.py:513
  78.3 2.6 %collective-permute-start.6 = (f32[8,256]{1,0:T(8,128)S(1)}, f32[8,256]{1,0:T(8,128)S(1)}, u32[]{:S(2)}, u32[]{:S(2)}) collective-permute-start(f32[8,256]{1,0:T(8,128)S(1)} %get-tuple-element.35), channel_id=1, source_target_pairs={{63,64},{64,63},{127,128},{128,127},{191,192},{192,191}} | collective-permute-start | bytes 24584 | tf_op jit(solution)/shard_map/ppermute | solution.py:512

commit v3 on v2

--- a/solution.py
+++ b/solution.py
@@ -109,32 +109,29 @@
     return [far] + rims[::-1]
 
 
-def neighbours(rows, near, away, far, r, me):
+def local_rows(rows, r):
     lane = iota((ROWS, WIDE), 1)
     row_l = jnp.where(lane < ROWS, lane, lane - TILE)
     same = r.owner_l == r.owner_s
     before = ones_where(same & (r.rank_s + 1.0 == r.rank_l))
     after = ones_where(same & (r.rank_s == r.rank_l + 1.0))
     here = ones_where(iota((ROWS, WIDE), 0) == row_l)
+    return [dot(rows, pick) for pick in (before, here, after)]
+
+
+def rim_rows(near, away, far, r, me):
     bucket = iota((128, WIDE), 0)
     even = me % 2 == 0
-    from_left = jnp.where(even, away, near)
-    from_right = jnp.where(even, near, away)
-    head, tail = far_pick(r, me, WIDE)
     result = []
-    for local, rim, edge, end in (
-        (before, from_left, r.rank_l, head), (here, None, None, None), (after, from_right, r.after_l, tail)
+    for rim, edge, end in zip(
+        (jnp.where(even, away, near), jnp.where(even, near, away)), (r.rank_l, r.after_l), far_pick(r, me, WIDE)
     ):
-        own = dot(rows, local)
-        if rim is not None:
-            ends = []
-            for side in (0, 1):
-                want = bucket - TILE * side
-                want = jnp.where((want >= 0) & (want < TILE), want, -1).astype(F32)
-                ends.append(dot(rim, ones_where((want == r.owner_l) & (edge == 0.0))))
-            own = own + jnp.concatenate(ends, 0)
-            own = own + lax.dot_general(far, end, TN, preferred_element_type=F32)
-        result.append(own)
+        ends = []
+        for side in (0, 1):
+            want = bucket - TILE * side
+            want = jnp.where((want >= 0) & (want < TILE), want, -1).astype(F32)
+            ends.append(dot(rim, ones_where((want == r.owner_l) & (edge == 0.0))))
+        result.append(jnp.concatenate(ends, 0) + lax.dot_general(far, end, TN, preferred_element_type=F32))
     return result
 
 
@@ -144,17 +141,24 @@
         ref[tile, k] = part.reshape(-1, TILE, 128)
 
 
-def chunk_copy(a_hbm, a_ref, sems, n):
-    return pltpu.make_async_copy(a_hbm.at[:, pl.ds(16 * n, 16)], a_ref.at[:, pl.ds(16 * n, 16)], sems.at[n])
-
-
-def start_copies(a_hbm, a_ref, sems):
+def chunk_copies(a_hbm, a_ref, sems, planes, n):
+    rows = pl.ds(16 * n, 16)
+    return [
+        pltpu.make_async_copy(a_hbm.at[k, rows], a_ref.at[at, rows], sems.at[at, n])
+        for at, k in enumerate(planes)
+    ]
+
+
+def start_copies(a_hbm, a_ref, sems, planes):
     for n in range(TILE // 16):
-        chunk_copy(a_hbm, a_ref, sems, n).start()
-
-
-def set_groups(a_ref, ib, group_ref):
-    for k in range(3):
+        for copy in chunk_copies(a_hbm, a_ref, sems, planes, n):
+            copy.start()
+
+
+def next_groups(a_hbm, a_ref, sems, planes, ib, group_ref):
+    for copy in chunk_copies(a_hbm, a_ref, sems, planes, ib):
+        copy.wait()
+    for k in range(len(planes)):
         for i in range(8):
             low, high = (a_ref[k, 16 * ib + i + n].astype(F32) for n in (0, 8))
             group_ref[0, k, i] = low[:, :128]
@@ -194,8 +198,9 @@
     return jnp.concatenate([top, bottom], 0)
 
 
-def first_kernel(me_ref, owner_ref, p_ref, wide_ref, tall_ref, far_out, away_out, near_out):
+def first_kernel(me_ref, owner_ref, p_ref, wide_ref, tall_ref, p_out, far_out, away_out, near_out):
     rows, columns = rank_arrays(owner_ref[...])
+    p_out[...] = p_ref[...]
     wide_ref[...] = jnp.zeros_like(wide_ref)
     for n in range(3):
         wide_ref[n : n + 1, :] = rows[n]
@@ -206,8 +211,53 @@
         ref[...] = rim
 
 
+def halves(ib):
+    return pl.ds(pl.multiple_of(16 * ib, 8), 8), pl.ds(pl.multiple_of(16 * ib + 8, 8), 8)
+
+
+def middle_kernel(
+    order_l_ref, order_s_ref, a_hbm, p_ref, mid_ref, scale_ref, local_ref,
+    a_ref, sems, group_ref, wide_ref, out_ref,
+):
+    ib = pl.program_id(0)
+
+    @pl.when(ib == 0)
+    def _():
+        start_copies(a_hbm, a_ref, sems, (1,))
+        before, here, after = local_rows(p_ref[...], Order(order_l_ref, order_s_ref))
+        set_wide(wide_ref, 0, here)
+        set_wide(local_ref, 0, before)
+        set_wide(local_ref, 1, after)
+
+    next_groups(a_hbm, a_ref, sems, (1,), ib, group_ref)
+    sub, lane = iota((8, 128), 0), iota((8, 128), 1)
+    lower, upper = halves(ib)
+
+    def one_group(g, carry):
+        tile = jnp.where(g == 2, 1, 0)
+        second = (g == 1) | ((g == 2) & (lane >= TILE))
+        diag = jnp.zeros((8, 128), F32)
+        for i in range(8):
+            entry = jnp.where(second, group_ref[g, 0, i, upper, :], group_ref[g, 0, i, lower, :])
+            diag = jnp.where(sub == i, entry, diag)
+        scale = 0.6 * (1.0 / diag)
+        scale_ref[ib, g] = scale
+        for half in (0, 1):
+            columns = [3 * half + c for c in range(3)]
+            sums = contracted(group_ref, wide_ref, g, tile, [(0, 0)], columns)
+            for c, total in zip(columns, sums):
+                own = jnp.where(second, wide_ref[tile, 0, c, upper, :], wide_ref[tile, 0, c, lower, :])
+                out_ref[g, c] = own - scale * total
+        return carry
+
+    lax.fori_loop(0, 3, one_group, 0)
+    rows = pl.ds(pl.multiple_of(16 * ib, 16), 16)
+    for index in range(6):
+        mid_ref[index, rows, :] = ungrouped(out_ref, index).astype(BF16)
+
+
 def smooth_kernel(
-    me_ref, order_l_ref, order_s_ref, a_hbm, p_ref, far_ref, away_ref, near_ref,
+    me_ref, order_l_ref, order_s_ref, a_hbm, mid_ref, scale_ref, local_ref, far_ref, away_ref, near_ref,
     s_ref, far_out, away_out, near_out, a_ref, sems, group_ref, wide_ref, out_ref,
 ):
     ib = pl.program_id(0)
@@ -215,43 +265,30 @@
 
     @pl.when(ib == 0)
     def _():
-        start_copies(a_hbm, a_ref, sems)
+        start_copies(a_hbm, a_ref, sems, (0, 2))
         r = Order(order_l_ref, order_s_ref)
-        near = neighbours(p_ref[...], near_ref[...], away_ref[...], far_ref[...], r, me)
-        for k, value in enumerate(near):
+        for k, value in enumerate(rim_rows(near_ref[...], away_ref[...], far_ref[...], r, me)):
             set_wide(wide_ref, k, value)
-
-    chunk_copy(a_hbm, a_ref, sems, ib).wait()
-    set_groups(a_ref, ib, group_ref)
-    sub, lane = iota((8, 128), 0), iota((8, 128), 1)
+        wide_ref[...] += local_ref[...]
+        s_ref[6:12] = mid_ref[...]
+
+    next_groups(a_hbm, a_ref, sems, (0, 2), ib, group_ref)
 
     def one_group(g, carry):
         tile = jnp.where(g == 2, 1, 0)
-        second = (g == 1) | ((g == 2) & (lane >= TILE))
-        lower, upper = pl.ds(pl.multiple_of(16 * ib, 8), 8), pl.ds(pl.multiple_of(16 * ib + 8, 8), 8)
-        diag = jnp.zeros((8, 128), F32)
-        for i in range(8):
-            entry = jnp.where(second, group_ref[g, 1, i, upper, :], group_ref[g, 1, i, lower, :])
-            diag = jnp.where(sub == i, entry, diag)
-        scale = 0.6 * (1.0 / diag)
-        for k in range(3):
+        scale = 0.0 - scale_ref[ib, g]
+        for k in range(2):
             for half in (0, 1):
                 columns = [3 * half + c for c in range(3)]
                 sums = contracted(group_ref, wide_ref, g, tile, [(k, 0)], columns)
                 for c, total in zip(columns, sums):
-                    value = scale * total
-                    if k == 1:
-                        own = jnp.where(second, wide_ref[tile, 1, c, upper, :], wide_ref[tile, 1, c, lower, :])
-                        value = own - value
-                    else:
-                        value = 0.0 - value
-                    out_ref[g, 6 * k + c] = value
+                    out_ref[g, 6 * k + c] = scale * total
         return carry
 
     lax.fori_loop(0, 3, one_group, 0)
     rows = pl.ds(pl.multiple_of(16 * ib, 16), 16)
-    for index in range(18):
-        s_ref[index, rows, :] = ungrouped(out_ref, index).astype(BF16)
+    for index in range(12):
+        s_ref[index if index < 6 else index + 6, rows, :] = ungrouped(out_ref, index).astype(BF16)
 
     @pl.when(ib == pl.num_programs(0) - 1)
     def _():
@@ -293,15 +330,15 @@
 
     @pl.when(ib == 0)
     def _():
-        start_copies(a_hbm, a_ref, sems)
+        start_copies(a_hbm, a_ref, sems, (0, 1, 2))
         r = Order(order_l_ref, order_s_ref)
-        near = neighbours(s_ref[...], near_ref[...], away_ref[...], far_ref[...], r, me)
-        for k, value in enumerate(near):
+        before, here, after = local_rows(s_ref[...], r)
+        left, right = rim_rows(near_ref[...], away_ref[...], far_ref[...], r, me)
+        for k, value in enumerate((before + left, here, after + right)):
             set_wide(wide_ref, k, value)
         term_ref[...] = jnp.zeros_like(term_ref)
 
-    chunk_copy(a_hbm, a_ref, sems, ib).wait()
-    set_groups(a_ref, ib, group_ref)
+    next_groups(a_hbm, a_ref, sems, (0, 1, 2), ib, group_ref)
     lane = iota((8, 128), 1)
 
     def one_group(step, carry):
@@ -449,11 +486,13 @@
     p = p_tent.transpose(1, 2, 0).reshape(MODES * TILE, ROWS)
     a_spec = pl.BlockSpec(memory_space=pltpu.HBM)
     grid = (TILE // 16,)
-    a_scratch = [
-        pltpu.VMEM((3, TILE, TILE, ROWS), BF16),
-        pltpu.SemaphoreType.DMA((TILE // 16,)),
-        pltpu.VMEM((3, 3, 8, TILE, 128), F32),
-    ]
+
+    def a_scratch(planes):
+        return [
+            pltpu.VMEM((planes, TILE, TILE, ROWS), BF16),
+            pltpu.SemaphoreType.DMA((planes, TILE // 16)),
+            pltpu.VMEM((3, planes, 8, TILE, 128), F32),
+        ]
 
     def exchanged(far, away, near):
         far = lax.ppermute(far, axes, across)
@@ -463,25 +502,36 @@
     def rims(length):
         return [shaped((8, length)), shaped((length // 2, 128)), shaped((length // 2, 128))]
 
-    order_l, order_s, *sent = call(
+    order_l, order_s, p, *sent = call(
         first_kernel,
-        [shaped((8, WIDE), F32), shaped((ROWS, 128), F32)] + rims(MODES * TILE),
+        [shaped((8, WIDE), F32), shaped((ROWS, 128), F32), shaped(p.shape)] + rims(MODES * TILE),
         (me, new_owner.reshape(1, ROWS), p),
         name="rims",
     )
     got = exchanged(*sent)
-
+    local = shaped((2, 2, MODES, TILE, 128), F32)
+    parts = call(
+        middle_kernel,
+        [shaped((MODES, TILE, ROWS)), shaped((TILE // 16, 3, 8, 128), F32), local],
+        (order_l, order_s, a, p),
+        grid=grid,
+        in_specs={2: a_spec},
+        scratch=[
+            *a_scratch(1),
+            pltpu.VMEM((2, 1, MODES, TILE, 128), F32),
+            pltpu.VMEM((3, MODES, 8, 128), F32),
+        ],
+        flops=10**9,
+        mib=50,
+        name="middle",
+    )
     s, *sent = call(
         smooth_kernel,
         [shaped((18, TILE, ROWS))] + rims(COLS),
-        (me, order_l, order_s, a, p, *got),
+        (me, order_l, order_s, a, *parts, *got),
         grid=grid,
         in_specs={3: a_spec},
-        scratch=[
-            *a_scratch,
-            pltpu.VMEM((2, 3, MODES, TILE, 128), F32),
-            pltpu.VMEM((3, 18, 8, 128), F32),
-        ],
+        scratch=[*a_scratch(2), pltpu.VMEM(local.shape, F32), pltpu.VMEM((3, 12, 8, 128), F32)],
         flops=10**9,
         mib=50,
         name="smooth",
@@ -499,7 +549,7 @@
         grid=grid,
         in_specs={3: a_spec},
         scratch=[
-            *a_scratch,
+            *a_scratch(3),
             pltpu.VMEM((2, 3, 18, TILE, 128), F32),
             pltpu.VMEM((3, TILE // 16, 30, 8, 128), F32),
             pltpu.VMEM((3, TILE // 16, 18, 8, 128), F32),

time: 97.4 us -> 94.1 us (0.966)
  starting transfers between devices: 39.8 us -> 35.9 us
  Pallas kernels: 35.5 us -> 37.1 us
    ppermute x2, starting transfers between devices: 15.7 us -> 12.8 us  [exchanged(): return (far, away, lax.ppermute(near, axes, near_pairs))]
    pallas_call x6 -> x7, Pallas kernels: 35.5 us -> 37.1 us  [call(): pl.pallas_call(kernel, grid=(1,) if grid is None else grid, in_specs=spec...]
    all_to_all x1, starting transfers between devices: 12.9 us -> 11.9 us  [per_device(): lax.all_to_all(packed, 'member', split_axis=0, concat_axis=0, tiled=True)]
    unnamed x6 -> x4, local copies, waits for them, and re-layouts: 2.53 us -> 1.6 us
  transfers between devices with their start and end apart: 9 -> 9, of which waited for: 3 -> 2; matrix products, arithmetic and copies ran while one was open for 0% -> 0% of each run, Pallas kernels for 27% -> 31%
where the time goes in v3:
time: 94.1 us; the launch traced here: 93.7 us
  Pallas kernels  37.1 us (39%)
  starting transfers between devices  35.9 us (38%)
  waiting for transfers between devices  18.3 us (19%)
  local copies, waits for them, and re-layouts  1.6 us (2%)
    pallas_call x7, Pallas kernels, call(): pl.pallas_call(kernel, grid=(1,) if grid is None else grid, in_specs=spec...  37.1 us
    all_to_all x1, waiting for transfers between devices, per_device(): lax.all_to_all(sums.reshape(MEMBERS, SLOTS, WIDE), 'member', split_axis=0...  15.2 us
    ppermute x2, starting transfers between devices, exchanged(): return (far, away, lax.ppermute(near, axes, near_pairs))  12.8 us
    all_to_all x1, starting transfers between devices, per_device(): lax.all_to_all(packed, 'member', split_axis=0, concat_axis=0, tiled=True)  11.9 us
    all_to_all x1, starting transfers between devices, per_device(): lax.all_to_all(sums.reshape(MEMBERS, SLOTS, WIDE), 'member', split_axis=0...  7.16 us
    all_to_all x1, waiting for transfers between devices, per_device(): lax.all_to_all(packed, 'member', split_axis=0, concat_axis=0, tiled=True)  3.15 us
    ppermute x2, starting transfers between devices, exchanged(): away = lax.ppermute(away, axes, away_pairs)  2.04 us
  transfers between devices with their start and end apart: 9, of which 2 were waited for; matrix products, arithmetic and copies ran while one was open for 0% of the time, Pallas kernels for 31%

profile of v3, /device:TPU:3, one launch (start us, length us, event | category | flops | bytes accessed | tf_op | source)
XLA Modules:
  0.0 93.7 jit_solution(5193656758231753212)
XLA Ops:
  0.6 0.0 copy-start
  0.6 0.9 copy-done
  1.6 0.0 copy-start.1
  1.6 0.7 copy-done.1
  2.2 0.8 rims.1
  3.0 0.7 collective-permute-start
  3.7 1.9 %collective-permute-start.1 = (bf16[192,128]{1,0:T(8,128)(2,1)S(1)}, bf16[192,128]{1,0:T(8,128)(2,1)S(1)}, u32[]{:S(2)}, u32[]{:S(2)}) collective-permute-start(bf16[192,128]{1,0:T(8,128)(2,1)S(1)} %get-tuple-element.30), channel_id=1, source_target_pairs={{1,2},{2,1},{3,4},{4,3},{5,6},{6,5},{7,8},{8,7},{9,10},{10,9},{11,... | collective-permute-start | bytes 147464 | tf_op jit(solution)/shard_map/ppermute | solution.py:499
  5.6 7.9 %collective-permute-start.2 = (bf16[192,128]{1,0:T(8,128)(2,1)S(1)}, bf16[192,128]{1,0:T(8,128)(2,1)S(1)}, u32[]{:S(2)}, u32[]{:S(2)}) collective-permute-start(bf16[192,128]{1,0:T(8,128)(2,1)S(1)} %get-tuple-element.31), channel_id=1, source_target_pairs={{0,1},{1,0},{2,3},{3,2},{4,5},{5,4},{6,7},{7,6},{8,9},{9,8},{10,11... | collective-permute-start | bytes 147464 | tf_op jit(solution)/shard_map/ppermute | solution.py:500
  13.5 3.5 %middle.1 = (bf16[6,64,192]{2,1,0:T(8,128)(2,1)S(1)}, f32[4,3,8,128]{3,2,1,0:T(8,128)S(1)}, f32[2,2,6,64,128]{4,3,2,1,0:T(8,128)S(1)}) custom-call(f32[8,256]{1,0:T(8,128)S(1)} %get-tuple-element.23.order_l_ref, f32[192,128]{1,0:T(8,128)S(1)} %get-tuple-element.24.order_s_ref, bf16[3,64,64,192]{3,2,1,0:T(8,128)(2,1)} %bitcast.17, ...), custom_call_target="tpu_custom_call" | custom-call | flops 1000000000 | bytes 5955584 | tf_op jit(solution)/shard_map/middle/pallas_call | solution.py:455
  17.1 0.0 collective-permute-done.far_ref
  17.1 0.0 collective-permute-done.1.away_ref
  17.1 0.0 collective-permute-done.2.near_ref
  17.1 6.0 %smooth.1 = (bf16[18,64,192]{2,1,0:T(8,128)(2,1)S(1)}, bf16[8,1152]{1,0:T(8,128)(2,1)S(1)}, bf16[576,128]{1,0:T(8,128)(2,1)S(1)}, bf16[576,128]{1,0:T(8,128)(2,1)S(1)}) custom-call(s32[1]{0:T(128)} %bitcast.me_ref, f32[8,256]{1,0:T(8,128)S(1)} %get-tuple-element.23.order_l_ref, f32[192,128]{1,0:T(8,128)S(1)} %get-tuple-element.24.order_s_ref, ...), custom_call_target="tpu_custom_call" | custom-call | flops 1000000000 | bytes 6668292 | tf_op jit(solution)/shard_map/smooth/pallas_call | solution.py:455
  23.1 0.1 collective-permute-start.4
  23.2 5.0 %collective-permute-start.5 = (bf16[576,128]{1,0:T(8,128)(2,1)S(1)}, bf16[576,128]{1,0:T(8,128)(2,1)S(1)}, u32[]{:S(2)}, u32[]{:S(2)}) collective-permute-start(bf16[576,128]{1,0:T(8,128)(2,1)S(1)} %get-tuple-element.35), channel_id=1, source_target_pairs={{0,1},{1,0},{2,3},{3,2},{4,5},{5,4},{6,7},{7,6},{8,9},{9,8},{10,11... | collective-permute-start | bytes 442376 | tf_op jit(solution)/shard_map/ppermute | solution.py:500
  28.1 0.7 collective-permute-start.3
  28.8 1.8 %pack.1 = bf16[64,56,128]{2,1,0:T(8,128)(2,1)} custom-call(f32[8,256]{1,0:T(8,128)S(1)} %get-tuple-element.23.order_l_ref, bf16[1152,192]{1,0:T(8,128)(2,1)S(1)} %bitcast.13), custom_call_target="tpu_custom_call" | custom-call | bytes 1368064 | tf_op jit(solution)/shard_map/pack/pallas_call | solution.py:455
  30.6 0.0 collective-permute-done.3.far_ref
  30.6 0.0 collective-permute-done.4.away_ref
  30.6 0.0 collective-permute-done.5.near_ref
  30.6 11.9 %all-to-all-start = ((bf16[64,56,128]{2,1,0:T(8,128)(2,1)}), bf16[64,56,128]{2,1,0:T(8,128)(2,1)S(1)}, u32[]{:S(2)}, u32[]{:S(2)}) async-start(bf16[64,56,128]{2,1,0:T(8,128)(2,1)} %pack.1), calls=%async_computation | async-start | bytes 1835008 | tf_op jit(solution)/shard_map/all_to_all | solution.py:543
  42.5 22.1 %product.1 = (f32[512,256]{1,0:T(8,128)}, f32[8,256]{1,0:T(8,128)S(1)}) custom-call(s32[1]{0:T(128)} %bitcast.me_ref, f32[8,256]{1,0:T(8,128)S(1)} %get-tuple-element.23.order_l_ref, f32[192,128]{1,0:T(8,128)S(1)} %get-tuple-element.24.order_s_ref, bf16[3,64,64,192]{3,2,1,0:T(8,128)(2,1)} %bitcast.19, bf16[1152,192]{1,0:T(8,128)(2,1)S(1)} %bitcast.14, ...), custom_call_target="tpu_custom_call" | custom-call | flops 10000000000 | bytes 6113284 | tf_op jit(solution)/shard_map/product/pallas_call | solution.py:455
  64.6 3.2 %all-to-all-done.recv_ref = bf16[64,56,128]{2,1,0:T(8,128)(2,1)S(1)} async-done(((bf16[64,56,128]{2,1,0:T(8,128)(2,1)}), bf16[64,56,128]{2,1,0:T(8,128)(2,1)S(1)}, u32[]{:S(2)}, u32[]{:S(2)}) %all-to-all-start) | async-done | bytes 917536 | tf_op jit(solution)/shard_map/all_to_all | solution.py:543
  67.8 7.2 %all-to-all-start.1 = ((f32[64,8,256]{2,1,0:T(8,128)}), f32[64,8,256]{2,1,0:T(8,128)S(1)}, u32[]{:S(2)}, u32[]{:S(2)}) async-start(f32[64,8,256]{2,1,0:T(8,128)} %bitcast.8), calls=%async_computation.1 | async-start | bytes 1048576 | tf_op jit(solution)/shard_map/all_to_all | solution.py:563
  75.0 0.7 collective-permute-start.6
  75.6 1.9 %unpack_smooth.1 = (bf16[1152,192]{1,0:T(8,128)(2,1)}, bf16[192,512]{1,0:T(8,128)(2,1)S(1)}) custom-call(bf16[64,56,128]{2,1,0:T(8,128)(2,1)S(1)} %all-to-all-done.recv_ref), custom_call_target="tpu_custom_call" | custom-call | flops 1000000000 | bytes 1556480 | tf_op jit(solution)/shard_map/unpack_smooth/pallas_call | solution.py:455
  77.5 0.0 collective-permute-done.6.far_ref
  77.5 15.2 %all-to-all-done.1 = f32[64,8,256]{2,1,0:T(8,128)S(1)} async-done(((f32[64,8,256]{2,1,0:T(8,128)}), f32[64,8,256]{2,1,0:T(8,128)S(1)}, u32[]{:S(2)}, u32[]{:S(2)}) %all-to-all-start.1) | async-done | bytes 524320 | tf_op jit(solution)/shard_map/all_to_all | solution.py:563
  92.7 1.0 %unpack_coarse.1 = f32[192,252]{1,0:T(8,128)} custom-call(s32[1]{0:T(128)} %bitcast.me_ref, bf16[192,512]{1,0:T(8,128)(2,1)S(1)} %get-tuple-element.38.pick_ref, f32[512,256]{1,0:T(8,128)S(1)} %bitcast.12, f32[8,256]{1,0:T(8,128)S(1)} %collective-permute-done.6.far_ref), custom_call_target="tpu_custom_call" | custom-call | bytes 922628 | tf_op jit(solution)/shard_map/unpack_coarse/pallas_call | solution.py:455
Async XLA Ops:
  0.6 0.9 copy-start
  1.6 0.7 copy-start.1
  3.0 14.0 %collective-permute-start = (bf16[8,384]{1,0:T(8,128)(2,1)S(1)}, bf16[8,384]{1,0:T(8,128)(2,1)S(1)}, u32[]{:S(2)}, u32[]{:S(2)}) collective-permute-start(bf16[8,384]{1,0:T(8,128)(2,1)S(1)} %get-tuple-element.29), channel_id=1, source_target_pairs={{63,64},{64,63},{127,128},{128,127},{191,192},{192,191}} | collective-permute-start | bytes 18440 | tf_op jit(solution)/shard_map/ppermute | solution.py:498
  3.7 13.4 %collective-permute-start.1 = (bf16[192,128]{1,0:T(8,128)(2,1)S(1)}, bf16[192,128]{1,0:T(8,128)(2,1)S(1)}, u32[]{:S(2)}, u32[]{:S(2)}) collective-permute-start(bf16[192,128]{1,0:T(8,128)(2,1)S(1)} %get-tuple-element.30), channel_id=1, source_target_pairs={{1,2},{2,1},{3,4},{4,3},{5,6},{6,5},{7,8},{8,7},{9,10},{10,9},{11,... | collective-permute-start | bytes 147464 | tf_op jit(solution)/shard_map/ppermute | solution.py:499
  5.6 11.5 %collective-permute-start.2 = (bf16[192,128]{1,0:T(8,128)(2,1)S(1)}, bf16[192,128]{1,0:T(8,128)(2,1)S(1)}, u32[]{:S(2)}, u32[]{:S(2)}) collective-permute-start(bf16[192,128]{1,0:T(8,128)(2,1)S(1)} %get-tuple-element.31), channel_id=1, source_target_pairs={{0,1},{1,0},{2,3},{3,2},{4,5},{5,4},{6,7},{7,6},{8,9},{9,8},{10,11... | collective-permute-start | bytes 147464 | tf_op jit(solution)/shard_map/ppermute | solution.py:500
  23.1 7.5 %collective-permute-start.4 = (bf16[576,128]{1,0:T(8,128)(2,1)S(1)}, bf16[576,128]{1,0:T(8,128)(2,1)S(1)}, u32[]{:S(2)}, u32[]{:S(2)}) collective-permute-start(bf16[576,128]{1,0:T(8,128)(2,1)S(1)} %get-tuple-element.34), channel_id=1, source_target_pairs={{1,2},{2,1},{3,4},{4,3},{5,6},{6,5},{7,8},{8,7},{9,10},{10,9},{11,... | collective-permute-start | bytes 442376 | tf_op jit(solution)/shard_map/ppermute | solution.py:499
  23.2 7.4 %collective-permute-start.5 = (bf16[576,128]{1,0:T(8,128)(2,1)S(1)}, bf16[576,128]{1,0:T(8,128)(2,1)S(1)}, u32[]{:S(2)}, u32[]{:S(2)}) collective-permute-start(bf16[576,128]{1,0:T(8,128)(2,1)S(1)} %get-tuple-element.35), channel_id=1, source_target_pairs={{0,1},{1,0},{2,3},{3,2},{4,5},{5,4},{6,7},{7,6},{8,9},{9,8},{10,11... | collective-permute-start | bytes 442376 | tf_op jit(solution)/shard_map/ppermute | solution.py:500
  28.1 2.4 %collective-permute-start.3 = (bf16[8,1152]{1,0:T(8,128)(2,1)S(1)}, bf16[8,1152]{1,0:T(8,128)(2,1)S(1)}, u32[]{:S(2)}, u32[]{:S(2)}) collective-permute-start(bf16[8,1152]{1,0:T(8,128)(2,1)S(1)} %get-tuple-element.33), channel_id=1, source_target_pairs={{63,64},{64,63},{127,128},{128,127},{191,192},{192,191}} | collective-permute-start | bytes 55304 | tf_op jit(solution)/shard_map/ppermute | solution.py:498
  30.6 37.2 %all-to-all-start = ((bf16[64,56,128]{2,1,0:T(8,128)(2,1)}), bf16[64,56,128]{2,1,0:T(8,128)(2,1)S(1)}, u32[]{:S(2)}, u32[]{:S(2)}) async-start(bf16[64,56,128]{2,1,0:T(8,128)(2,1)} %pack.1), calls=%async_computation | async-start | bytes 1835008 | tf_op jit(solution)/shard_map/all_to_all | solution.py:543
  67.8 24.9 %all-to-all-start.1 = ((f32[64,8,256]{2,1,0:T(8,128)}), f32[64,8,256]{2,1,0:T(8,128)S(1)}, u32[]{:S(2)}, u32[]{:S(2)}) async-start(f32[64,8,256]{2,1,0:T(8,128)} %bitcast.8), calls=%async_computation.1 | async-start | bytes 1048576 | tf_op jit(solution)/shard_map/all_to_all | solution.py:563
  75.0 2.6 %collective-permute-start.6 = (f32[8,256]{1,0:T(8,128)S(1)}, f32[8,256]{1,0:T(8,128)S(1)}, u32[]{:S(2)}, u32[]{:S(2)}) collective-permute-start(f32[8,256]{1,0:T(8,128)S(1)} %get-tuple-element.43), channel_id=1, source_target_pairs={{63,64},{64,63},{127,128},{128,127},{191,192},{192,191}} | collective-permute-start | bytes 24584 | tf_op jit(solution)/shard_map/ppermute | solution.py:562

commit v4 on v3

--- a/solution.py
+++ b/solution.py
@@ -539,7 +539,6 @@
     got = exchanged(*sent)
     s = s.reshape(COLS, ROWS)
     (packed,) = call(pack_kernel, [shaped((MEMBERS, PACKED, 128))], (order_l, s), name="pack")
-    packed, *got = lax.optimization_barrier((packed, *got))
     recv = lax.all_to_all(packed, "member", split_axis=0, concat_axis=0, tiled=True)
 
     sums, far = call(

time: 94.1 us -> 106 us (1.13)
  starting transfers between devices: 35.9 us -> 50.8 us
  waiting for transfers between devices: 18.3 us -> 15.5 us
    all_to_all x1, starting transfers between devices: 7.16 us -> 26.2 us  [per_device(): lax.all_to_all(sums.reshape(MEMBERS, SLOTS, WIDE), 'member', split_axis=0...]
    all_to_all x1, starting transfers between devices: 11.9 us -> 7.21 us  [per_device(): lax.all_to_all(packed, 'member', split_axis=0, concat_axis=0, tiled=True)]
    all_to_all x1, waiting for transfers between devices: 3.15 us -> 0.01 us  [per_device(): lax.all_to_all(packed, 'member', split_axis=0, concat_axis=0, tiled=True)]
    ppermute x2, starting transfers between devices: 2.04 us -> 3.67 us  [exchanged(): away = lax.ppermute(away, axes, away_pairs)]
    ppermute x2, starting transfers between devices: 12.8 us -> 11.8 us  [exchanged(): return (far, away, lax.ppermute(near, axes, near_pairs))]
  transfers between devices with their start and end apart: 9 -> 9, of which waited for: 2 -> 3; matrix products, arithmetic and copies ran while one was open for 0% -> 0% of each run, Pallas kernels for 31% -> 26%
where the time goes in v4:
time: 106 us
  starting transfers between devices  50.8 us (48%)
  Pallas kernels  37.1 us (35%)
  waiting for transfers between devices  15.5 us (15%)
  local copies, waits for them, and re-layouts  1.6 us (2%)
    pallas_call x7, Pallas kernels, call(): pl.pallas_call(kernel, grid=(1,) if grid is None else grid, in_specs=spec...  37.1 us
    all_to_all x1, starting transfers between devices, per_device(): lax.all_to_all(sums.reshape(MEMBERS, SLOTS, WIDE), 'member', split_axis=0...  26.2 us
    all_to_all x1, waiting for transfers between devices, per_device(): lax.all_to_all(sums.reshape(MEMBERS, SLOTS, WIDE), 'member', split_axis=0...  15.2 us
    ppermute x2, starting transfers between devices, exchanged(): return (far, away, lax.ppermute(near, axes, near_pairs))  11.8 us
    all_to_all x1, starting transfers between devices, per_device(): lax.all_to_all(packed, 'member', split_axis=0, concat_axis=0, tiled=True)  7.21 us
    ppermute x2, starting transfers between devices, exchanged(): away = lax.ppermute(away, axes, away_pairs)  3.67 us
  transfers between devices with their start and end apart: 9, of which 3 were waited for; matrix products, arithmetic and copies ran while one was open for 0% of the time, Pallas kernels for 26%

profile of v4, /device:TPU:3, one launch (start us, length us, event | category | flops | bytes accessed | tf_op | source)
XLA Modules:
  0.0 105.7 jit_solution(12987734472935511476)
XLA Ops:
  0.6 0.0 copy-start
  0.6 0.9 copy-done
  1.6 0.0 copy-start.1
  1.6 0.7 copy-done.1
  2.2 0.8 rims.1
  3.0 0.7 collective-permute-start
  3.7 1.9 %collective-permute-start.1 = (bf16[192,128]{1,0:T(8,128)(2,1)S(1)}, bf16[192,128]{1,0:T(8,128)(2,1)S(1)}, u32[]{:S(2)}, u32[]{:S(2)}) collective-permute-start(bf16[192,128]{1,0:T(8,128)(2,1)S(1)} %get-tuple-element.26), channel_id=1, source_target_pairs={{1,2},{2,1},{3,4},{4,3},{5,6},{6,5},{7,8},{8,7},{9,10},{10,9},{11,... | collective-permute-start | bytes 147464 | tf_op jit(solution)/shard_map/ppermute | solution.py:499
  5.6 7.9 %collective-permute-start.2 = (bf16[192,128]{1,0:T(8,128)(2,1)S(1)}, bf16[192,128]{1,0:T(8,128)(2,1)S(1)}, u32[]{:S(2)}, u32[]{:S(2)}) collective-permute-start(bf16[192,128]{1,0:T(8,128)(2,1)S(1)} %get-tuple-element.27), channel_id=1, source_target_pairs={{0,1},{1,0},{2,3},{3,2},{4,5},{5,4},{6,7},{7,6},{8,9},{9,8},{10,11... | collective-permute-start | bytes 147464 | tf_op jit(solution)/shard_map/ppermute | solution.py:500
  13.5 3.5 %middle.1 = (bf16[6,64,192]{2,1,0:T(8,128)(2,1)S(1)}, f32[4,3,8,128]{3,2,1,0:T(8,128)S(1)}, f32[2,2,6,64,128]{4,3,2,1,0:T(8,128)S(1)}) custom-call(f32[8,256]{1,0:T(8,128)S(1)} %get-tuple-element.19.order_l_ref, f32[192,128]{1,0:T(8,128)S(1)} %get-tuple-element.20.order_s_ref, bf16[3,64,64,192]{3,2,1,0:T(8,128)(2,1)} %bitcast.17, ...), custom_call_target="tpu_custom_call" | custom-call | flops 1000000000 | bytes 5955584 | tf_op jit(solution)/shard_map/middle/pallas_call | solution.py:455
  17.1 0.0 collective-permute-done.far_ref
  17.1 0.0 collective-permute-done.1.away_ref
  17.1 0.0 collective-permute-done.2.near_ref
  17.1 6.0 %smooth.1 = (bf16[18,64,192]{2,1,0:T(8,128)(2,1)S(1)}, bf16[8,1152]{1,0:T(8,128)(2,1)S(1)}, bf16[576,128]{1,0:T(8,128)(2,1)S(1)}, bf16[576,128]{1,0:T(8,128)(2,1)S(1)}) custom-call(s32[1]{0:T(128)} %bitcast.me_ref, f32[8,256]{1,0:T(8,128)S(1)} %get-tuple-element.19.order_l_ref, f32[192,128]{1,0:T(8,128)S(1)} %get-tuple-element.20.order_s_ref, ...), custom_call_target="tpu_custom_call" | custom-call | flops 1000000000 | bytes 6668292 | tf_op jit(solution)/shard_map/smooth/pallas_call | solution.py:455
  23.1 1.8 %pack.1 = bf16[64,56,128]{2,1,0:T(8,128)(2,1)} custom-call(f32[8,256]{1,0:T(8,128)S(1)} %get-tuple-element.19.order_l_ref, bf16[1152,192]{1,0:T(8,128)(2,1)S(1)} %bitcast.13), custom_call_target="tpu_custom_call" | custom-call | bytes 1368064 | tf_op jit(solution)/shard_map/pack/pallas_call | solution.py:455
  24.8 7.2 %all-to-all-start = ((bf16[64,56,128]{2,1,0:T(8,128)(2,1)}), bf16[64,56,128]{2,1,0:T(8,128)(2,1)S(1)}, u32[]{:S(2)}, u32[]{:S(2)}) async-start(bf16[64,56,128]{2,1,0:T(8,128)(2,1)} %pack.1), calls=%async_computation | async-start | bytes 1835008 | tf_op jit(solution)/shard_map/all_to_all | solution.py:542
  32.1 1.7 %collective-permute-start.4 = (bf16[576,128]{1,0:T(8,128)(2,1)S(1)}, bf16[576,128]{1,0:T(8,128)(2,1)S(1)}, u32[]{:S(2)}, u32[]{:S(2)}) collective-permute-start(bf16[576,128]{1,0:T(8,128)(2,1)S(1)} %get-tuple-element.32), channel_id=1, source_target_pairs={{1,2},{2,1},{3,4},{4,3},{5,6},{6,5},{7,8},{8,7},{9,10},{10,9},{11,... | collective-permute-start | bytes 442376 | tf_op jit(solution)/shard_map/ppermute | solution.py:499
  33.8 3.9 %collective-permute-start.5 = (bf16[576,128]{1,0:T(8,128)(2,1)S(1)}, bf16[576,128]{1,0:T(8,128)(2,1)S(1)}, u32[]{:S(2)}, u32[]{:S(2)}) collective-permute-start(bf16[576,128]{1,0:T(8,128)(2,1)S(1)} %get-tuple-element.33), channel_id=1, source_target_pairs={{0,1},{1,0},{2,3},{3,2},{4,5},{5,4},{6,7},{7,6},{8,9},{9,8},{10,11... | collective-permute-start | bytes 442376 | tf_op jit(solution)/shard_map/ppermute | solution.py:500
  37.7 0.7 collective-permute-start.3
  38.3 0.0 collective-permute-done.3.far_ref
  38.3 0.2 collective-permute-done.4.away_ref
  38.5 0.1 collective-permute-done.5.near_ref
  38.7 22.1 %product.1 = (f32[512,256]{1,0:T(8,128)}, f32[8,256]{1,0:T(8,128)S(1)}) custom-call(s32[1]{0:T(128)} %bitcast.me_ref, f32[8,256]{1,0:T(8,128)S(1)} %get-tuple-element.19.order_l_ref, f32[192,128]{1,0:T(8,128)S(1)} %get-tuple-element.20.order_s_ref, bf16[3,64,64,192]{3,2,1,0:T(8,128)(2,1)} %bitcast.19, bf16[1152,192]{1,0:T(8,128)(2,1)S(1)} %bitcast.14, ...), custom_call_target="tpu_custom_call" | custom-call | flops 10000000000 | bytes 6113284 | tf_op jit(solution)/shard_map/product/pallas_call | solution.py:455
  60.8 0.0 all-to-all-done.recv_ref
  60.8 26.2 %all-to-all-start.1 = ((f32[64,8,256]{2,1,0:T(8,128)}), f32[64,8,256]{2,1,0:T(8,128)S(1)}, u32[]{:S(2)}, u32[]{:S(2)}) async-start(f32[64,8,256]{2,1,0:T(8,128)} %bitcast.8), calls=%async_computation.1 | async-start | bytes 1048576 | tf_op jit(solution)/shard_map/all_to_all | solution.py:562
  87.0 0.7 collective-permute-start.6
  87.7 1.9 %unpack_smooth.1 = (bf16[1152,192]{1,0:T(8,128)(2,1)}, bf16[192,512]{1,0:T(8,128)(2,1)S(1)}) custom-call(bf16[64,56,128]{2,1,0:T(8,128)(2,1)S(1)} %all-to-all-done.recv_ref), custom_call_target="tpu_custom_call" | custom-call | flops 1000000000 | bytes 1556480 | tf_op jit(solution)/shard_map/unpack_smooth/pallas_call | solution.py:455
  89.6 0.0 collective-permute-done.6.far_ref
  89.6 15.2 %all-to-all-done.1 = f32[64,8,256]{2,1,0:T(8,128)S(1)} async-done(((f32[64,8,256]{2,1,0:T(8,128)}), f32[64,8,256]{2,1,0:T(8,128)S(1)}, u32[]{:S(2)}, u32[]{:S(2)}) %all-to-all-start.1) | async-done | bytes 524320 | tf_op jit(solution)/shard_map/all_to_all | solution.py:562
  104.7 1.0 unpack_coarse.1
Async XLA Ops:
  0.6 0.9 copy-start
  1.6 0.7 copy-start.1
  3.0 14.0 %collective-permute-start = (bf16[8,384]{1,0:T(8,128)(2,1)S(1)}, bf16[8,384]{1,0:T(8,128)(2,1)S(1)}, u32[]{:S(2)}, u32[]{:S(2)}) collective-permute-start(bf16[8,384]{1,0:T(8,128)(2,1)S(1)} %get-tuple-element.25), channel_id=1, source_target_pairs={{63,64},{64,63},{127,128},{128,127},{191,192},{192,191}} | collective-permute-start | bytes 18440 | tf_op jit(solution)/shard_map/ppermute | solution.py:498
  3.7 13.4 %collective-permute-start.1 = (bf16[192,128]{1,0:T(8,128)(2,1)S(1)}, bf16[192,128]{1,0:T(8,128)(2,1)S(1)}, u32[]{:S(2)}, u32[]{:S(2)}) collective-permute-start(bf16[192,128]{1,0:T(8,128)(2,1)S(1)} %get-tuple-element.26), channel_id=1, source_target_pairs={{1,2},{2,1},{3,4},{4,3},{5,6},{6,5},{7,8},{8,7},{9,10},{10,9},{11,... | collective-permute-start | bytes 147464 | tf_op jit(solution)/shard_map/ppermute | solution.py:499
  5.6 11.5 %collective-permute-start.2 = (bf16[192,128]{1,0:T(8,128)(2,1)S(1)}, bf16[192,128]{1,0:T(8,128)(2,1)S(1)}, u32[]{:S(2)}, u32[]{:S(2)}) collective-permute-start(bf16[192,128]{1,0:T(8,128)(2,1)S(1)} %get-tuple-element.27), channel_id=1, source_target_pairs={{0,1},{1,0},{2,3},{3,2},{4,5},{5,4},{6,7},{7,6},{8,9},{9,8},{10,11... | collective-permute-start | bytes 147464 | tf_op jit(solution)/shard_map/ppermute | solution.py:500
  24.8 36.0 %all-to-all-start = ((bf16[64,56,128]{2,1,0:T(8,128)(2,1)}), bf16[64,56,128]{2,1,0:T(8,128)(2,1)S(1)}, u32[]{:S(2)}, u32[]{:S(2)}) async-start(bf16[64,56,128]{2,1,0:T(8,128)(2,1)} %pack.1), calls=%async_computation | async-start | bytes 1835008 | tf_op jit(solution)/shard_map/all_to_all | solution.py:542
  32.1 6.5 %collective-permute-start.4 = (bf16[576,128]{1,0:T(8,128)(2,1)S(1)}, bf16[576,128]{1,0:T(8,128)(2,1)S(1)}, u32[]{:S(2)}, u32[]{:S(2)}) collective-permute-start(bf16[576,128]{1,0:T(8,128)(2,1)S(1)} %get-tuple-element.32), channel_id=1, source_target_pairs={{1,2},{2,1},{3,4},{4,3},{5,6},{6,5},{7,8},{8,7},{9,10},{10,9},{11,... | collective-permute-start | bytes 442376 | tf_op jit(solution)/shard_map/ppermute | solution.py:499
  33.8 4.9 %collective-permute-start.5 = (bf16[576,128]{1,0:T(8,128)(2,1)S(1)}, bf16[576,128]{1,0:T(8,128)(2,1)S(1)}, u32[]{:S(2)}, u32[]{:S(2)}) collective-permute-start(bf16[576,128]{1,0:T(8,128)(2,1)S(1)} %get-tuple-element.33), channel_id=1, source_target_pairs={{0,1},{1,0},{2,3},{3,2},{4,5},{5,4},{6,7},{7,6},{8,9},{9,8},{10,11... | collective-permute-start | bytes 442376 | tf_op jit(solution)/shard_map/ppermute | solution.py:500
  37.7 0.7 collective-permute-start.3
  60.8 43.9 %all-to-all-start.1 = ((f32[64,8,256]{2,1,0:T(8,128)}), f32[64,8,256]{2,1,0:T(8,128)S(1)}, u32[]{:S(2)}, u32[]{:S(2)}) async-start(f32[64,8,256]{2,1,0:T(8,128)} %bitcast.8), calls=%async_computation.1 | async-start | bytes 1048576 | tf_op jit(solution)/shard_map/all_to_all | solution.py:562
  87.0 2.6 %collective-permute-start.6 = (f32[8,256]{1,0:T(8,128)S(1)}, f32[8,256]{1,0:T(8,128)S(1)}, u32[]{:S(2)}, u32[]{:S(2)}) collective-permute-start(f32[8,256]{1,0:T(8,128)S(1)} %get-tuple-element.35), channel_id=1, source_target_pairs={{63,64},{64,63},{127,128},{128,127},{191,192},{192,191}} | collective-permute-start | bytes 24584 | tf_op jit(solution)/shard_map/ppermute | solution.py:561

commit v5 on v3

--- a/solution.py
+++ b/solution.py
@@ -319,6 +319,11 @@
 
 
 OFFSETS = [[(k, 6 * (e - k)) for k in range(3) if 0 <= e - k <= 2] for e in range(5)]
+
+
+def spare_lanes(axis):
+    entry, spare = iota((WIDE, WIDE), axis), iota((WIDE, WIDE), 1 - axis) - 252
+    return ones_where((spare >= 0) & (entry == 108 + 7 * spare))
 
 
 def product_kernel(
@@ -404,7 +409,9 @@
         for k in range(3):
             prod = exact_dot(picks[k], terms[k], NT, True)
             total = prod if total is None else total + prod
-        out_ref[...] = total
+        high = total.astype(BF16).astype(F32)
+        rest = dot((total - high).astype(BF16), spare_lanes(0))
+        out_ref[...] = (high + rest).astype(BF16)
         head, tail = far_pick(r, me, ROWS)
         far_out[...] = exact_dot(head, terms[0], NT, True) + exact_dot(tail, terms[2], NT, True)
 
@@ -435,7 +442,8 @@
 
 def unpack_coarse_kernel(me_ref, pick_ref, sums_ref, far_ref, out_ref):
     me = me_ref[0]
-    total = exact_dot(pick_ref[...], sums_ref[...], (((1,), (0,)), ((), ())), True)
+    total = dot(pick_ref[...], sums_ref[...])
+    total = total + dot(total.astype(BF16), spare_lanes(1))
     row = iota((ROWS, WIDE), 0)
     edge = jnp.where(me == 0, 0, ROWS - 1)
     far = jnp.broadcast_to(far_ref[0:1, :], (ROWS, WIDE))
@@ -544,7 +552,7 @@
 
     sums, far = call(
         product_kernel,
-        [shaped((MEMBERS * SLOTS, WIDE), F32), shaped((8, WIDE), F32)],
+        [shaped((MEMBERS * SLOTS, WIDE)), shaped((8, WIDE), F32)],
         (me, order_l, order_s, a, s, *got),
         grid=grid,
         in_specs={3: a_spec},

time: 94.1 us -> 90 us (0.956)
  waiting for transfers between devices: 18.3 us -> 13.3 us
    all_to_all x1, waiting for transfers between devices: 15.2 us -> 10.6 us  [per_device(): lax.all_to_all(sums.reshape(MEMBERS, SLOTS, WIDE), 'member', split_axis=0...]
  transfers between devices with their start and end apart: 9 -> 9, of which waited for: 2 -> 2; matrix products, arithmetic and copies ran while one was open for 0% -> 0% of each run, Pallas kernels for 31% -> 33%
where the time goes in v5:
time: 90 us; the launch traced here: 89.7 us
  Pallas kernels  37.6 us (42%)
  starting transfers between devices  36.4 us (40%)
  waiting for transfers between devices  13.3 us (15%)
  local copies, waits for them, and re-layouts  1.6 us (2%)
    pallas_call x7, Pallas kernels, call(): pl.pallas_call(kernel, grid=(1,) if grid is None else grid, in_specs=spec...  37.6 us
    ppermute x2, starting transfers between devices, exchanged(): return (far, away, lax.ppermute(near, axes, near_pairs))  12.8 us
    all_to_all x1, starting transfers between devices, per_device(): lax.all_to_all(packed, 'member', split_axis=0, concat_axis=0, tiled=True)  11.9 us
    all_to_all x1, waiting for transfers between devices, per_device(): lax.all_to_all(sums.reshape(MEMBERS, SLOTS, WIDE), 'member', split_axis=0...  10.6 us
    all_to_all x1, starting transfers between devices, per_device(): lax.all_to_all(sums.reshape(MEMBERS, SLOTS, WIDE), 'member', split_axis=0...  7.66 us
    all_to_all x1, waiting for transfers between devices, per_device(): lax.all_to_all(packed, 'member', split_axis=0, concat_axis=0, tiled=True)  2.66 us
    ppermute x2, starting transfers between devices, exchanged(): away = lax.ppermute(away, axes, away_pairs)  2.04 us
  transfers between devices with their start and end apart: 9, of which 2 were waited for; matrix products, arithmetic and copies ran while one was open for 0% of the time, Pallas kernels for 33%

profile of v5, /device:TPU:3, one launch (start us, length us, event | category | flops | bytes accessed | tf_op | source)
XLA Modules:
  0.0 89.7 jit_solution(369809624571101417)
XLA Ops:
  0.6 0.0 copy-start
  0.6 0.9 %copy-done = bf16[192,6,64]{0,2,1:T(8,128)(2,1)S(1)} copy-done((bf16[192,6,64]{0,2,1:T(8,128)(2,1)S(1)}, bf16[192,6,64]{0,2,1:T(8,128)(2,1)}, u32[]{:S(2)}) %copy-start) | copy-done | bytes 147480
  1.6 0.0 copy-start.1
  1.6 0.7 copy-done.1
  2.2 0.8 rims.1
  3.0 0.7 collective-permute-start
  3.7 1.9 %collective-permute-start.1 = (bf16[192,128]{1,0:T(8,128)(2,1)S(1)}, bf16[192,128]{1,0:T(8,128)(2,1)S(1)}, u32[]{:S(2)}, u32[]{:S(2)}) collective-permute-start(bf16[192,128]{1,0:T(8,128)(2,1)S(1)} %get-tuple-element.30), channel_id=1, source_target_pairs={{1,2},{2,1},{3,4},{4,3},{5,6},{6,5},{7,8},{8,7},{9,10},{10,9},{11,... | collective-permute-start | bytes 147464 | tf_op jit(solution)/shard_map/ppermute | solution.py:507
  5.6 7.9 %collective-permute-start.2 = (bf16[192,128]{1,0:T(8,128)(2,1)S(1)}, bf16[192,128]{1,0:T(8,128)(2,1)S(1)}, u32[]{:S(2)}, u32[]{:S(2)}) collective-permute-start(bf16[192,128]{1,0:T(8,128)(2,1)S(1)} %get-tuple-element.31), channel_id=1, source_target_pairs={{0,1},{1,0},{2,3},{3,2},{4,5},{5,4},{6,7},{7,6},{8,9},{9,8},{10,11... | collective-permute-start | bytes 147464 | tf_op jit(solution)/shard_map/ppermute | solution.py:508
  13.5 3.5 %middle.1 = (bf16[6,64,192]{2,1,0:T(8,128)(2,1)S(1)}, f32[4,3,8,128]{3,2,1,0:T(8,128)S(1)}, f32[2,2,6,64,128]{4,3,2,1,0:T(8,128)S(1)}) custom-call(f32[8,256]{1,0:T(8,128)S(1)} %get-tuple-element.23.order_l_ref, f32[192,128]{1,0:T(8,128)S(1)} %get-tuple-element.24.order_s_ref, bf16[3,64,64,192]{3,2,1,0:T(8,128)(2,1)} %bitcast.17, ...), custom_call_target="tpu_custom_call" | custom-call | flops 1000000000 | bytes 5955584 | tf_op jit(solution)/shard_map/middle/pallas_call | solution.py:463
  17.1 0.0 collective-permute-done.far_ref
  17.1 0.0 collective-permute-done.1.away_ref
  17.1 0.0 collective-permute-done.2.near_ref
  17.1 6.0 %smooth.1 = (bf16[18,64,192]{2,1,0:T(8,128)(2,1)S(1)}, bf16[8,1152]{1,0:T(8,128)(2,1)S(1)}, bf16[576,128]{1,0:T(8,128)(2,1)S(1)}, bf16[576,128]{1,0:T(8,128)(2,1)S(1)}) custom-call(s32[1]{0:T(128)} %bitcast.me_ref, f32[8,256]{1,0:T(8,128)S(1)} %get-tuple-element.23.order_l_ref, f32[192,128]{1,0:T(8,128)S(1)} %get-tuple-element.24.order_s_ref, ...), custom_call_target="tpu_custom_call" | custom-call | flops 1000000000 | bytes 6668292 | tf_op jit(solution)/shard_map/smooth/pallas_call | solution.py:463
  23.1 0.1 collective-permute-start.4
  23.2 5.0 %collective-permute-start.5 = (bf16[576,128]{1,0:T(8,128)(2,1)S(1)}, bf16[576,128]{1,0:T(8,128)(2,1)S(1)}, u32[]{:S(2)}, u32[]{:S(2)}) collective-permute-start(bf16[576,128]{1,0:T(8,128)(2,1)S(1)} %get-tuple-element.35), channel_id=1, source_target_pairs={{0,1},{1,0},{2,3},{3,2},{4,5},{5,4},{6,7},{7,6},{8,9},{9,8},{10,11... | collective-permute-start | bytes 442376 | tf_op jit(solution)/shard_map/ppermute | solution.py:508
  28.1 0.7 collective-permute-start.3
  28.8 1.8 %pack.1 = bf16[64,56,128]{2,1,0:T(8,128)(2,1)} custom-call(f32[8,256]{1,0:T(8,128)S(1)} %get-tuple-element.23.order_l_ref, bf16[1152,192]{1,0:T(8,128)(2,1)S(1)} %bitcast.13), custom_call_target="tpu_custom_call" | custom-call | bytes 1368064 | tf_op jit(solution)/shard_map/pack/pallas_call | solution.py:463
  30.6 0.0 collective-permute-done.3.far_ref
  30.6 0.0 collective-permute-done.4.away_ref
  30.6 0.0 collective-permute-done.5.near_ref
  30.6 11.9 %all-to-all-start = ((bf16[64,56,128]{2,1,0:T(8,128)(2,1)}), bf16[64,56,128]{2,1,0:T(8,128)(2,1)S(1)}, u32[]{:S(2)}, u32[]{:S(2)}) async-start(bf16[64,56,128]{2,1,0:T(8,128)(2,1)} %pack.1), calls=%async_computation | async-start | bytes 1835008 | tf_op jit(solution)/shard_map/all_to_all | solution.py:551
  42.5 22.6 %product.1 = (bf16[512,256]{1,0:T(8,128)(2,1)}, f32[8,256]{1,0:T(8,128)S(1)}) custom-call(s32[1]{0:T(128)} %bitcast.me_ref, f32[8,256]{1,0:T(8,128)S(1)} %get-tuple-element.23.order_l_ref, f32[192,128]{1,0:T(8,128)S(1)} %get-tuple-element.24.order_s_ref, bf16[3,64,64,192]{3,2,1,0:T(8,128)(2,1)} %bitcast.19, bf16[1152,192]{1,0:T(8,128)(2,1)S(1)} %bitcast.14, ...), custom_call_target="tpu_custom_call" | custom-call | flops 10000000000 | bytes 5851140 | tf_op jit(solution)/shard_map/product/pallas_call | solution.py:463
  65.1 2.7 %all-to-all-done.recv_ref = bf16[64,56,128]{2,1,0:T(8,128)(2,1)S(1)} async-done(((bf16[64,56,128]{2,1,0:T(8,128)(2,1)}), bf16[64,56,128]{2,1,0:T(8,128)(2,1)S(1)}, u32[]{:S(2)}, u32[]{:S(2)}) %all-to-all-start) | async-done | bytes 917536 | tf_op jit(solution)/shard_map/all_to_all | solution.py:551
  67.8 7.7 %all-to-all-start.1 = ((bf16[64,8,256]{2,1,0:T(8,128)(2,1)}), bf16[64,8,256]{2,1,0:T(8,128)(2,1)S(1)}, u32[]{:S(2)}, u32[]{:S(2)}) async-start(bf16[64,8,256]{2,1,0:T(8,128)(2,1)} %bitcast.8), calls=%async_computation.1 | async-start | bytes 524288 | tf_op jit(solution)/shard_map/all_to_all | solution.py:571
  75.5 0.7 collective-permute-start.6
  76.1 1.9 %unpack_smooth.1 = (bf16[1152,192]{1,0:T(8,128)(2,1)}, bf16[192,512]{1,0:T(8,128)(2,1)S(1)}) custom-call(bf16[64,56,128]{2,1,0:T(8,128)(2,1)S(1)} %all-to-all-done.recv_ref), custom_call_target="tpu_custom_call" | custom-call | flops 1000000000 | bytes 1556480 | tf_op jit(solution)/shard_map/unpack_smooth/pallas_call | solution.py:463
  78.0 0.0 collective-permute-done.6.far_ref
  78.0 10.6 %all-to-all-done.1 = bf16[64,8,256]{2,1,0:T(8,128)(2,1)S(1)} async-done(((bf16[64,8,256]{2,1,0:T(8,128)(2,1)}), bf16[64,8,256]{2,1,0:T(8,128)(2,1)S(1)}, u32[]{:S(2)}, u32[]{:S(2)}) %all-to-all-start.1) | async-done | bytes 262176 | tf_op jit(solution)/shard_map/all_to_all | solution.py:571
  88.6 1.0 %unpack_coarse.1 = f32[192,252]{1,0:T(8,128)} custom-call(s32[1]{0:T(128)} %bitcast.me_ref, bf16[192,512]{1,0:T(8,128)(2,1)S(1)} %get-tuple-element.38.pick_ref, bf16[512,256]{1,0:T(8,128)(2,1)S(1)} %bitcast.12, f32[8,256]{1,0:T(8,128)S(1)} %collective-permute-done.6.far_ref), custom_call_target="tpu_custom_call" | custom-call | bytes 660484 | tf_op jit(solution)/shard_map/unpack_coarse/pallas_call | solution.py:463
Async XLA Ops:
  0.6 0.9 %copy-start = (bf16[192,6,64]{0,2,1:T(8,128)(2,1)S(1)}, bf16[192,6,64]{0,2,1:T(8,128)(2,1)}, u32[]{:S(2)}) copy-start(bf16[192,6,64]{0,2,1:T(8,128)(2,1)} %param.4) | copy-start | bytes 442372
  1.6 0.7 copy-start.1
  3.0 14.0 %collective-permute-start = (bf16[8,384]{1,0:T(8,128)(2,1)S(1)}, bf16[8,384]{1,0:T(8,128)(2,1)S(1)}, u32[]{:S(2)}, u32[]{:S(2)}) collective-permute-start(bf16[8,384]{1,0:T(8,128)(2,1)S(1)} %get-tuple-element.29), channel_id=1, source_target_pairs={{63,64},{64,63},{127,128},{128,127},{191,192},{192,191}} | collective-permute-start | bytes 18440 | tf_op jit(solution)/shard_map/ppermute | solution.py:506
  3.7 13.4 %collective-permute-start.1 = (bf16[192,128]{1,0:T(8,128)(2,1)S(1)}, bf16[192,128]{1,0:T(8,128)(2,1)S(1)}, u32[]{:S(2)}, u32[]{:S(2)}) collective-permute-start(bf16[192,128]{1,0:T(8,128)(2,1)S(1)} %get-tuple-element.30), channel_id=1, source_target_pairs={{1,2},{2,1},{3,4},{4,3},{5,6},{6,5},{7,8},{8,7},{9,10},{10,9},{11,... | collective-permute-start | bytes 147464 | tf_op jit(solution)/shard_map/ppermute | solution.py:507
  5.6 11.5 %collective-permute-start.2 = (bf16[192,128]{1,0:T(8,128)(2,1)S(1)}, bf16[192,128]{1,0:T(8,128)(2,1)S(1)}, u32[]{:S(2)}, u32[]{:S(2)}) collective-permute-start(bf16[192,128]{1,0:T(8,128)(2,1)S(1)} %get-tuple-element.31), channel_id=1, source_target_pairs={{0,1},{1,0},{2,3},{3,2},{4,5},{5,4},{6,7},{7,6},{8,9},{9,8},{10,11... | collective-permute-start | bytes 147464 | tf_op jit(solution)/shard_map/ppermute | solution.py:508
  23.1 7.5 %collective-permute-start.4 = (bf16[576,128]{1,0:T(8,128)(2,1)S(1)}, bf16[576,128]{1,0:T(8,128)(2,1)S(1)}, u32[]{:S(2)}, u32[]{:S(2)}) collective-permute-start(bf16[576,128]{1,0:T(8,128)(2,1)S(1)} %get-tuple-element.34), channel_id=1, source_target_pairs={{1,2},{2,1},{3,4},{4,3},{5,6},{6,5},{7,8},{8,7},{9,10},{10,9},{11,... | collective-permute-start | bytes 442376 | tf_op jit(solution)/shard_map/ppermute | solution.py:507
  23.2 7.4 %collective-permute-start.5 = (bf16[576,128]{1,0:T(8,128)(2,1)S(1)}, bf16[576,128]{1,0:T(8,128)(2,1)S(1)}, u32[]{:S(2)}, u32[]{:S(2)}) collective-permute-start(bf16[576,128]{1,0:T(8,128)(2,1)S(1)} %get-tuple-element.35), channel_id=1, source_target_pairs={{0,1},{1,0},{2,3},{3,2},{4,5},{5,4},{6,7},{7,6},{8,9},{9,8},{10,11... | collective-permute-start | bytes 442376 | tf_op jit(solution)/shard_map/ppermute | solution.py:508
  28.1 2.4 %collective-permute-start.3 = (bf16[8,1152]{1,0:T(8,128)(2,1)S(1)}, bf16[8,1152]{1,0:T(8,128)(2,1)S(1)}, u32[]{:S(2)}, u32[]{:S(2)}) collective-permute-start(bf16[8,1152]{1,0:T(8,128)(2,1)S(1)} %get-tuple-element.33), channel_id=1, source_target_pairs={{63,64},{64,63},{127,128},{128,127},{191,192},{192,191}} | collective-permute-start | bytes 55304 | tf_op jit(solution)/shard_map/ppermute | solution.py:506
  30.6 37.2 %all-to-all-start = ((bf16[64,56,128]{2,1,0:T(8,128)(2,1)}), bf16[64,56,128]{2,1,0:T(8,128)(2,1)S(1)}, u32[]{:S(2)}, u32[]{:S(2)}) async-start(bf16[64,56,128]{2,1,0:T(8,128)(2,1)} %pack.1), calls=%async_computation | async-start | bytes 1835008 | tf_op jit(solution)/shard_map/all_to_all | solution.py:551
  67.8 20.8 %all-to-all-start.1 = ((bf16[64,8,256]{2,1,0:T(8,128)(2,1)}), bf16[64,8,256]{2,1,0:T(8,128)(2,1)S(1)}, u32[]{:S(2)}, u32[]{:S(2)}) async-start(bf16[64,8,256]{2,1,0:T(8,128)(2,1)} %bitcast.8), calls=%async_computation.1 | async-start | bytes 524288 | tf_op jit(solution)/shard_map/all_to_all | solution.py:571
  75.5 2.6 %collective-permute-start.6 = (f32[8,256]{1,0:T(8,128)S(1)}, f32[8,256]{1,0:T(8,128)S(1)}, u32[]{:S(2)}, u32[]{:S(2)}) collective-permute-start(f32[8,256]{1,0:T(8,128)S(1)} %get-tuple-element.43), channel_id=1, source_target_pairs={{63,64},{64,63},{127,128},{128,127},{191,192},{192,191}} | collective-permute-start | bytes 24584 | tf_op jit(solution)/shard_map/ppermute | solution.py:570

commit v6 on v5

--- a/solution.py
+++ b/solution.py
@@ -215,87 +215,110 @@
     return pl.ds(pl.multiple_of(16 * ib, 8), 8), pl.ds(pl.multiple_of(16 * ib + 8, 8), 8)
 
 
+def end_picks(r):
+    lane = iota((ROWS, 128), 1)
+    bucket = jnp.where(lane < TILE, lane, lane - TILE).astype(F32)
+    mine = r.owner_s == bucket
+    first = ones_where(mine & (lane < TILE) & (r.rank_s == 0.0))
+    last = ones_where(mine & (lane >= TILE) & (r.after_s == 0.0))
+    return first, last
+
+
 def middle_kernel(
-    order_l_ref, order_s_ref, a_hbm, p_ref, mid_ref, scale_ref, local_ref,
-    a_ref, sems, group_ref, wide_ref, out_ref,
+    order_l_ref, order_s_ref, a_hbm, p_ref, s_ref, ends_ref, end_scale_ref,
+    a_ref, sems, group_ref, wide_ref, out_ref, scale_ref,
 ):
     ib = pl.program_id(0)
+    r = Order(order_l_ref, order_s_ref)
 
     @pl.when(ib == 0)
     def _():
-        start_copies(a_hbm, a_ref, sems, (1,))
-        before, here, after = local_rows(p_ref[...], Order(order_l_ref, order_s_ref))
-        set_wide(wide_ref, 0, here)
-        set_wide(local_ref, 0, before)
-        set_wide(local_ref, 1, after)
-
-    next_groups(a_hbm, a_ref, sems, (1,), ib, group_ref)
+        start_copies(a_hbm, a_ref, sems, (0, 1, 2))
+        for k, value in enumerate(local_rows(p_ref[...], r)):
+            set_wide(wide_ref, k, value)
+
+    next_groups(a_hbm, a_ref, sems, (0, 1, 2), ib, group_ref)
     sub, lane = iota((8, 128), 0), iota((8, 128), 1)
     lower, upper = halves(ib)
+    rows = pl.ds(pl.multiple_of(16 * ib, 16), 16)
+    first, last = end_picks(r)
+    ends = dot(a_ref[0, rows].reshape(16 * TILE, ROWS), first) + dot(a_ref[2, rows].reshape(16 * TILE, ROWS), last)
+    ends_ref[rows] = ends.reshape(16, TILE, 128).astype(BF16)
 
     def one_group(g, carry):
         tile = jnp.where(g == 2, 1, 0)
         second = (g == 1) | ((g == 2) & (lane >= TILE))
         diag = jnp.zeros((8, 128), F32)
         for i in range(8):
-            entry = jnp.where(second, group_ref[g, 0, i, upper, :], group_ref[g, 0, i, lower, :])
+            entry = jnp.where(second, group_ref[g, 1, i, upper, :], group_ref[g, 1, i, lower, :])
             diag = jnp.where(sub == i, entry, diag)
         scale = 0.6 * (1.0 / diag)
-        scale_ref[ib, g] = scale
-        for half in (0, 1):
-            columns = [3 * half + c for c in range(3)]
-            sums = contracted(group_ref, wide_ref, g, tile, [(0, 0)], columns)
-            for c, total in zip(columns, sums):
-                own = jnp.where(second, wide_ref[tile, 0, c, upper, :], wide_ref[tile, 0, c, lower, :])
-                out_ref[g, c] = own - scale * total
-        return carry
-
-    lax.fori_loop(0, 3, one_group, 0)
-    rows = pl.ds(pl.multiple_of(16 * ib, 16), 16)
-    for index in range(6):
-        mid_ref[index, rows, :] = ungrouped(out_ref, index).astype(BF16)
-
-
-def smooth_kernel(
-    me_ref, order_l_ref, order_s_ref, a_hbm, mid_ref, scale_ref, local_ref, far_ref, away_ref, near_ref,
-    s_ref, far_out, away_out, near_out, a_ref, sems, group_ref, wide_ref, out_ref,
-):
-    ib = pl.program_id(0)
-    me = me_ref[0]
-
-    @pl.when(ib == 0)
-    def _():
-        start_copies(a_hbm, a_ref, sems, (0, 2))
-        r = Order(order_l_ref, order_s_ref)
-        for k, value in enumerate(rim_rows(near_ref[...], away_ref[...], far_ref[...], r, me)):
-            set_wide(wide_ref, k, value)
-        wide_ref[...] += local_ref[...]
-        s_ref[6:12] = mid_ref[...]
-
-    next_groups(a_hbm, a_ref, sems, (0, 2), ib, group_ref)
-
-    def one_group(g, carry):
-        tile = jnp.where(g == 2, 1, 0)
-        scale = 0.0 - scale_ref[ib, g]
-        for k in range(2):
+        out_ref[g, 18] = scale
+        for k in range(3):
             for half in (0, 1):
                 columns = [3 * half + c for c in range(3)]
                 sums = contracted(group_ref, wide_ref, g, tile, [(k, 0)], columns)
                 for c, total in zip(columns, sums):
-                    out_ref[g, 6 * k + c] = scale * total
+                    value = scale * total
+                    if k == 1:
+                        own = jnp.where(second, wide_ref[tile, 1, c, upper, :], wide_ref[tile, 1, c, lower, :])
+                        value = own - value
+                    else:
+                        value = 0.0 - value
+                    out_ref[g, 6 * k + c] = value
         return carry
 
     lax.fori_loop(0, 3, one_group, 0)
-    rows = pl.ds(pl.multiple_of(16 * ib, 16), 16)
-    for index in range(12):
-        s_ref[index if index < 6 else index + 6, rows, :] = ungrouped(out_ref, index).astype(BF16)
+    for index in range(18):
+        s_ref[index, rows, :] = ungrouped(out_ref, index).astype(BF16)
+    scale_ref[rows, :] = ungrouped(out_ref, 18)
 
     @pl.when(ib == pl.num_programs(0) - 1)
     def _():
-        r = Order(order_l_ref, order_s_ref)
-        flat = s_ref[...].reshape(COLS, ROWS)
-        for ref, rim in zip((far_out, away_out, near_out), rims_of(flat, r, me)):
-            ref[...] = rim
+        end_scale_ref[...] = exact_dot(first + last, scale_ref[...], (((1,), (0,)), ((), ())), False)
+
+
+def smooth_kernel(
+    me_ref, order_l_ref, order_s_ref, part_ref, ends_ref, end_scale_ref, far_ref, away_ref, near_ref,
+    s_ref, far_out, away_out, near_out, group_ref, wide_ref, end_ref,
+):
+    me = me_ref[0]
+    even = me % 2 == 0
+    near, away = near_ref[...].astype(F32), away_ref[...].astype(F32)
+    left, right = jnp.where(even, away, near), jnp.where(even, near, away)
+    top = jnp.concatenate([left[:, :TILE], right[:, :TILE]], 1)
+    bottom = jnp.concatenate([left[:, TILE:], right[:, TILE:]], 1)
+    row, lane = iota((8, 128), 0), iota((8, 128), 1)
+    spot = ((me == 0) & (lane == 0)) | ((me == MEMBERS - 1) & (lane == 127))
+    across = lax.dot_general(far_ref[...], ones_where((row == 0) & spot), TN, preferred_element_type=F32)
+    wide_ref[0, 0] = (jnp.concatenate([top, bottom], 0) + across).reshape(MODES, TILE, 128)
+
+    def one_group(g, carry):
+        rows = pl.ds(pl.multiple_of(8 * g, 8), 8)
+        for i in range(8):
+            group_ref[0, 0, i] = ends_ref[8 * g + i].astype(F32)
+        for half in (0, 1):
+            columns = [3 * half + c for c in range(3)]
+            sums = contracted(group_ref, wide_ref, 0, 0, [(0, 0)], columns)
+            for c, total in zip(columns, sums):
+                end_ref[c, rows, :] = 0.0 - end_scale_ref[rows, :] * total
+        return carry
+
+    lax.fori_loop(0, TILE // 8, one_group, 0)
+    r = Order(order_l_ref, order_s_ref)
+    bucket = iota((128, ROWS), 0).astype(F32)
+    owner = r.owner_l[:, :ROWS]
+    first = ones_where((owner == bucket) & (r.rank_l[:, :ROWS] == 0.0))
+    last = ones_where((owner + float(TILE) == bucket) & (r.after_l[:, :ROWS] == 0.0))
+    found = end_ref[...].astype(BF16).reshape(MODES * TILE, 128)
+    s_ref[MODES : 2 * MODES] = part_ref[MODES : 2 * MODES]
+    for k, pick in ((0, first), (2, last)):
+        at = slice(MODES * k, MODES * (k + 1))
+        value = dot(found, pick).reshape(MODES, TILE, ROWS) + part_ref[at].astype(F32)
+        s_ref[at] = value.astype(BF16)
+    flat = s_ref[...].reshape(COLS, ROWS)
+    for ref, rim in zip((far_out, away_out, near_out), rims_of(flat, r, me)):
+        ref[...] = rim
 
 
 def slot_grid(width):
@@ -517,17 +540,17 @@
         name="rims",
     )
     got = exchanged(*sent)
-    local = shaped((2, 2, MODES, TILE, 128), F32)
     parts = call(
         middle_kernel,
-        [shaped((MODES, TILE, ROWS)), shaped((TILE // 16, 3, 8, 128), F32), local],
+        [shaped((18, TILE, ROWS)), shaped((TILE, TILE, 128)), shaped((TILE, 128), F32)],
         (order_l, order_s, a, p),
         grid=grid,
         in_specs={2: a_spec},
         scratch=[
-            *a_scratch(1),
-            pltpu.VMEM((2, 1, MODES, TILE, 128), F32),
-            pltpu.VMEM((3, MODES, 8, 128), F32),
+            *a_scratch(3),
+            pltpu.VMEM((2, 3, MODES, TILE, 128), F32),
+            pltpu.VMEM((3, 19, 8, 128), F32),
+            pltpu.VMEM((TILE, ROWS), F32),
         ],
         flops=10**9,
         mib=50,
@@ -536,12 +559,14 @@
     s, *sent = call(
         smooth_kernel,
         [shaped((18, TILE, ROWS))] + rims(COLS),
-        (me, order_l, order_s, a, *parts, *got),
-        grid=grid,
-        in_specs={3: a_spec},
-        scratch=[*a_scratch(2), pltpu.VMEM(local.shape, F32), pltpu.VMEM((3, 12, 8, 128), F32)],
+        (me, order_l, order_s, *parts, *got),
+        scratch=[
+            pltpu.VMEM((1, 1, 8, TILE, 128), F32),
+            pltpu.VMEM((1, 1, MODES, TILE, 128), F32),
+            pltpu.VMEM((MODES, TILE, 128), F32),
+        ],
         flops=10**9,
-        mib=50,
+        mib=24,
         name="smooth",
     )
     got = exchanged(*sent)

time: 90 us -> 91 us (1.011)
  Pallas kernels: 37.6 us -> 39.2 us
  starting transfers between devices: 36.4 us -> 35.4 us
    pallas_call x7, Pallas kernels: 37.6 us -> 39.2 us  [call(): pl.pallas_call(kernel, grid=(1,) if grid is None else grid, in_specs=spec...]
    all_to_all x1, starting transfers between devices: 11.9 us -> 10.9 us  [per_device(): lax.all_to_all(packed, 'member', split_axis=0, concat_axis=0, tiled=True)]
  transfers between devices with their start and end apart: 9 -> 9, of which waited for: 2 -> 2; matrix products, arithmetic and copies ran while one was open for 0% -> 0% of each run, Pallas kernels for 33% -> 39%
where the time goes in v6:
time: 91 us; the launch traced here: 90.3 us
  Pallas kernels  39.2 us (43%)
  starting transfers between devices  35.4 us (39%)
  waiting for transfers between devices  13.4 us (15%)
  local copies, waits for them, and re-layouts  1.6 us (2%)
    pallas_call x7, Pallas kernels, call(): pl.pallas_call(kernel, grid=(1,) if grid is None else grid, in_specs=spec...  39.2 us
    ppermute x2, starting transfers between devices, exchanged(): return (far, away, lax.ppermute(near, axes, near_pairs))  12.8 us
    all_to_all x1, starting transfers between devices, per_device(): lax.all_to_all(packed, 'member', split_axis=0, concat_axis=0, tiled=True)  10.9 us
    all_to_all x1, waiting for transfers between devices, per_device(): lax.all_to_all(sums.reshape(MEMBERS, SLOTS, WIDE), 'member', split_axis=0...  10.6 us
    all_to_all x1, starting transfers between devices, per_device(): lax.all_to_all(sums.reshape(MEMBERS, SLOTS, WIDE), 'member', split_axis=0...  7.65 us
    all_to_all x1, waiting for transfers between devices, per_device(): lax.all_to_all(packed, 'member', split_axis=0, concat_axis=0, tiled=True)  2.78 us
    ppermute x2, starting transfers between devices, exchanged(): away = lax.ppermute(away, axes, away_pairs)  1.95 us
  transfers between devices with their start and end apart: 9, of which 2 were waited for; matrix products, arithmetic and copies ran while one was open for 0% of the time, Pallas kernels for 39%

profile of v6, /device:TPU:3, one launch (start us, length us, event | category | flops | bytes accessed | tf_op | source)
XLA Modules:
  0.0 90.3 jit_solution(9263959449042164942)
XLA Ops:
  0.6 0.0 copy-start
  0.6 0.9 %copy-done = bf16[192,6,64]{0,2,1:T(8,128)(2,1)S(1)} copy-done((bf16[192,6,64]{0,2,1:T(8,128)(2,1)S(1)}, bf16[192,6,64]{0,2,1:T(8,128)(2,1)}, u32[]{:S(2)}) %copy-start) | copy-done | bytes 147480
  1.6 0.0 copy-start.1
  1.6 0.7 copy-done.1
  2.2 0.8 rims.1
  3.0 0.7 collective-permute-start
  3.7 1.9 %collective-permute-start.1 = (bf16[192,128]{1,0:T(8,128)(2,1)S(1)}, bf16[192,128]{1,0:T(8,128)(2,1)S(1)}, u32[]{:S(2)}, u32[]{:S(2)}) collective-permute-start(bf16[192,128]{1,0:T(8,128)(2,1)S(1)} %get-tuple-element.30), channel_id=1, source_target_pairs={{1,2},{2,1},{3,4},{4,3},{5,6},{6,5},{7,8},{8,7},{9,10},{10,9},{11,... | collective-permute-start | bytes 147464 | tf_op jit(solution)/shard_map/ppermute | solution.py:530
  5.6 7.9 %collective-permute-start.2 = (bf16[192,128]{1,0:T(8,128)(2,1)S(1)}, bf16[192,128]{1,0:T(8,128)(2,1)S(1)}, u32[]{:S(2)}, u32[]{:S(2)}) collective-permute-start(bf16[192,128]{1,0:T(8,128)(2,1)S(1)} %get-tuple-element.31), channel_id=1, source_target_pairs={{0,1},{1,0},{2,3},{3,2},{4,5},{5,4},{6,7},{7,6},{8,9},{9,8},{10,11... | collective-permute-start | bytes 147464 | tf_op jit(solution)/shard_map/ppermute | solution.py:531
  13.5 9.0 %middle.1 = (bf16[18,64,192]{2,1,0:T(8,128)(2,1)S(1)}, bf16[64,64,128]{2,1,0:T(8,128)(2,1)S(1)}, f32[64,128]{1,0:T(8,128)S(1)}) custom-call(f32[8,256]{1,0:T(8,128)S(1)} %get-tuple-element.23.order_l_ref, f32[192,128]{1,0:T(8,128)S(1)} %get-tuple-element.24.order_s_ref, bf16[3,64,64,192]{3,2,1,0:T(8,128)(2,1)} %bitcast.17, ...), custom_call_target="tpu_custom_call" | custom-call | flops 1000000000 | bytes 6496256 | tf_op jit(solution)/shard_map/middle/pallas_call | solution.py:486
  22.5 0.0 collective-permute-done.far_ref
  22.5 0.0 collective-permute-done.1.away_ref
  22.5 0.0 collective-permute-done.2.near_ref
  22.6 2.1 %smooth.1 = (bf16[18,64,192]{2,1,0:T(8,128)(2,1)S(1)}, bf16[8,1152]{1,0:T(8,128)(2,1)S(1)}, bf16[576,128]{1,0:T(8,128)(2,1)S(1)}, bf16[576,128]{1,0:T(8,128)(2,1)S(1)}) custom-call(s32[1]{0:T(128)} %bitcast.me_ref, f32[8,256]{1,0:T(8,128)S(1)} %get-tuple-element.23.order_l_ref, f32[192,128]{1,0:T(8,128)S(1)} %get-tuple-element.24.order_s_ref, ...), custom_call_target="tpu_custom_call" | custom-call | flops 1000000000 | bytes 2490372 | tf_op jit(solution)/shard_map/smooth/pallas_call | solution.py:486
  24.7 0.0 collective-permute-start.4
  24.7 5.0 %collective-permute-start.5 = (bf16[576,128]{1,0:T(8,128)(2,1)S(1)}, bf16[576,128]{1,0:T(8,128)(2,1)S(1)}, u32[]{:S(2)}, u32[]{:S(2)}) collective-permute-start(bf16[576,128]{1,0:T(8,128)(2,1)S(1)} %get-tuple-element.35), channel_id=1, source_target_pairs={{0,1},{1,0},{2,3},{3,2},{4,5},{5,4},{6,7},{7,6},{8,9},{9,8},{10,11... | collective-permute-start | bytes 442376 | tf_op jit(solution)/shard_map/ppermute | solution.py:531
  29.7 0.7 collective-permute-start.3
  30.3 1.8 %pack.1 = bf16[64,56,128]{2,1,0:T(8,128)(2,1)} custom-call(f32[8,256]{1,0:T(8,128)S(1)} %get-tuple-element.23.order_l_ref, bf16[1152,192]{1,0:T(8,128)(2,1)S(1)} %bitcast.13), custom_call_target="tpu_custom_call" | custom-call | bytes 1368064 | tf_op jit(solution)/shard_map/pack/pallas_call | solution.py:486
  32.1 0.0 collective-permute-done.3.far_ref
  32.1 0.0 collective-permute-done.4.away_ref
  32.1 0.0 collective-permute-done.5.near_ref
  32.1 10.9 %all-to-all-start = ((bf16[64,56,128]{2,1,0:T(8,128)(2,1)}), bf16[64,56,128]{2,1,0:T(8,128)(2,1)S(1)}, u32[]{:S(2)}, u32[]{:S(2)}) async-start(bf16[64,56,128]{2,1,0:T(8,128)(2,1)} %pack.1), calls=%async_computation | async-start | bytes 1835008 | tf_op jit(solution)/shard_map/all_to_all | solution.py:576
  43.0 22.6 %product.1 = (bf16[512,256]{1,0:T(8,128)(2,1)}, f32[8,256]{1,0:T(8,128)S(1)}) custom-call(s32[1]{0:T(128)} %bitcast.me_ref, f32[8,256]{1,0:T(8,128)S(1)} %get-tuple-element.23.order_l_ref, f32[192,128]{1,0:T(8,128)S(1)} %get-tuple-element.24.order_s_ref, bf16[3,64,64,192]{3,2,1,0:T(8,128)(2,1)} %bitcast.18, bf16[1152,192]{1,0:T(8,128)(2,1)S(1)} %bitcast.14, ...), custom_call_target="tpu_custom_call" | custom-call | flops 10000000000 | bytes 5851140 | tf_op jit(solution)/shard_map/product/pallas_call | solution.py:486
  65.7 2.8 %all-to-all-done.recv_ref = bf16[64,56,128]{2,1,0:T(8,128)(2,1)S(1)} async-done(((bf16[64,56,128]{2,1,0:T(8,128)(2,1)}), bf16[64,56,128]{2,1,0:T(8,128)(2,1)S(1)}, u32[]{:S(2)}, u32[]{:S(2)}) %all-to-all-start) | async-done | bytes 917536 | tf_op jit(solution)/shard_map/all_to_all | solution.py:576
  68.5 7.7 %all-to-all-start.1 = ((bf16[64,8,256]{2,1,0:T(8,128)(2,1)}), bf16[64,8,256]{2,1,0:T(8,128)(2,1)S(1)}, u32[]{:S(2)}, u32[]{:S(2)}) async-start(bf16[64,8,256]{2,1,0:T(8,128)(2,1)} %bitcast.8), calls=%async_computation.1 | async-start | bytes 524288 | tf_op jit(solution)/shard_map/all_to_all | solution.py:596
  76.1 0.7 collective-permute-start.6
  76.8 1.9 %unpack_smooth.1 = (bf16[1152,192]{1,0:T(8,128)(2,1)}, bf16[192,512]{1,0:T(8,128)(2,1)S(1)}) custom-call(bf16[64,56,128]{2,1,0:T(8,128)(2,1)S(1)} %all-to-all-done.recv_ref), custom_call_target="tpu_custom_call" | custom-call | flops 1000000000 | bytes 1556480 | tf_op jit(solution)/shard_map/unpack_smooth/pallas_call | solution.py:486
  78.7 0.0 collective-permute-done.6.far_ref
  78.7 10.6 %all-to-all-done.1 = bf16[64,8,256]{2,1,0:T(8,128)(2,1)S(1)} async-done(((bf16[64,8,256]{2,1,0:T(8,128)(2,1)}), bf16[64,8,256]{2,1,0:T(8,128)(2,1)S(1)}, u32[]{:S(2)}, u32[]{:S(2)}) %all-to-all-start.1) | async-done | bytes 262176 | tf_op jit(solution)/shard_map/all_to_all | solution.py:596
  89.3 1.0 %unpack_coarse.1 = f32[192,252]{1,0:T(8,128)} custom-call(s32[1]{0:T(128)} %bitcast.me_ref, bf16[192,512]{1,0:T(8,128)(2,1)S(1)} %get-tuple-element.38.pick_ref, bf16[512,256]{1,0:T(8,128)(2,1)S(1)} %bitcast.12, f32[8,256]{1,0:T(8,128)S(1)} %collective-permute-done.6.far_ref), custom_call_target="tpu_custom_call" | custom-call | bytes 660484 | tf_op jit(solution)/shard_map/unpack_coarse/pallas_call | solution.py:486
Async XLA Ops:
  0.6 0.9 %copy-start = (bf16[192,6,64]{0,2,1:T(8,128)(2,1)S(1)}, bf16[192,6,64]{0,2,1:T(8,128)(2,1)}, u32[]{:S(2)}) copy-start(bf16[192,6,64]{0,2,1:T(8,128)(2,1)} %param.4) | copy-start | bytes 442372
  1.6 0.7 copy-start.1
  3.0 19.5 %collective-permute-start = (bf16[8,384]{1,0:T(8,128)(2,1)S(1)}, bf16[8,384]{1,0:T(8,128)(2,1)S(1)}, u32[]{:S(2)}, u32[]{:S(2)}) collective-permute-start(bf16[8,384]{1,0:T(8,128)(2,1)S(1)} %get-tuple-element.29), channel_id=1, source_target_pairs={{63,64},{64,63},{127,128},{128,127},{191,192},{192,191}} | collective-permute-start | bytes 18440 | tf_op jit(solution)/shard_map/ppermute | solution.py:529
  3.7 18.8 %collective-permute-start.1 = (bf16[192,128]{1,0:T(8,128)(2,1)S(1)}, bf16[192,128]{1,0:T(8,128)(2,1)S(1)}, u32[]{:S(2)}, u32[]{:S(2)}) collective-permute-start(bf16[192,128]{1,0:T(8,128)(2,1)S(1)} %get-tuple-element.30), channel_id=1, source_target_pairs={{1,2},{2,1},{3,4},{4,3},{5,6},{6,5},{7,8},{8,7},{9,10},{10,9},{11,... | collective-permute-start | bytes 147464 | tf_op jit(solution)/shard_map/ppermute | solution.py:530
  5.6 16.9 %collective-permute-start.2 = (bf16[192,128]{1,0:T(8,128)(2,1)S(1)}, bf16[192,128]{1,0:T(8,128)(2,1)S(1)}, u32[]{:S(2)}, u32[]{:S(2)}) collective-permute-start(bf16[192,128]{1,0:T(8,128)(2,1)S(1)} %get-tuple-element.31), channel_id=1, source_target_pairs={{0,1},{1,0},{2,3},{3,2},{4,5},{5,4},{6,7},{7,6},{8,9},{9,8},{10,11... | collective-permute-start | bytes 147464 | tf_op jit(solution)/shard_map/ppermute | solution.py:531
  24.7 7.4 %collective-permute-start.4 = (bf16[576,128]{1,0:T(8,128)(2,1)S(1)}, bf16[576,128]{1,0:T(8,128)(2,1)S(1)}, u32[]{:S(2)}, u32[]{:S(2)}) collective-permute-start(bf16[576,128]{1,0:T(8,128)(2,1)S(1)} %get-tuple-element.34), channel_id=1, source_target_pairs={{1,2},{2,1},{3,4},{4,3},{5,6},{6,5},{7,8},{8,7},{9,10},{10,9},{11,... | collective-permute-start | bytes 442376 | tf_op jit(solution)/shard_map/ppermute | solution.py:530
  24.7 7.4 %collective-permute-start.5 = (bf16[576,128]{1,0:T(8,128)(2,1)S(1)}, bf16[576,128]{1,0:T(8,128)(2,1)S(1)}, u32[]{:S(2)}, u32[]{:S(2)}) collective-permute-start(bf16[576,128]{1,0:T(8,128)(2,1)S(1)} %get-tuple-element.35), channel_id=1, source_target_pairs={{0,1},{1,0},{2,3},{3,2},{4,5},{5,4},{6,7},{7,6},{8,9},{9,8},{10,11... | collective-permute-start | bytes 442376 | tf_op jit(solution)/shard_map/ppermute | solution.py:531
  29.7 2.4 %collective-permute-start.3 = (bf16[8,1152]{1,0:T(8,128)(2,1)S(1)}, bf16[8,1152]{1,0:T(8,128)(2,1)S(1)}, u32[]{:S(2)}, u32[]{:S(2)}) collective-permute-start(bf16[8,1152]{1,0:T(8,128)(2,1)S(1)} %get-tuple-element.33), channel_id=1, source_target_pairs={{63,64},{64,63},{127,128},{128,127},{191,192},{192,191}} | collective-permute-start | bytes 55304 | tf_op jit(solution)/shard_map/ppermute | solution.py:529
  32.1 36.4 %all-to-all-start = ((bf16[64,56,128]{2,1,0:T(8,128)(2,1)}), bf16[64,56,128]{2,1,0:T(8,128)(2,1)S(1)}, u32[]{:S(2)}, u32[]{:S(2)}) async-start(bf16[64,56,128]{2,1,0:T(8,128)(2,1)} %pack.1), calls=%async_computation | async-start | bytes 1835008 | tf_op jit(solution)/shard_map/all_to_all | solution.py:576
  68.5 20.8 %all-to-all-start.1 = ((bf16[64,8,256]{2,1,0:T(8,128)(2,1)}), bf16[64,8,256]{2,1,0:T(8,128)(2,1)S(1)}, u32[]{:S(2)}, u32[]{:S(2)}) async-start(bf16[64,8,256]{2,1,0:T(8,128)(2,1)} %bitcast.8), calls=%async_computation.1 | async-start | bytes 524288 | tf_op jit(solution)/shard_map/all_to_all | solution.py:596
  76.1 2.6 %collective-permute-start.6 = (f32[8,256]{1,0:T(8,128)S(1)}, f32[8,256]{1,0:T(8,128)S(1)}, u32[]{:S(2)}, u32[]{:S(2)}) collective-permute-start(f32[8,256]{1,0:T(8,128)S(1)} %get-tuple-element.43), channel_id=1, source_target_pairs={{63,64},{64,63},{127,128},{128,127},{191,192},{192,191}} | collective-permute-start | bytes 24584 | tf_op jit(solution)/shard_map/ppermute | solution.py:595

commit v7 on v5

--- a/solution.py
+++ b/solution.py
@@ -17,6 +17,7 @@
 NT = (((1,), (1,)), ((), ()))
 TN = (((0,), (0,)), ((), ()))
 MIB = 1024 * 1024
+BACK = 3328
 PACKED = 56
 
 
@@ -198,7 +199,7 @@
     return jnp.concatenate([top, bottom], 0)
 
 
-def first_kernel(me_ref, owner_ref, p_ref, wide_ref, tall_ref, p_out, far_out, away_out, near_out):
+def first_kernel(me_ref, owner_ref, p_ref, wide_ref, tall_ref, p_out, back_out, far_out, away_out, near_out):
     rows, columns = rank_arrays(owner_ref[...])
     p_out[...] = p_ref[...]
     wide_ref[...] = jnp.zeros_like(wide_ref)
@@ -209,6 +210,8 @@
     r = Order(wide_ref, tall_ref)
     for ref, rim in zip((far_out, away_out, near_out), rims_of(p_ref[...], r, me_ref[0])):
         ref[...] = rim
+    back_out[...] = jnp.zeros_like(back_out)
+    back_out[:, : MODES * TILE] = far_out[...]
 
 
 def halves(ib):
@@ -257,7 +260,7 @@
 
 
 def smooth_kernel(
-    me_ref, order_l_ref, order_s_ref, a_hbm, mid_ref, scale_ref, local_ref, far_ref, away_ref, near_ref,
+    me_ref, order_l_ref, order_s_ref, a_hbm, mid_ref, scale_ref, local_ref, on_ref, away_ref, near_ref, back_ref,
     s_ref, far_out, away_out, near_out, a_ref, sems, group_ref, wide_ref, out_ref,
 ):
     ib = pl.program_id(0)
@@ -267,7 +270,7 @@
     def _():
         start_copies(a_hbm, a_ref, sems, (0, 2))
         r = Order(order_l_ref, order_s_ref)
-        for k, value in enumerate(rim_rows(near_ref[...], away_ref[...], far_ref[...], r, me)):
+        for k, value in enumerate(rim_rows(near_ref[...], away_ref[...], on_ref[...] + back_ref[:, : MODES * TILE], r, me)):
             set_wide(wide_ref, k, value)
         wide_ref[...] += local_ref[...]
         s_ref[6:12] = mid_ref[...]
@@ -510,13 +513,18 @@
     def rims(length):
         return [shaped((8, length)), shaped((length // 2, 128)), shaped((length // 2, 128))]
 
-    order_l, order_s, p, *sent = call(
+    order_l, order_s, p, back, *sent = call(
         first_kernel,
-        [shaped((8, WIDE), F32), shaped((ROWS, 128), F32), shaped(p.shape)] + rims(MODES * TILE),
+        [shaped((8, WIDE), F32), shaped((ROWS, 128), F32), shaped(p.shape), shaped((8, BACK))] + rims(MODES * TILE),
         (me, new_owner.reshape(1, ROWS), p),
         name="rims",
     )
-    got = exchanged(*sent)
+    far, away, near = sent
+    on = lax.ppermute(far, axes, across[::2])
+    away = lax.ppermute(away, axes, away_pairs)
+    near = lax.ppermute(near, axes, near_pairs)
+    back = lax.ppermute(back, axes, across[1::2])
+    got = on, away, near, back
     local = shaped((2, 2, MODES, TILE, 128), F32)
     parts = call(
         middle_kernel,

time: 90 us -> 89.8 us (level)
    ppermute x0 -> x4, starting transfers between devices: none -> 10.4 us  [the longest x1 7.19 us: per_device(): near = lax.ppermute(near, axes, near_pairs)]
    ppermute x2 -> x1, starting transfers between devices: 12.8 us -> 5.58 us  [exchanged(): return (far, away, lax.ppermute(near, axes, near_pairs))]
    ppermute x2 -> x1, starting transfers between devices: 2.04 us -> 0.09 us  [exchanged(): away = lax.ppermute(away, axes, away_pairs)]
    all_to_all x1, starting transfers between devices: 11.9 us -> 10.9 us  [per_device(): lax.all_to_all(packed, 'member', split_axis=0, concat_axis=0, tiled=True)]
  transfers between devices with their start and end apart: 9 -> 10, of which waited for: 2 -> 2; matrix products, arithmetic and copies ran while one was open for 0% -> 0% of each run, Pallas kernels for 33% -> 33%
where the time goes in v7:
time: 89.8 us; the launch traced here: 89.4 us
  Pallas kernels  37.6 us (42%)
  starting transfers between devices  36 us (40%)
  waiting for transfers between devices  13.4 us (15%)
  local copies, waits for them, and re-layouts  1.6 us (2%)
    pallas_call x7, Pallas kernels, call(): pl.pallas_call(kernel, grid=(1,) if grid is None else grid, in_specs=spec...  37.6 us
    all_to_all x1, starting transfers between devices, per_device(): lax.all_to_all(packed, 'member', split_axis=0, concat_axis=0, tiled=True)  10.9 us
    all_to_all x1, waiting for transfers between devices, per_device(): lax.all_to_all(sums.reshape(MEMBERS, SLOTS, WIDE), 'member', split_axis=0...  10.6 us
    all_to_all x1, starting transfers between devices, per_device(): lax.all_to_all(sums.reshape(MEMBERS, SLOTS, WIDE), 'member', split_axis=0...  7.66 us
    ppermute x1, starting transfers between devices, per_device(): near = lax.ppermute(near, axes, near_pairs)  7.19 us
    ppermute x1, starting transfers between devices, exchanged(): return (far, away, lax.ppermute(near, axes, near_pairs))  5.58 us
    all_to_all x1, waiting for transfers between devices, per_device(): lax.all_to_all(packed, 'member', split_axis=0, concat_axis=0, tiled=True)  2.78 us
    ppermute x1, starting transfers between devices, per_device(): away = lax.ppermute(away, axes, away_pairs)  1.95 us
  transfers between devices with their start and end apart: 10, of which 2 were waited for; matrix products, arithmetic and copies ran while one was open for 0% of the time, Pallas kernels for 33%

profile of v7, /device:TPU:3, one launch (start us, length us, event | category | flops | bytes accessed | tf_op | source)
XLA Modules:
  0.0 89.4 jit_solution(3003173550317732723)
XLA Ops:
  0.6 0.0 copy-start
  0.6 0.9 %copy-done = bf16[192,6,64]{0,2,1:T(8,128)(2,1)S(1)} copy-done((bf16[192,6,64]{0,2,1:T(8,128)(2,1)S(1)}, bf16[192,6,64]{0,2,1:T(8,128)(2,1)}, u32[]{:S(2)}) %copy-start) | copy-done | bytes 147480
  1.6 0.0 copy-start.1
  1.6 0.7 copy-done.1
  2.2 0.8 rims.1
  3.0 0.7 collective-permute-start
  3.7 1.9 %collective-permute-start.1 = (bf16[192,128]{1,0:T(8,128)(2,1)S(1)}, bf16[192,128]{1,0:T(8,128)(2,1)S(1)}, u32[]{:S(2)}, u32[]{:S(2)}) collective-permute-start(bf16[192,128]{1,0:T(8,128)(2,1)S(1)} %get-tuple-element.31), channel_id=1, source_target_pairs={{1,2},{2,1},{3,4},{4,3},{5,6},{6,5},{7,8},{8,7},{9,10},{10,9},{11,... | collective-permute-start | bytes 147464 | tf_op jit(solution)/shard_map/ppermute | solution.py:524
  5.6 7.2 %collective-permute-start.2 = (bf16[192,128]{1,0:T(8,128)(2,1)S(1)}, bf16[192,128]{1,0:T(8,128)(2,1)S(1)}, u32[]{:S(2)}, u32[]{:S(2)}) collective-permute-start(bf16[192,128]{1,0:T(8,128)(2,1)S(1)} %get-tuple-element.32), channel_id=1, source_target_pairs={{0,1},{1,0},{2,3},{3,2},{4,5},{5,4},{6,7},{7,6},{8,9},{9,8},{10,11... | collective-permute-start | bytes 147464 | tf_op jit(solution)/shard_map/ppermute | solution.py:525
  12.8 0.7 collective-permute-start.3
  13.5 3.6 %middle.1 = (bf16[6,64,192]{2,1,0:T(8,128)(2,1)S(1)}, f32[4,3,8,128]{3,2,1,0:T(8,128)S(1)}, f32[2,2,6,64,128]{4,3,2,1,0:T(8,128)S(1)}) custom-call(f32[8,256]{1,0:T(8,128)S(1)} %get-tuple-element.24.order_l_ref, f32[192,128]{1,0:T(8,128)S(1)} %get-tuple-element.25.order_s_ref, bf16[3,64,64,192]{3,2,1,0:T(8,128)(2,1)} %bitcast.17, ...), custom_call_target="tpu_custom_call" | custom-call | flops 1000000000 | bytes 5955584 | tf_op jit(solution)/shard_map/middle/pallas_call | solution.py:466
  17.1 0.0 collective-permute-done.on_ref
  17.1 0.0 collective-permute-done.1.away_ref
  17.1 0.0 collective-permute-done.2.near_ref
  17.1 0.0 collective-permute-done.3.back_ref
  17.1 6.0 %smooth.1 = (bf16[18,64,192]{2,1,0:T(8,128)(2,1)S(1)}, bf16[8,1152]{1,0:T(8,128)(2,1)S(1)}, bf16[576,128]{1,0:T(8,128)(2,1)S(1)}, bf16[576,128]{1,0:T(8,128)(2,1)S(1)}) custom-call(s32[1]{0:T(128)} %bitcast.me_ref, f32[8,256]{1,0:T(8,128)S(1)} %get-tuple-element.24.order_l_ref, f32[192,128]{1,0:T(8,128)S(1)} %get-tuple-element.25.order_s_ref, ...), custom_call_target="tpu_custom_call" | custom-call | flops 1000000000 | bytes 6721540 | tf_op jit(solution)/shard_map/smooth/pallas_call | solution.py:466
  23.1 0.1 collective-permute-start.5
  23.2 5.6 %collective-permute-start.6 = (bf16[576,128]{1,0:T(8,128)(2,1)S(1)}, bf16[576,128]{1,0:T(8,128)(2,1)S(1)}, u32[]{:S(2)}, u32[]{:S(2)}) collective-permute-start(bf16[576,128]{1,0:T(8,128)(2,1)S(1)} %get-tuple-element.37), channel_id=1, source_target_pairs={{0,1},{1,0},{2,3},{3,2},{4,5},{5,4},{6,7},{7,6},{8,9},{9,8},{10,11... | collective-permute-start | bytes 442376 | tf_op jit(solution)/shard_map/ppermute | solution.py:511
  28.7 0.7 collective-permute-start.4
  29.4 1.8 %pack.1 = bf16[64,56,128]{2,1,0:T(8,128)(2,1)} custom-call(f32[8,256]{1,0:T(8,128)S(1)} %get-tuple-element.24.order_l_ref, bf16[1152,192]{1,0:T(8,128)(2,1)S(1)} %bitcast.13), custom_call_target="tpu_custom_call" | custom-call | bytes 1368064 | tf_op jit(solution)/shard_map/pack/pallas_call | solution.py:466
  31.2 0.0 collective-permute-done.4.far_ref
  31.2 0.0 collective-permute-done.5.away_ref
  31.2 0.0 collective-permute-done.6.near_ref
  31.2 10.9 %all-to-all-start = ((bf16[64,56,128]{2,1,0:T(8,128)(2,1)}), bf16[64,56,128]{2,1,0:T(8,128)(2,1)S(1)}, u32[]{:S(2)}, u32[]{:S(2)}) async-start(bf16[64,56,128]{2,1,0:T(8,128)(2,1)} %pack.1), calls=%async_computation | async-start | bytes 1835008 | tf_op jit(solution)/shard_map/all_to_all | solution.py:559
  42.1 22.6 %product.1 = (bf16[512,256]{1,0:T(8,128)(2,1)}, f32[8,256]{1,0:T(8,128)S(1)}) custom-call(s32[1]{0:T(128)} %bitcast.me_ref, f32[8,256]{1,0:T(8,128)S(1)} %get-tuple-element.24.order_l_ref, f32[192,128]{1,0:T(8,128)S(1)} %get-tuple-element.25.order_s_ref, bf16[3,64,64,192]{3,2,1,0:T(8,128)(2,1)} %bitcast.19, bf16[1152,192]{1,0:T(8,128)(2,1)S(1)} %bitcast.14, ...), custom_call_target="tpu_custom_call" | custom-call | flops 10000000000 | bytes 5851140 | tf_op jit(solution)/shard_map/product/pallas_call | solution.py:466
  64.8 2.8 %all-to-all-done.recv_ref = bf16[64,56,128]{2,1,0:T(8,128)(2,1)S(1)} async-done(((bf16[64,56,128]{2,1,0:T(8,128)(2,1)}), bf16[64,56,128]{2,1,0:T(8,128)(2,1)S(1)}, u32[]{:S(2)}, u32[]{:S(2)}) %all-to-all-start) | async-done | bytes 917536 | tf_op jit(solution)/shard_map/all_to_all | solution.py:559
  67.5 7.7 %all-to-all-start.1 = ((bf16[64,8,256]{2,1,0:T(8,128)(2,1)}), bf16[64,8,256]{2,1,0:T(8,128)(2,1)S(1)}, u32[]{:S(2)}, u32[]{:S(2)}) async-start(bf16[64,8,256]{2,1,0:T(8,128)(2,1)} %bitcast.8), calls=%async_computation.1 | async-start | bytes 524288 | tf_op jit(solution)/shard_map/all_to_all | solution.py:579
  75.2 0.7 collective-permute-start.7
  75.9 1.9 %unpack_smooth.1 = (bf16[1152,192]{1,0:T(8,128)(2,1)}, bf16[192,512]{1,0:T(8,128)(2,1)S(1)}) custom-call(bf16[64,56,128]{2,1,0:T(8,128)(2,1)S(1)} %all-to-all-done.recv_ref), custom_call_target="tpu_custom_call" | custom-call | flops 1000000000 | bytes 1556480 | tf_op jit(solution)/shard_map/unpack_smooth/pallas_call | solution.py:466
  77.8 0.0 collective-permute-done.7.far_ref
  77.8 10.6 %all-to-all-done.1 = bf16[64,8,256]{2,1,0:T(8,128)(2,1)S(1)} async-done(((bf16[64,8,256]{2,1,0:T(8,128)(2,1)}), bf16[64,8,256]{2,1,0:T(8,128)(2,1)S(1)}, u32[]{:S(2)}, u32[]{:S(2)}) %all-to-all-start.1) | async-done | bytes 262176 | tf_op jit(solution)/shard_map/all_to_all | solution.py:579
  88.4 1.0 %unpack_coarse.1 = f32[192,252]{1,0:T(8,128)} custom-call(s32[1]{0:T(128)} %bitcast.me_ref, bf16[192,512]{1,0:T(8,128)(2,1)S(1)} %get-tuple-element.40.pick_ref, bf16[512,256]{1,0:T(8,128)(2,1)S(1)} %bitcast.12, f32[8,256]{1,0:T(8,128)S(1)} %collective-permute-done.7.far_ref), custom_call_target="tpu_custom_call" | custom-call | bytes 660484 | tf_op jit(solution)/shard_map/unpack_coarse/pallas_call | solution.py:466
Async XLA Ops:
  0.6 0.9 %copy-start = (bf16[192,6,64]{0,2,1:T(8,128)(2,1)S(1)}, bf16[192,6,64]{0,2,1:T(8,128)(2,1)}, u32[]{:S(2)}) copy-start(bf16[192,6,64]{0,2,1:T(8,128)(2,1)} %param.4) | copy-start | bytes 442372
  1.6 0.7 copy-start.1
  3.0 14.0 %collective-permute-start = (bf16[8,384]{1,0:T(8,128)(2,1)S(1)}, bf16[8,384]{1,0:T(8,128)(2,1)S(1)}, u32[]{:S(2)}, u32[]{:S(2)}) collective-permute-start(bf16[8,384]{1,0:T(8,128)(2,1)S(1)} %get-tuple-element.30), channel_id=1, source_target_pairs={{63,64},{127,128},{191,192}} | collective-permute-start | bytes 18440 | tf_op jit(solution)/shard_map/ppermute | solution.py:523
  3.7 13.4 %collective-permute-start.1 = (bf16[192,128]{1,0:T(8,128)(2,1)S(1)}, bf16[192,128]{1,0:T(8,128)(2,1)S(1)}, u32[]{:S(2)}, u32[]{:S(2)}) collective-permute-start(bf16[192,128]{1,0:T(8,128)(2,1)S(1)} %get-tuple-element.31), channel_id=1, source_target_pairs={{1,2},{2,1},{3,4},{4,3},{5,6},{6,5},{7,8},{8,7},{9,10},{10,9},{11,... | collective-permute-start | bytes 147464 | tf_op jit(solution)/shard_map/ppermute | solution.py:524
  5.6 11.4 %collective-permute-start.2 = (bf16[192,128]{1,0:T(8,128)(2,1)S(1)}, bf16[192,128]{1,0:T(8,128)(2,1)S(1)}, u32[]{:S(2)}, u32[]{:S(2)}) collective-permute-start(bf16[192,128]{1,0:T(8,128)(2,1)S(1)} %get-tuple-element.32), channel_id=1, source_target_pairs={{0,1},{1,0},{2,3},{3,2},{4,5},{5,4},{6,7},{7,6},{8,9},{9,8},{10,11... | collective-permute-start | bytes 147464 | tf_op jit(solution)/shard_map/ppermute | solution.py:525
  12.8 4.3 %collective-permute-start.3 = (bf16[8,3328]{1,0:T(8,128)(2,1)S(1)}, bf16[8,3328]{1,0:T(8,128)(2,1)S(1)}, u32[]{:S(2)}, u32[]{:S(2)}) collective-permute-start(bf16[8,3328]{1,0:T(8,128)(2,1)S(1)} %get-tuple-element.33), channel_id=1, source_target_pairs={{64,63},{128,127},{192,191}} | collective-permute-start | bytes 159752 | tf_op jit(solution)/shard_map/ppermute | solution.py:526
  23.1 8.1 %collective-permute-start.5 = (bf16[576,128]{1,0:T(8,128)(2,1)S(1)}, bf16[576,128]{1,0:T(8,128)(2,1)S(1)}, u32[]{:S(2)}, u32[]{:S(2)}) collective-permute-start(bf16[576,128]{1,0:T(8,128)(2,1)S(1)} %get-tuple-element.36), channel_id=1, source_target_pairs={{1,2},{2,1},{3,4},{4,3},{5,6},{6,5},{7,8},{8,7},{9,10},{10,9},{11,... | collective-permute-start | bytes 442376 | tf_op jit(solution)/shard_map/ppermute | solution.py:510
  23.2 8.0 %collective-permute-start.6 = (bf16[576,128]{1,0:T(8,128)(2,1)S(1)}, bf16[576,128]{1,0:T(8,128)(2,1)S(1)}, u32[]{:S(2)}, u32[]{:S(2)}) collective-permute-start(bf16[576,128]{1,0:T(8,128)(2,1)S(1)} %get-tuple-element.37), channel_id=1, source_target_pairs={{0,1},{1,0},{2,3},{3,2},{4,5},{5,4},{6,7},{7,6},{8,9},{9,8},{10,11... | collective-permute-start | bytes 442376 | tf_op jit(solution)/shard_map/ppermute | solution.py:511
  28.7 2.4 %collective-permute-start.4 = (bf16[8,1152]{1,0:T(8,128)(2,1)S(1)}, bf16[8,1152]{1,0:T(8,128)(2,1)S(1)}, u32[]{:S(2)}, u32[]{:S(2)}) collective-permute-start(bf16[8,1152]{1,0:T(8,128)(2,1)S(1)} %get-tuple-element.35), channel_id=1, source_target_pairs={{63,64},{64,63},{127,128},{128,127},{191,192},{192,191}} | collective-permute-start | bytes 55304 | tf_op jit(solution)/shard_map/ppermute | solution.py:509
  31.2 36.3 %all-to-all-start = ((bf16[64,56,128]{2,1,0:T(8,128)(2,1)}), bf16[64,56,128]{2,1,0:T(8,128)(2,1)S(1)}, u32[]{:S(2)}, u32[]{:S(2)}) async-start(bf16[64,56,128]{2,1,0:T(8,128)(2,1)} %pack.1), calls=%async_computation | async-start | bytes 1835008 | tf_op jit(solution)/shard_map/all_to_all | solution.py:559
  67.5 20.8 %all-to-all-start.1 = ((bf16[64,8,256]{2,1,0:T(8,128)(2,1)}), bf16[64,8,256]{2,1,0:T(8,128)(2,1)S(1)}, u32[]{:S(2)}, u32[]{:S(2)}) async-start(bf16[64,8,256]{2,1,0:T(8,128)(2,1)} %bitcast.8), calls=%async_computation.1 | async-start | bytes 524288 | tf_op jit(solution)/shard_map/all_to_all | solution.py:579
  75.2 2.6 %collective-permute-start.7 = (f32[8,256]{1,0:T(8,128)S(1)}, f32[8,256]{1,0:T(8,128)S(1)}, u32[]{:S(2)}, u32[]{:S(2)}) collective-permute-start(f32[8,256]{1,0:T(8,128)S(1)} %get-tuple-element.45), channel_id=1, source_target_pairs={{63,64},{64,63},{127,128},{128,127},{191,192},{192,191}} | collective-permute-start | bytes 24584 | tf_op jit(solution)/shard_map/ppermute | solution.py:578

commit v8 on v7

--- a/solution.py
+++ b/solution.py
@@ -159,7 +159,11 @@
 def next_groups(a_hbm, a_ref, sems, planes, ib, group_ref):
     for copy in chunk_copies(a_hbm, a_ref, sems, planes, ib):
         copy.wait()
-    for k in range(len(planes)):
+    set_groups(a_ref, ib, group_ref)
+
+
+def set_groups(a_ref, ib, group_ref):
+    for k in range(a_ref.shape[0]):
         for i in range(8):
             low, high = (a_ref[k, 16 * ib + i + n].astype(F32) for n in (0, 8))
             group_ref[0, k, i] = low[:, :128]
@@ -219,14 +223,16 @@
 
 
 def middle_kernel(
-    order_l_ref, order_s_ref, a_hbm, p_ref, mid_ref, scale_ref, local_ref,
-    a_ref, sems, group_ref, wide_ref, out_ref,
+    order_l_ref, order_s_ref, a_hbm, p_ref, mid_ref, scale_ref, local_ref, outer_ref,
+    a_ref, sems, outer_sem, group_ref, wide_ref, out_ref,
 ):
     ib = pl.program_id(0)
 
     @pl.when(ib == 0)
     def _():
         start_copies(a_hbm, a_ref, sems, (1,))
+        for at in range(2):
+            pltpu.make_async_copy(a_hbm.at[2 * at], outer_ref.at[at], outer_sem.at[at]).start()
         before, here, after = local_rows(p_ref[...], Order(order_l_ref, order_s_ref))
         set_wide(wide_ref, 0, here)
         set_wide(local_ref, 0, before)
@@ -253,29 +259,33 @@
                 out_ref[g, c] = own - scale * total
         return carry
 
-    lax.fori_loop(0, 3, one_group, 0)
+    lax.fori_loop(0, 3, one_group, 0, unroll=True)
     rows = pl.ds(pl.multiple_of(16 * ib, 16), 16)
     for index in range(6):
         mid_ref[index, rows, :] = ungrouped(out_ref, index).astype(BF16)
 
+    @pl.when(ib == pl.num_programs(0) - 1)
+    def _():
+        for at in range(2):
+            pltpu.make_async_copy(a_hbm.at[2 * at], outer_ref.at[at], outer_sem.at[at]).wait()
+
 
 def smooth_kernel(
-    me_ref, order_l_ref, order_s_ref, a_hbm, mid_ref, scale_ref, local_ref, on_ref, away_ref, near_ref, back_ref,
-    s_ref, far_out, away_out, near_out, a_ref, sems, group_ref, wide_ref, out_ref,
+    me_ref, order_l_ref, order_s_ref, mid_ref, scale_ref, local_ref, outer_ref, on_ref, away_ref, near_ref, back_ref,
+    s_ref, far_out, away_out, near_out, group_ref, wide_ref, out_ref,
 ):
     ib = pl.program_id(0)
     me = me_ref[0]
 
     @pl.when(ib == 0)
     def _():
-        start_copies(a_hbm, a_ref, sems, (0, 2))
         r = Order(order_l_ref, order_s_ref)
         for k, value in enumerate(rim_rows(near_ref[...], away_ref[...], on_ref[...] + back_ref[:, : MODES * TILE], r, me)):
             set_wide(wide_ref, k, value)
         wide_ref[...] += local_ref[...]
         s_ref[6:12] = mid_ref[...]
 
-    next_groups(a_hbm, a_ref, sems, (0, 2), ib, group_ref)
+    set_groups(outer_ref, ib, group_ref)
 
     def one_group(g, carry):
         tile = jnp.where(g == 2, 1, 0)
@@ -288,7 +298,7 @@
                     out_ref[g, 6 * k + c] = scale * total
         return carry
 
-    lax.fori_loop(0, 3, one_group, 0)
+    lax.fori_loop(0, 3, one_group, 0, unroll=True)
     rows = pl.ds(pl.multiple_of(16 * ib, 16), 16)
     for index in range(12):
         s_ref[index if index < 6 else index + 6, rows, :] = ungrouped(out_ref, index).astype(BF16)
@@ -454,7 +464,7 @@
     out_ref[...] = total[:, :252]
 
 
-def call(kernel, outs, args, grid=None, in_specs=None, scratch=(), flops=0, mib=16, name=None):
+def call(kernel, outs, args, grid=None, in_specs=None, out_specs=None, scratch=(), flops=0, mib=16, name=None):
     whole = lambda shape: pl.BlockSpec(shape, lambda *_: (0,) * len(shape))
     specs = []
     for n, arg in enumerate(args):
@@ -467,7 +477,7 @@
         kernel,
         grid=(1,) if grid is None else grid,
         in_specs=specs,
-        out_specs=[whole(o.shape) for o in outs],
+        out_specs=[(out_specs or {}).get(n, whole(o.shape)) for n, o in enumerate(outs)],
         out_shape=outs,
         scratch_shapes=list(scratch),
         compiler_params=pltpu.CompilerParams(vmem_limit_bytes=mib * MIB),
@@ -528,28 +538,31 @@
     local = shaped((2, 2, MODES, TILE, 128), F32)
     parts = call(
         middle_kernel,
-        [shaped((MODES, TILE, ROWS)), shaped((TILE // 16, 3, 8, 128), F32), local],
+        [shaped((MODES, TILE, ROWS)), shaped((TILE // 16, 3, 8, 128), F32), local, shaped((2, TILE, TILE, ROWS))],
         (order_l, order_s, a, p),
         grid=grid,
         in_specs={2: a_spec},
+        out_specs={3: pl.BlockSpec(memory_space=pltpu.VMEM)},
         scratch=[
-            *a_scratch(1),
+            *a_scratch(1)[:2],
+            pltpu.SemaphoreType.DMA((2,)),
+            *a_scratch(1)[2:],
             pltpu.VMEM((2, 1, MODES, TILE, 128), F32),
             pltpu.VMEM((3, MODES, 8, 128), F32),
         ],
         flops=10**9,
-        mib=50,
+        mib=46,
         name="middle",
     )
     s, *sent = call(
         smooth_kernel,
         [shaped((18, TILE, ROWS))] + rims(COLS),
-        (me, order_l, order_s, a, *parts, *got),
+        (me, order_l, order_s, *parts, *got),
         grid=grid,
-        in_specs={3: a_spec},
-        scratch=[*a_scratch(2), pltpu.VMEM(local.shape, F32), pltpu.VMEM((3, 12, 8, 128), F32)],
+        in_specs={6: pl.BlockSpec(memory_space=pltpu.VMEM)},
+        scratch=[a_scratch(2)[2], pltpu.VMEM(local.shape, F32), pltpu.VMEM((3, 12, 8, 128), F32)],
         flops=10**9,
-        mib=50,
+        mib=46,
         name="smooth",
     )
     got = exchanged(*sent)

time: 89.8 us -> 88.8 us (0.989)
  Pallas kernels: 37.6 us -> 36.2 us
    pallas_call x7, Pallas kernels: 37.6 us -> 36.2 us  [call(): pl.pallas_call(kernel, grid=(1,) if grid is None else grid, in_specs=spec...]
where the time goes in v8:
time: 88.8 us; the launch traced here: 88.5 us
  starting transfers between devices  36.5 us (41%)
  Pallas kernels  36.2 us (41%)
  waiting for transfers between devices  13.4 us (15%)
  local copies, waits for them, and re-layouts  1.6 us (2%)
    pallas_call x7, Pallas kernels, call(): pl.pallas_call(kernel, grid=(1,) if grid is None else grid, in_specs=spec...  36.2 us
    all_to_all x1, starting transfers between devices, per_device(): lax.all_to_all(packed, 'member', split_axis=0, concat_axis=0, tiled=True)  10.9 us
    all_to_all x1, waiting for transfers between devices, per_device(): lax.all_to_all(sums.reshape(MEMBERS, SLOTS, WIDE), 'member', split_axis=0...  10.6 us
    all_to_all x1, starting transfers between devices, per_device(): lax.all_to_all(sums.reshape(MEMBERS, SLOTS, WIDE), 'member', split_axis=0...  7.66 us
    ppermute x1, starting transfers between devices, per_device(): near = lax.ppermute(near, axes, near_pairs)  7.19 us
    ppermute x1, starting transfers between devices, exchanged(): return (far, away, lax.ppermute(near, axes, near_pairs))  6.12 us
    all_to_all x1, waiting for transfers between devices, per_device(): lax.all_to_all(packed, 'member', split_axis=0, concat_axis=0, tiled=True)  2.78 us
    ppermute x1, starting transfers between devices, per_device(): away = lax.ppermute(away, axes, away_pairs)  1.95 us
  transfers between devices with their start and end apart: 10, of which 2 were waited for; matrix products, arithmetic and copies ran while one was open for 0% of the time, Pallas kernels for 33%

profile of v8, /device:TPU:3, one launch (start us, length us, event | category | flops | bytes accessed | tf_op | source)
XLA Modules:
  0.0 88.5 jit_solution(2971257820427211432)
XLA Ops:
  0.6 0.0 copy-start
  0.6 0.9 %copy-done = bf16[192,6,64]{0,2,1:T(8,128)(2,1)S(1)} copy-done((bf16[192,6,64]{0,2,1:T(8,128)(2,1)S(1)}, bf16[192,6,64]{0,2,1:T(8,128)(2,1)}, u32[]{:S(2)}) %copy-start) | copy-done | bytes 147480
  1.6 0.0 copy-start.1
  1.6 0.7 copy-done.1
  2.2 0.8 rims.1
  3.0 0.7 collective-permute-start
  3.7 1.9 %collective-permute-start.1 = (bf16[192,128]{1,0:T(8,128)(2,1)S(1)}, bf16[192,128]{1,0:T(8,128)(2,1)S(1)}, u32[]{:S(2)}, u32[]{:S(2)}) collective-permute-start(bf16[192,128]{1,0:T(8,128)(2,1)S(1)} %get-tuple-element.33), channel_id=1, source_target_pairs={{1,2},{2,1},{3,4},{4,3},{5,6},{6,5},{7,8},{8,7},{9,10},{10,9},{11,... | collective-permute-start | bytes 147464 | tf_op jit(solution)/shard_map/ppermute | solution.py:534
  5.6 7.2 %collective-permute-start.2 = (bf16[192,128]{1,0:T(8,128)(2,1)S(1)}, bf16[192,128]{1,0:T(8,128)(2,1)S(1)}, u32[]{:S(2)}, u32[]{:S(2)}) collective-permute-start(bf16[192,128]{1,0:T(8,128)(2,1)S(1)} %get-tuple-element.34), channel_id=1, source_target_pairs={{0,1},{1,0},{2,3},{3,2},{4,5},{5,4},{6,7},{7,6},{8,9},{9,8},{10,11... | collective-permute-start | bytes 147464 | tf_op jit(solution)/shard_map/ppermute | solution.py:535
  12.8 0.7 collective-permute-start.3
  13.5 3.0 %middle.1 = (bf16[6,64,192]{2,1,0:T(8,128)(2,1)S(1)}, f32[4,3,8,128]{3,2,1,0:T(8,128)S(1)}, f32[2,2,6,64,128]{4,3,2,1,0:T(8,128)S(1)}, bf16[2,64,64,192]{3,2,1,0:T(8,128)(2,1)S(1)}) custom-call(f32[8,256]{1,0:T(8,128)S(1)} %get-tuple-element.25.order_l_ref, f32[192,128]{1,0:T(8,128)S(1)} %get-tuple-element.26.order_s_ref, bf16[3,64,64,192]{3,2,1,0:T(8,128)(2,1)} %bitcast.17, ...), custom_call_target="tpu_custom_call" | custom-call | flops 1000000000 | bytes 9101312 | tf_op jit(solution)/shard_map/middle/pallas_call | solution.py:476
  16.5 0.0 collective-permute-done.on_ref
  16.5 0.0 collective-permute-done.1.away_ref
  16.5 0.0 collective-permute-done.2.near_ref
  16.6 0.0 collective-permute-done.3.back_ref
  16.6 5.1 %smooth.1 = (bf16[18,64,192]{2,1,0:T(8,128)(2,1)S(1)}, bf16[8,1152]{1,0:T(8,128)(2,1)S(1)}, bf16[576,128]{1,0:T(8,128)(2,1)S(1)}, bf16[576,128]{1,0:T(8,128)(2,1)S(1)}) custom-call(s32[1]{0:T(128)} %bitcast.me_ref, f32[8,256]{1,0:T(8,128)S(1)} %get-tuple-element.25.order_l_ref, f32[192,128]{1,0:T(8,128)S(1)} %get-tuple-element.26.order_s_ref, ...), custom_call_target="tpu_custom_call" | custom-call | flops 1000000000 | bytes 5148676 | tf_op jit(solution)/shard_map/smooth/pallas_call | solution.py:476
  21.7 0.0 collective-permute-start.5
  21.7 6.1 %collective-permute-start.6 = (bf16[576,128]{1,0:T(8,128)(2,1)S(1)}, bf16[576,128]{1,0:T(8,128)(2,1)S(1)}, u32[]{:S(2)}, u32[]{:S(2)}) collective-permute-start(bf16[576,128]{1,0:T(8,128)(2,1)S(1)} %get-tuple-element.39), channel_id=1, source_target_pairs={{0,1},{1,0},{2,3},{3,2},{4,5},{5,4},{6,7},{7,6},{8,9},{9,8},{10,11... | collective-permute-start | bytes 442376 | tf_op jit(solution)/shard_map/ppermute | solution.py:521
  27.8 0.7 collective-permute-start.4
  28.5 1.8 %pack.1 = bf16[64,56,128]{2,1,0:T(8,128)(2,1)} custom-call(f32[8,256]{1,0:T(8,128)S(1)} %get-tuple-element.25.order_l_ref, bf16[1152,192]{1,0:T(8,128)(2,1)S(1)} %bitcast.13), custom_call_target="tpu_custom_call" | custom-call | bytes 1368064 | tf_op jit(solution)/shard_map/pack/pallas_call | solution.py:476
  30.2 0.0 collective-permute-done.4.far_ref
  30.3 0.0 collective-permute-done.5.away_ref
  30.3 0.0 collective-permute-done.6.near_ref
  30.3 10.9 %all-to-all-start = ((bf16[64,56,128]{2,1,0:T(8,128)(2,1)}), bf16[64,56,128]{2,1,0:T(8,128)(2,1)S(1)}, u32[]{:S(2)}, u32[]{:S(2)}) async-start(bf16[64,56,128]{2,1,0:T(8,128)(2,1)} %pack.1), calls=%async_computation | async-start | bytes 1835008 | tf_op jit(solution)/shard_map/all_to_all | solution.py:572
  41.2 22.6 %product.1 = (bf16[512,256]{1,0:T(8,128)(2,1)}, f32[8,256]{1,0:T(8,128)S(1)}) custom-call(s32[1]{0:T(128)} %bitcast.me_ref, f32[8,256]{1,0:T(8,128)S(1)} %get-tuple-element.25.order_l_ref, f32[192,128]{1,0:T(8,128)S(1)} %get-tuple-element.26.order_s_ref, bf16[3,64,64,192]{3,2,1,0:T(8,128)(2,1)} %bitcast.18, bf16[1152,192]{1,0:T(8,128)(2,1)S(1)} %bitcast.14, ...), custom_call_target="tpu_custom_call" | custom-call | flops 10000000000 | bytes 5851140 | tf_op jit(solution)/shard_map/product/pallas_call | solution.py:476
  63.8 2.8 %all-to-all-done.recv_ref = bf16[64,56,128]{2,1,0:T(8,128)(2,1)S(1)} async-done(((bf16[64,56,128]{2,1,0:T(8,128)(2,1)}), bf16[64,56,128]{2,1,0:T(8,128)(2,1)S(1)}, u32[]{:S(2)}, u32[]{:S(2)}) %all-to-all-start) | async-done | bytes 917536 | tf_op jit(solution)/shard_map/all_to_all | solution.py:572
  66.6 7.7 %all-to-all-start.1 = ((bf16[64,8,256]{2,1,0:T(8,128)(2,1)}), bf16[64,8,256]{2,1,0:T(8,128)(2,1)S(1)}, u32[]{:S(2)}, u32[]{:S(2)}) async-start(bf16[64,8,256]{2,1,0:T(8,128)(2,1)} %bitcast.8), calls=%async_computation.1 | async-start | bytes 524288 | tf_op jit(solution)/shard_map/all_to_all | solution.py:592
  74.3 0.7 collective-permute-start.7
  74.9 1.9 %unpack_smooth.1 = (bf16[1152,192]{1,0:T(8,128)(2,1)}, bf16[192,512]{1,0:T(8,128)(2,1)S(1)}) custom-call(bf16[64,56,128]{2,1,0:T(8,128)(2,1)S(1)} %all-to-all-done.recv_ref), custom_call_target="tpu_custom_call" | custom-call | flops 1000000000 | bytes 1556480 | tf_op jit(solution)/shard_map/unpack_smooth/pallas_call | solution.py:476
  76.8 0.0 collective-permute-done.7.far_ref
  76.8 10.6 %all-to-all-done.1 = bf16[64,8,256]{2,1,0:T(8,128)(2,1)S(1)} async-done(((bf16[64,8,256]{2,1,0:T(8,128)(2,1)}), bf16[64,8,256]{2,1,0:T(8,128)(2,1)S(1)}, u32[]{:S(2)}, u32[]{:S(2)}) %all-to-all-start.1) | async-done | bytes 262176 | tf_op jit(solution)/shard_map/all_to_all | solution.py:592
  87.4 1.0 %unpack_coarse.1 = f32[192,252]{1,0:T(8,128)} custom-call(s32[1]{0:T(128)} %bitcast.me_ref, bf16[192,512]{1,0:T(8,128)(2,1)S(1)} %get-tuple-element.42.pick_ref, bf16[512,256]{1,0:T(8,128)(2,1)S(1)} %bitcast.12, f32[8,256]{1,0:T(8,128)S(1)} %collective-permute-done.7.far_ref), custom_call_target="tpu_custom_call" | custom-call | bytes 660484 | tf_op jit(solution)/shard_map/unpack_coarse/pallas_call | solution.py:476
Async XLA Ops:
  0.6 0.9 %copy-start = (bf16[192,6,64]{0,2,1:T(8,128)(2,1)S(1)}, bf16[192,6,64]{0,2,1:T(8,128)(2,1)}, u32[]{:S(2)}) copy-start(bf16[192,6,64]{0,2,1:T(8,128)(2,1)} %param.4) | copy-start | bytes 442372
  1.6 0.7 copy-start.1
  3.0 13.5 %collective-permute-start = (bf16[8,384]{1,0:T(8,128)(2,1)S(1)}, bf16[8,384]{1,0:T(8,128)(2,1)S(1)}, u32[]{:S(2)}, u32[]{:S(2)}) collective-permute-start(bf16[8,384]{1,0:T(8,128)(2,1)S(1)} %get-tuple-element.32), channel_id=1, source_target_pairs={{63,64},{127,128},{191,192}} | collective-permute-start | bytes 18440 | tf_op jit(solution)/shard_map/ppermute | solution.py:533
  3.7 12.8 %collective-permute-start.1 = (bf16[192,128]{1,0:T(8,128)(2,1)S(1)}, bf16[192,128]{1,0:T(8,128)(2,1)S(1)}, u32[]{:S(2)}, u32[]{:S(2)}) collective-permute-start(bf16[192,128]{1,0:T(8,128)(2,1)S(1)} %get-tuple-element.33), channel_id=1, source_target_pairs={{1,2},{2,1},{3,4},{4,3},{5,6},{6,5},{7,8},{8,7},{9,10},{10,9},{11,... | collective-permute-start | bytes 147464 | tf_op jit(solution)/shard_map/ppermute | solution.py:534
  5.6 10.9 %collective-permute-start.2 = (bf16[192,128]{1,0:T(8,128)(2,1)S(1)}, bf16[192,128]{1,0:T(8,128)(2,1)S(1)}, u32[]{:S(2)}, u32[]{:S(2)}) collective-permute-start(bf16[192,128]{1,0:T(8,128)(2,1)S(1)} %get-tuple-element.34), channel_id=1, source_target_pairs={{0,1},{1,0},{2,3},{3,2},{4,5},{5,4},{6,7},{7,6},{8,9},{9,8},{10,11... | collective-permute-start | bytes 147464 | tf_op jit(solution)/shard_map/ppermute | solution.py:535
  12.8 3.7 %collective-permute-start.3 = (bf16[8,3328]{1,0:T(8,128)(2,1)S(1)}, bf16[8,3328]{1,0:T(8,128)(2,1)S(1)}, u32[]{:S(2)}, u32[]{:S(2)}) collective-permute-start(bf16[8,3328]{1,0:T(8,128)(2,1)S(1)} %get-tuple-element.35), channel_id=1, source_target_pairs={{64,63},{128,127},{192,191}} | collective-permute-start | bytes 159752 | tf_op jit(solution)/shard_map/ppermute | solution.py:536
  21.7 8.6 %collective-permute-start.5 = (bf16[576,128]{1,0:T(8,128)(2,1)S(1)}, bf16[576,128]{1,0:T(8,128)(2,1)S(1)}, u32[]{:S(2)}, u32[]{:S(2)}) collective-permute-start(bf16[576,128]{1,0:T(8,128)(2,1)S(1)} %get-tuple-element.38), channel_id=1, source_target_pairs={{1,2},{2,1},{3,4},{4,3},{5,6},{6,5},{7,8},{8,7},{9,10},{10,9},{11,... | collective-permute-start | bytes 442376 | tf_op jit(solution)/shard_map/ppermute | solution.py:520
  21.7 8.6 %collective-permute-start.6 = (bf16[576,128]{1,0:T(8,128)(2,1)S(1)}, bf16[576,128]{1,0:T(8,128)(2,1)S(1)}, u32[]{:S(2)}, u32[]{:S(2)}) collective-permute-start(bf16[576,128]{1,0:T(8,128)(2,1)S(1)} %get-tuple-element.39), channel_id=1, source_target_pairs={{0,1},{1,0},{2,3},{3,2},{4,5},{5,4},{6,7},{7,6},{8,9},{9,8},{10,11... | collective-permute-start | bytes 442376 | tf_op jit(solution)/shard_map/ppermute | solution.py:521
  27.8 2.4 %collective-permute-start.4 = (bf16[8,1152]{1,0:T(8,128)(2,1)S(1)}, bf16[8,1152]{1,0:T(8,128)(2,1)S(1)}, u32[]{:S(2)}, u32[]{:S(2)}) collective-permute-start(bf16[8,1152]{1,0:T(8,128)(2,1)S(1)} %get-tuple-element.37), channel_id=1, source_target_pairs={{63,64},{64,63},{127,128},{128,127},{191,192},{192,191}} | collective-permute-start | bytes 55304 | tf_op jit(solution)/shard_map/ppermute | solution.py:519
  30.3 36.3 %all-to-all-start = ((bf16[64,56,128]{2,1,0:T(8,128)(2,1)}), bf16[64,56,128]{2,1,0:T(8,128)(2,1)S(1)}, u32[]{:S(2)}, u32[]{:S(2)}) async-start(bf16[64,56,128]{2,1,0:T(8,128)(2,1)} %pack.1), calls=%async_computation | async-start | bytes 1835008 | tf_op jit(solution)/shard_map/all_to_all | solution.py:572
  66.6 20.8 %all-to-all-start.1 = ((bf16[64,8,256]{2,1,0:T(8,128)(2,1)}), bf16[64,8,256]{2,1,0:T(8,128)(2,1)S(1)}, u32[]{:S(2)}, u32[]{:S(2)}) async-start(bf16[64,8,256]{2,1,0:T(8,128)(2,1)} %bitcast.8), calls=%async_computation.1 | async-start | bytes 524288 | tf_op jit(solution)/shard_map/all_to_all | solution.py:592
  74.3 2.6 %collective-permute-start.7 = (f32[8,256]{1,0:T(8,128)S(1)}, f32[8,256]{1,0:T(8,128)S(1)}, u32[]{:S(2)}, u32[]{:S(2)}) collective-permute-start(f32[8,256]{1,0:T(8,128)S(1)} %get-tuple-element.47), channel_id=1, source_target_pairs={{63,64},{64,63},{127,128},{128,127},{191,192},{192,191}} | collective-permute-start | bytes 24584 | tf_op jit(solution)/shard_map/ppermute | solution.py:591

commit v9 on v8

--- a/solution.py
+++ b/solution.py
@@ -196,6 +196,30 @@
     return [folded(t) for t in totals]
 
 
+def contracted_rows(a_ref, wide_ref, k, ib, g, columns):
+    totals = [[None] * 8 for _ in columns]
+    for pair in range(TILE // 16):
+        j = slice(16 * pair, 16 * (pair + 1))
+        a = []
+        for i in range(8):
+            low, high = 16 * ib + i, 16 * ib + 8 + i
+            if g < 2:
+                part = a_ref[k, high if g else low, j, 0:128].astype(F32)
+            else:
+                part = jnp.concatenate(
+                    [a_ref[k, row, j, 128:ROWS].astype(F32) for row in (low, high)], 1
+                )
+            a.append(part)
+        for half in (0, 1):
+            rows = slice(16 * pair + 8 * half, 16 * pair + 8 * half + 8)
+            for n, column in enumerate(columns):
+                x = wide_ref[g // 2, k, column, rows, :]
+                for i in range(8):
+                    term = a[i][8 * half : 8 * half + 8] * x
+                    totals[n][i] = term if totals[n][i] is None else totals[n][i] + term
+    return [folded(t) for t in totals]
+
+
 def ungrouped(out_ref, index):
     low, high, both = out_ref[0, index], out_ref[1, index], out_ref[2, index]
     top = jnp.concatenate([low, both[:, :TILE]], 1)
@@ -272,7 +296,7 @@
 
 def smooth_kernel(
     me_ref, order_l_ref, order_s_ref, mid_ref, scale_ref, local_ref, outer_ref, on_ref, away_ref, near_ref, back_ref,
-    s_ref, far_out, away_out, near_out, group_ref, wide_ref, out_ref,
+    s_ref, far_out, away_out, near_out, wide_ref, out_ref,
 ):
     ib = pl.program_id(0)
     me = me_ref[0]
@@ -285,20 +309,14 @@
         wide_ref[...] += local_ref[...]
         s_ref[6:12] = mid_ref[...]
 
-    set_groups(outer_ref, ib, group_ref)
-
-    def one_group(g, carry):
-        tile = jnp.where(g == 2, 1, 0)
+    for g in range(3):
         scale = 0.0 - scale_ref[ib, g]
         for k in range(2):
-            for half in (0, 1):
-                columns = [3 * half + c for c in range(3)]
-                sums = contracted(group_ref, wide_ref, g, tile, [(k, 0)], columns)
-                for c, total in zip(columns, sums):
-                    out_ref[g, 6 * k + c] = scale * total
-        return carry
-
-    lax.fori_loop(0, 3, one_group, 0, unroll=True)
+            columns = list(range(6))
+            sums = contracted_rows(outer_ref, wide_ref, k, ib, g, columns)
+            for c, total in zip(columns, sums):
+                out_ref[g, 6 * k + c] = scale * total
+
     rows = pl.ds(pl.multiple_of(16 * ib, 16), 16)
     for index in range(12):
         s_ref[index if index < 6 else index + 6, rows, :] = ungrouped(out_ref, index).astype(BF16)
@@ -560,7 +578,7 @@
         (me, order_l, order_s, *parts, *got),
         grid=grid,
         in_specs={6: pl.BlockSpec(memory_space=pltpu.VMEM)},
-        scratch=[a_scratch(2)[2], pltpu.VMEM(local.shape, F32), pltpu.VMEM((3, 12, 8, 128), F32)],
+        scratch=[pltpu.VMEM(local.shape, F32), pltpu.VMEM((3, 12, 8, 128), F32)],
         flops=10**9,
         mib=46,
         name="smooth",

time: 88.8 us -> 88.6 us (level)
  no operation moved by 1% of the time
where the time goes in v9:
time: 88.6 us; the launch traced here: 88.2 us
  starting transfers between devices  36.5 us (41%)
  Pallas kernels  35.9 us (41%)
  waiting for transfers between devices  13.4 us (15%)
  local copies, waits for them, and re-layouts  1.6 us (2%)
    pallas_call x7, Pallas kernels, call(): pl.pallas_call(kernel, grid=(1,) if grid is None else grid, in_specs=spec...  35.9 us
    all_to_all x1, starting transfers between devices, per_device(): lax.all_to_all(packed, 'member', split_axis=0, concat_axis=0, tiled=True)  10.9 us
    all_to_all x1, waiting for transfers between devices, per_device(): lax.all_to_all(sums.reshape(MEMBERS, SLOTS, WIDE), 'member', split_axis=0...  10.6 us
    all_to_all x1, starting transfers between devices, per_device(): lax.all_to_all(sums.reshape(MEMBERS, SLOTS, WIDE), 'member', split_axis=0...  7.66 us
    ppermute x1, starting transfers between devices, per_device(): near = lax.ppermute(near, axes, near_pairs)  7.19 us
    ppermute x1, starting transfers between devices, exchanged(): return (far, away, lax.ppermute(near, axes, near_pairs))  6.12 us
    all_to_all x1, waiting for transfers between devices, per_device(): lax.all_to_all(packed, 'member', split_axis=0, concat_axis=0, tiled=True)  2.78 us
    ppermute x1, starting transfers between devices, per_device(): away = lax.ppermute(away, axes, away_pairs)  1.95 us
  transfers between devices with their start and end apart: 10, of which 2 were waited for; matrix products, arithmetic and copies ran while one was open for 0% of the time, Pallas kernels for 33%

profile of v9, /device:TPU:3, one launch (start us, length us, event | category | flops | bytes accessed | tf_op | source)
XLA Modules:
  0.0 88.2 jit_solution(3917126826903250462)
XLA Ops:
  0.6 0.0 copy-start
  0.6 0.9 %copy-done = bf16[192,6,64]{0,2,1:T(8,128)(2,1)S(1)} copy-done((bf16[192,6,64]{0,2,1:T(8,128)(2,1)S(1)}, bf16[192,6,64]{0,2,1:T(8,128)(2,1)}, u32[]{:S(2)}) %copy-start) | copy-done | bytes 147480
  1.6 0.0 copy-start.1
  1.6 0.7 copy-done.1
  2.2 0.8 rims.1
  3.0 0.7 collective-permute-start
  3.7 1.9 %collective-permute-start.1 = (bf16[192,128]{1,0:T(8,128)(2,1)S(1)}, bf16[192,128]{1,0:T(8,128)(2,1)S(1)}, u32[]{:S(2)}, u32[]{:S(2)}) collective-permute-start(bf16[192,128]{1,0:T(8,128)(2,1)S(1)} %get-tuple-element.33), channel_id=1, source_target_pairs={{1,2},{2,1},{3,4},{4,3},{5,6},{6,5},{7,8},{8,7},{9,10},{10,9},{11,... | collective-permute-start | bytes 147464 | tf_op jit(solution)/shard_map/ppermute | solution.py:552
  5.6 7.2 %collective-permute-start.2 = (bf16[192,128]{1,0:T(8,128)(2,1)S(1)}, bf16[192,128]{1,0:T(8,128)(2,1)S(1)}, u32[]{:S(2)}, u32[]{:S(2)}) collective-permute-start(bf16[192,128]{1,0:T(8,128)(2,1)S(1)} %get-tuple-element.34), channel_id=1, source_target_pairs={{0,1},{1,0},{2,3},{3,2},{4,5},{5,4},{6,7},{7,6},{8,9},{9,8},{10,11... | collective-permute-start | bytes 147464 | tf_op jit(solution)/shard_map/ppermute | solution.py:553
  12.8 0.7 collective-permute-start.3
  13.5 3.0 %middle.1 = (bf16[6,64,192]{2,1,0:T(8,128)(2,1)S(1)}, f32[4,3,8,128]{3,2,1,0:T(8,128)S(1)}, f32[2,2,6,64,128]{4,3,2,1,0:T(8,128)S(1)}, bf16[2,64,64,192]{3,2,1,0:T(8,128)(2,1)S(1)}) custom-call(f32[8,256]{1,0:T(8,128)S(1)} %get-tuple-element.25.order_l_ref, f32[192,128]{1,0:T(8,128)S(1)} %get-tuple-element.26.order_s_ref, bf16[3,64,64,192]{3,2,1,0:T(8,128)(2,1)} %bitcast.17, ...), custom_call_target="tpu_custom_call" | custom-call | flops 1000000000 | bytes 9101312 | tf_op jit(solution)/shard_map/middle/pallas_call | solution.py:494
  16.5 0.0 collective-permute-done.on_ref
  16.5 0.0 collective-permute-done.1.away_ref
  16.5 0.0 collective-permute-done.2.near_ref
  16.6 0.0 collective-permute-done.3.back_ref
  16.6 4.8 %smooth.1 = (bf16[18,64,192]{2,1,0:T(8,128)(2,1)S(1)}, bf16[8,1152]{1,0:T(8,128)(2,1)S(1)}, bf16[576,128]{1,0:T(8,128)(2,1)S(1)}, bf16[576,128]{1,0:T(8,128)(2,1)S(1)}) custom-call(s32[1]{0:T(128)} %bitcast.me_ref, f32[8,256]{1,0:T(8,128)S(1)} %get-tuple-element.25.order_l_ref, f32[192,128]{1,0:T(8,128)S(1)} %get-tuple-element.26.order_s_ref, ...), custom_call_target="tpu_custom_call" | custom-call | flops 1000000000 | bytes 5148676 | tf_op jit(solution)/shard_map/smooth/pallas_call | solution.py:494
  21.4 0.0 collective-permute-start.5
  21.4 6.1 %collective-permute-start.6 = (bf16[576,128]{1,0:T(8,128)(2,1)S(1)}, bf16[576,128]{1,0:T(8,128)(2,1)S(1)}, u32[]{:S(2)}, u32[]{:S(2)}) collective-permute-start(bf16[576,128]{1,0:T(8,128)(2,1)S(1)} %get-tuple-element.39), channel_id=1, source_target_pairs={{0,1},{1,0},{2,3},{3,2},{4,5},{5,4},{6,7},{7,6},{8,9},{9,8},{10,11... | collective-permute-start | bytes 442376 | tf_op jit(solution)/shard_map/ppermute | solution.py:539
  27.5 0.7 collective-permute-start.4
  28.2 1.8 %pack.1 = bf16[64,56,128]{2,1,0:T(8,128)(2,1)} custom-call(f32[8,256]{1,0:T(8,128)S(1)} %get-tuple-element.25.order_l_ref, bf16[1152,192]{1,0:T(8,128)(2,1)S(1)} %bitcast.13), custom_call_target="tpu_custom_call" | custom-call | bytes 1368064 | tf_op jit(solution)/shard_map/pack/pallas_call | solution.py:494
  30.0 0.0 collective-permute-done.4.far_ref
  30.0 0.0 collective-permute-done.5.away_ref
  30.0 0.0 collective-permute-done.6.near_ref
  30.0 10.9 %all-to-all-start = ((bf16[64,56,128]{2,1,0:T(8,128)(2,1)}), bf16[64,56,128]{2,1,0:T(8,128)(2,1)S(1)}, u32[]{:S(2)}, u32[]{:S(2)}) async-start(bf16[64,56,128]{2,1,0:T(8,128)(2,1)} %pack.1), calls=%async_computation | async-start | bytes 1835008 | tf_op jit(solution)/shard_map/all_to_all | solution.py:590
  40.9 22.6 %product.1 = (bf16[512,256]{1,0:T(8,128)(2,1)}, f32[8,256]{1,0:T(8,128)S(1)}) custom-call(s32[1]{0:T(128)} %bitcast.me_ref, f32[8,256]{1,0:T(8,128)S(1)} %get-tuple-element.25.order_l_ref, f32[192,128]{1,0:T(8,128)S(1)} %get-tuple-element.26.order_s_ref, bf16[3,64,64,192]{3,2,1,0:T(8,128)(2,1)} %bitcast.18, bf16[1152,192]{1,0:T(8,128)(2,1)S(1)} %bitcast.14, ...), custom_call_target="tpu_custom_call" | custom-call | flops 10000000000 | bytes 5851140 | tf_op jit(solution)/shard_map/product/pallas_call | solution.py:494
  63.5 2.8 %all-to-all-done.recv_ref = bf16[64,56,128]{2,1,0:T(8,128)(2,1)S(1)} async-done(((bf16[64,56,128]{2,1,0:T(8,128)(2,1)}), bf16[64,56,128]{2,1,0:T(8,128)(2,1)S(1)}, u32[]{:S(2)}, u32[]{:S(2)}) %all-to-all-start) | async-done | bytes 917536 | tf_op jit(solution)/shard_map/all_to_all | solution.py:590
  66.3 7.7 %all-to-all-start.1 = ((bf16[64,8,256]{2,1,0:T(8,128)(2,1)}), bf16[64,8,256]{2,1,0:T(8,128)(2,1)S(1)}, u32[]{:S(2)}, u32[]{:S(2)}) async-start(bf16[64,8,256]{2,1,0:T(8,128)(2,1)} %bitcast.8), calls=%async_computation.1 | async-start | bytes 524288 | tf_op jit(solution)/shard_map/all_to_all | solution.py:610
  74.0 0.7 collective-permute-start.7
  74.7 1.9 %unpack_smooth.1 = (bf16[1152,192]{1,0:T(8,128)(2,1)}, bf16[192,512]{1,0:T(8,128)(2,1)S(1)}) custom-call(bf16[64,56,128]{2,1,0:T(8,128)(2,1)S(1)} %all-to-all-done.recv_ref), custom_call_target="tpu_custom_call" | custom-call | flops 1000000000 | bytes 1556480 | tf_op jit(solution)/shard_map/unpack_smooth/pallas_call | solution.py:494
  76.5 0.0 collective-permute-done.7.far_ref
  76.5 10.6 %all-to-all-done.1 = bf16[64,8,256]{2,1,0:T(8,128)(2,1)S(1)} async-done(((bf16[64,8,256]{2,1,0:T(8,128)(2,1)}), bf16[64,8,256]{2,1,0:T(8,128)(2,1)S(1)}, u32[]{:S(2)}, u32[]{:S(2)}) %all-to-all-start.1) | async-done | bytes 262176 | tf_op jit(solution)/shard_map/all_to_all | solution.py:610
  87.2 1.0 %unpack_coarse.1 = f32[192,252]{1,0:T(8,128)} custom-call(s32[1]{0:T(128)} %bitcast.me_ref, bf16[192,512]{1,0:T(8,128)(2,1)S(1)} %get-tuple-element.42.pick_ref, bf16[512,256]{1,0:T(8,128)(2,1)S(1)} %bitcast.12, f32[8,256]{1,0:T(8,128)S(1)} %collective-permute-done.7.far_ref), custom_call_target="tpu_custom_call" | custom-call | bytes 660484 | tf_op jit(solution)/shard_map/unpack_coarse/pallas_call | solution.py:494
Async XLA Ops:
  0.6 0.9 %copy-start = (bf16[192,6,64]{0,2,1:T(8,128)(2,1)S(1)}, bf16[192,6,64]{0,2,1:T(8,128)(2,1)}, u32[]{:S(2)}) copy-start(bf16[192,6,64]{0,2,1:T(8,128)(2,1)} %param.4) | copy-start | bytes 442372
  1.6 0.7 copy-start.1
  3.0 13.5 %collective-permute-start = (bf16[8,384]{1,0:T(8,128)(2,1)S(1)}, bf16[8,384]{1,0:T(8,128)(2,1)S(1)}, u32[]{:S(2)}, u32[]{:S(2)}) collective-permute-start(bf16[8,384]{1,0:T(8,128)(2,1)S(1)} %get-tuple-element.32), channel_id=1, source_target_pairs={{63,64},{127,128},{191,192}} | collective-permute-start | bytes 18440 | tf_op jit(solution)/shard_map/ppermute | solution.py:551
  3.7 12.8 %collective-permute-start.1 = (bf16[192,128]{1,0:T(8,128)(2,1)S(1)}, bf16[192,128]{1,0:T(8,128)(2,1)S(1)}, u32[]{:S(2)}, u32[]{:S(2)}) collective-permute-start(bf16[192,128]{1,0:T(8,128)(2,1)S(1)} %get-tuple-element.33), channel_id=1, source_target_pairs={{1,2},{2,1},{3,4},{4,3},{5,6},{6,5},{7,8},{8,7},{9,10},{10,9},{11,... | collective-permute-start | bytes 147464 | tf_op jit(solution)/shard_map/ppermute | solution.py:552
  5.6 10.9 %collective-permute-start.2 = (bf16[192,128]{1,0:T(8,128)(2,1)S(1)}, bf16[192,128]{1,0:T(8,128)(2,1)S(1)}, u32[]{:S(2)}, u32[]{:S(2)}) collective-permute-start(bf16[192,128]{1,0:T(8,128)(2,1)S(1)} %get-tuple-element.34), channel_id=1, source_target_pairs={{0,1},{1,0},{2,3},{3,2},{4,5},{5,4},{6,7},{7,6},{8,9},{9,8},{10,11... | collective-permute-start | bytes 147464 | tf_op jit(solution)/shard_map/ppermute | solution.py:553
  12.8 3.7 %collective-permute-start.3 = (bf16[8,3328]{1,0:T(8,128)(2,1)S(1)}, bf16[8,3328]{1,0:T(8,128)(2,1)S(1)}, u32[]{:S(2)}, u32[]{:S(2)}) collective-permute-start(bf16[8,3328]{1,0:T(8,128)(2,1)S(1)} %get-tuple-element.35), channel_id=1, source_target_pairs={{64,63},{128,127},{192,191}} | collective-permute-start | bytes 159752 | tf_op jit(solution)/shard_map/ppermute | solution.py:554
  21.4 8.6 %collective-permute-start.5 = (bf16[576,128]{1,0:T(8,128)(2,1)S(1)}, bf16[576,128]{1,0:T(8,128)(2,1)S(1)}, u32[]{:S(2)}, u32[]{:S(2)}) collective-permute-start(bf16[576,128]{1,0:T(8,128)(2,1)S(1)} %get-tuple-element.38), channel_id=1, source_target_pairs={{1,2},{2,1},{3,4},{4,3},{5,6},{6,5},{7,8},{8,7},{9,10},{10,9},{11,... | collective-permute-start | bytes 442376 | tf_op jit(solution)/shard_map/ppermute | solution.py:538
  21.4 8.6 %collective-permute-start.6 = (bf16[576,128]{1,0:T(8,128)(2,1)S(1)}, bf16[576,128]{1,0:T(8,128)(2,1)S(1)}, u32[]{:S(2)}, u32[]{:S(2)}) collective-permute-start(bf16[576,128]{1,0:T(8,128)(2,1)S(1)} %get-tuple-element.39), channel_id=1, source_target_pairs={{0,1},{1,0},{2,3},{3,2},{4,5},{5,4},{6,7},{7,6},{8,9},{9,8},{10,11... | collective-permute-start | bytes 442376 | tf_op jit(solution)/shard_map/ppermute | solution.py:539
  27.5 2.4 %collective-permute-start.4 = (bf16[8,1152]{1,0:T(8,128)(2,1)S(1)}, bf16[8,1152]{1,0:T(8,128)(2,1)S(1)}, u32[]{:S(2)}, u32[]{:S(2)}) collective-permute-start(bf16[8,1152]{1,0:T(8,128)(2,1)S(1)} %get-tuple-element.37), channel_id=1, source_target_pairs={{63,64},{64,63},{127,128},{128,127},{191,192},{192,191}} | collective-permute-start | bytes 55304 | tf_op jit(solution)/shard_map/ppermute | solution.py:537
  30.0 36.3 %all-to-all-start = ((bf16[64,56,128]{2,1,0:T(8,128)(2,1)}), bf16[64,56,128]{2,1,0:T(8,128)(2,1)S(1)}, u32[]{:S(2)}, u32[]{:S(2)}) async-start(bf16[64,56,128]{2,1,0:T(8,128)(2,1)} %pack.1), calls=%async_computation | async-start | bytes 1835008 | tf_op jit(solution)/shard_map/all_to_all | solution.py:590
  66.3 20.8 %all-to-all-start.1 = ((bf16[64,8,256]{2,1,0:T(8,128)(2,1)}), bf16[64,8,256]{2,1,0:T(8,128)(2,1)S(1)}, u32[]{:S(2)}, u32[]{:S(2)}) async-start(bf16[64,8,256]{2,1,0:T(8,128)(2,1)} %bitcast.8), calls=%async_computation.1 | async-start | bytes 524288 | tf_op jit(solution)/shard_map/all_to_all | solution.py:610
  74.0 2.6 %collective-permute-start.7 = (f32[8,256]{1,0:T(8,128)S(1)}, f32[8,256]{1,0:T(8,128)S(1)}, u32[]{:S(2)}, u32[]{:S(2)}) collective-permute-start(f32[8,256]{1,0:T(8,128)S(1)} %get-tuple-element.47), channel_id=1, source_target_pairs={{63,64},{64,63},{127,128},{128,127},{191,192},{192,191}} | collective-permute-start | bytes 24584 | tf_op jit(solution)/shard_map/ppermute | solution.py:609

commit v10 on v9

--- a/solution.py
+++ b/solution.py
@@ -101,9 +101,9 @@
     return ones_where(head), ones_where(tail)
 
 
-def rims_of(rows, r, me):
+def rims_of(rows, r, me, picks):
     half = rows.shape[0] // 2
-    top, bottom = rim_picks(r, me)
+    top, bottom = picks
     rims = [(dot(rows[:half], a) + dot(rows[half:], b)).astype(BF16) for a, b in zip(top, bottom)]
     head, tail = far_pick(r, me, ROWS)
     far = lax.dot_general(head + tail, rows, NT, preferred_element_type=F32).astype(BF16)
@@ -227,7 +227,7 @@
     return jnp.concatenate([top, bottom], 0)
 
 
-def first_kernel(me_ref, owner_ref, p_ref, wide_ref, tall_ref, p_out, back_out, far_out, away_out, near_out):
+def first_kernel(me_ref, owner_ref, p_ref, wide_ref, tall_ref, p_out, picks_out, back_out, far_out, away_out, near_out):
     rows, columns = rank_arrays(owner_ref[...])
     p_out[...] = p_ref[...]
     wide_ref[...] = jnp.zeros_like(wide_ref)
@@ -236,7 +236,10 @@
     lane = iota((ROWS, 128), 1)
     tall_ref[...] = jnp.where(lane == 0, columns[0], jnp.where(lane == 1, columns[1], columns[2]))
     r = Order(wide_ref, tall_ref)
-    for ref, rim in zip((far_out, away_out, near_out), rims_of(p_ref[...], r, me_ref[0])):
+    picks = rim_picks(r, me_ref[0])
+    for n in range(4):
+        picks_out[n] = picks[n // 2][n % 2]
+    for ref, rim in zip((far_out, away_out, near_out), rims_of(p_ref[...], r, me_ref[0], picks)):
         ref[...] = rim
     back_out[...] = jnp.zeros_like(back_out)
     back_out[:, : MODES * TILE] = far_out[...]
@@ -295,7 +298,7 @@
 
 
 def smooth_kernel(
-    me_ref, order_l_ref, order_s_ref, mid_ref, scale_ref, local_ref, outer_ref, on_ref, away_ref, near_ref, back_ref,
+    me_ref, order_l_ref, order_s_ref, picks_ref, mid_ref, scale_ref, local_ref, outer_ref, on_ref, away_ref, near_ref, back_ref,
     s_ref, far_out, away_out, near_out, wide_ref, out_ref,
 ):
     ib = pl.program_id(0)
@@ -324,8 +327,9 @@
     @pl.when(ib == pl.num_programs(0) - 1)
     def _():
         r = Order(order_l_ref, order_s_ref)
+        picks = (picks_ref[0], picks_ref[1]), (picks_ref[2], picks_ref[3])
         flat = s_ref[...].reshape(COLS, ROWS)
-        for ref, rim in zip((far_out, away_out, near_out), rims_of(flat, r, me)):
+        for ref, rim in zip((far_out, away_out, near_out), rims_of(flat, r, me, picks)):
             ref[...] = rim
 
 
@@ -541,9 +545,9 @@
     def rims(length):
         return [shaped((8, length)), shaped((length // 2, 128)), shaped((length // 2, 128))]
 
-    order_l, order_s, p, back, *sent = call(
+    order_l, order_s, p, picks, back, *sent = call(
         first_kernel,
-        [shaped((8, WIDE), F32), shaped((ROWS, 128), F32), shaped(p.shape), shaped((8, BACK))] + rims(MODES * TILE),
+        [shaped((8, WIDE), F32), shaped((ROWS, 128), F32), shaped(p.shape), shaped((4, ROWS, 128)), shaped((8, BACK))] + rims(MODES * TILE),
         (me, new_owner.reshape(1, ROWS), p),
         name="rims",
     )
@@ -575,9 +579,9 @@
     s, *sent = call(
         smooth_kernel,
         [shaped((18, TILE, ROWS))] + rims(COLS),
-        (me, order_l, order_s, *parts, *got),
+        (me, order_l, order_s, picks, *parts, *got),
         grid=grid,
-        in_specs={6: pl.BlockSpec(memory_space=pltpu.VMEM)},
+        in_specs={7: pl.BlockSpec(memory_space=pltpu.VMEM)},
         scratch=[pltpu.VMEM(local.shape, F32), pltpu.VMEM((3, 12, 8, 128), F32)],
         flops=10**9,
         mib=46,

time: 88.6 us -> 88.4 us (level)
  no operation moved by 1% of the time
where the time goes in v10:
time: 88.4 us; the launch traced here: 88.1 us
  starting transfers between devices  36.5 us (41%)
  Pallas kernels  35.8 us (40%)
  waiting for transfers between devices  13.4 us (15%)
  local copies, waits for them, and re-layouts  1.6 us (2%)
    pallas_call x7, Pallas kernels, call(): pl.pallas_call(kernel, grid=(1,) if grid is None else grid, in_specs=spec...  35.8 us
    all_to_all x1, starting transfers between devices, per_device(): lax.all_to_all(packed, 'member', split_axis=0, concat_axis=0, tiled=True)  10.9 us
    all_to_all x1, waiting for transfers between devices, per_device(): lax.all_to_all(sums.reshape(MEMBERS, SLOTS, WIDE), 'member', split_axis=0...  10.6 us
    all_to_all x1, starting transfers between devices, per_device(): lax.all_to_all(sums.reshape(MEMBERS, SLOTS, WIDE), 'member', split_axis=0...  7.65 us
    ppermute x1, starting transfers between devices, per_device(): near = lax.ppermute(near, axes, near_pairs)  7.19 us
    ppermute x1, starting transfers between devices, exchanged(): return (far, away, lax.ppermute(near, axes, near_pairs))  6.13 us
    all_to_all x1, waiting for transfers between devices, per_device(): lax.all_to_all(packed, 'member', split_axis=0, concat_axis=0, tiled=True)  2.78 us
    ppermute x1, starting transfers between devices, per_device(): away = lax.ppermute(away, axes, away_pairs)  1.94 us
  transfers between devices with their start and end apart: 10, of which 2 were waited for; matrix products, arithmetic and copies ran while one was open for 0% of the time, Pallas kernels for 33%

profile of v10, /device:TPU:3, one launch (start us, length us, event | category | flops | bytes accessed | tf_op | source)
XLA Modules:
  0.0 88.1 jit_solution(3444007238864215231)
XLA Ops:
  0.6 0.0 copy-start
  0.6 0.9 %copy-done = bf16[192,6,64]{0,2,1:T(8,128)(2,1)S(1)} copy-done((bf16[192,6,64]{0,2,1:T(8,128)(2,1)S(1)}, bf16[192,6,64]{0,2,1:T(8,128)(2,1)}, u32[]{:S(2)}) %copy-start) | copy-done | bytes 147480
  1.6 0.0 copy-start.1
  1.6 0.7 copy-done.1
  2.2 0.8 rims.1
  3.0 0.7 collective-permute-start
  3.7 1.9 %collective-permute-start.1 = (bf16[192,128]{1,0:T(8,128)(2,1)S(1)}, bf16[192,128]{1,0:T(8,128)(2,1)S(1)}, u32[]{:S(2)}, u32[]{:S(2)}) collective-permute-start(bf16[192,128]{1,0:T(8,128)(2,1)S(1)} %get-tuple-element.35), channel_id=1, source_target_pairs={{1,2},{2,1},{3,4},{4,3},{5,6},{6,5},{7,8},{8,7},{9,10},{10,9},{11,... | collective-permute-start | bytes 147464 | tf_op jit(solution)/shard_map/ppermute | solution.py:556
  5.7 7.2 %collective-permute-start.2 = (bf16[192,128]{1,0:T(8,128)(2,1)S(1)}, bf16[192,128]{1,0:T(8,128)(2,1)S(1)}, u32[]{:S(2)}, u32[]{:S(2)}) collective-permute-start(bf16[192,128]{1,0:T(8,128)(2,1)S(1)} %get-tuple-element.36), channel_id=1, source_target_pairs={{0,1},{1,0},{2,3},{3,2},{4,5},{5,4},{6,7},{7,6},{8,9},{9,8},{10,11... | collective-permute-start | bytes 147464 | tf_op jit(solution)/shard_map/ppermute | solution.py:557
  12.8 0.7 collective-permute-start.3
  13.5 3.0 %middle.1 = (bf16[6,64,192]{2,1,0:T(8,128)(2,1)S(1)}, f32[4,3,8,128]{3,2,1,0:T(8,128)S(1)}, f32[2,2,6,64,128]{4,3,2,1,0:T(8,128)S(1)}, bf16[2,64,64,192]{3,2,1,0:T(8,128)(2,1)S(1)}) custom-call(f32[8,256]{1,0:T(8,128)S(1)} %get-tuple-element.26.order_l_ref, f32[192,128]{1,0:T(8,128)S(1)} %get-tuple-element.27.order_s_ref, bf16[3,64,64,192]{3,2,1,0:T(8,128)(2,1)} %bitcast.17, ...), custom_call_target="tpu_custom_call" | custom-call | flops 1000000000 | bytes 9101312 | tf_op jit(solution)/shard_map/middle/pallas_call | solution.py:498
  16.5 0.0 collective-permute-done.on_ref
  16.5 0.0 collective-permute-done.1.away_ref
  16.6 0.0 collective-permute-done.2.near_ref
  16.6 0.0 collective-permute-done.3.back_ref
  16.6 4.6 %smooth.1 = (bf16[18,64,192]{2,1,0:T(8,128)(2,1)S(1)}, bf16[8,1152]{1,0:T(8,128)(2,1)S(1)}, bf16[576,128]{1,0:T(8,128)(2,1)S(1)}, bf16[576,128]{1,0:T(8,128)(2,1)S(1)}) custom-call(s32[1]{0:T(128)} %bitcast.me_ref, f32[8,256]{1,0:T(8,128)S(1)} %get-tuple-element.26.order_l_ref, f32[192,128]{1,0:T(8,128)S(1)} %get-tuple-element.27.order_s_ref, ...), custom_call_target="tpu_custom_call" | custom-call | flops 1000000000 | bytes 5345284 | tf_op jit(solution)/shard_map/smooth/pallas_call | solution.py:498
  21.2 0.0 collective-permute-start.5
  21.3 6.1 %collective-permute-start.6 = (bf16[576,128]{1,0:T(8,128)(2,1)S(1)}, bf16[576,128]{1,0:T(8,128)(2,1)S(1)}, u32[]{:S(2)}, u32[]{:S(2)}) collective-permute-start(bf16[576,128]{1,0:T(8,128)(2,1)S(1)} %get-tuple-element.41), channel_id=1, source_target_pairs={{0,1},{1,0},{2,3},{3,2},{4,5},{5,4},{6,7},{7,6},{8,9},{9,8},{10,11... | collective-permute-start | bytes 442376 | tf_op jit(solution)/shard_map/ppermute | solution.py:543
  27.4 0.7 collective-permute-start.4
  28.0 1.8 %pack.1 = bf16[64,56,128]{2,1,0:T(8,128)(2,1)} custom-call(f32[8,256]{1,0:T(8,128)S(1)} %get-tuple-element.26.order_l_ref, bf16[1152,192]{1,0:T(8,128)(2,1)S(1)} %bitcast.13), custom_call_target="tpu_custom_call" | custom-call | bytes 1368064 | tf_op jit(solution)/shard_map/pack/pallas_call | solution.py:498
  29.8 0.0 collective-permute-done.4.far_ref
  29.8 0.0 collective-permute-done.5.away_ref
  29.8 0.0 collective-permute-done.6.near_ref
  29.8 10.9 %all-to-all-start = ((bf16[64,56,128]{2,1,0:T(8,128)(2,1)}), bf16[64,56,128]{2,1,0:T(8,128)(2,1)S(1)}, u32[]{:S(2)}, u32[]{:S(2)}) async-start(bf16[64,56,128]{2,1,0:T(8,128)(2,1)} %pack.1), calls=%async_computation | async-start | bytes 1835008 | tf_op jit(solution)/shard_map/all_to_all | solution.py:594
  40.8 22.6 %product.1 = (bf16[512,256]{1,0:T(8,128)(2,1)}, f32[8,256]{1,0:T(8,128)S(1)}) custom-call(s32[1]{0:T(128)} %bitcast.me_ref, f32[8,256]{1,0:T(8,128)S(1)} %get-tuple-element.26.order_l_ref, f32[192,128]{1,0:T(8,128)S(1)} %get-tuple-element.27.order_s_ref, bf16[3,64,64,192]{3,2,1,0:T(8,128)(2,1)} %bitcast.18, bf16[1152,192]{1,0:T(8,128)(2,1)S(1)} %bitcast.14, ...), custom_call_target="tpu_custom_call" | custom-call | flops 10000000000 | bytes 5851140 | tf_op jit(solution)/shard_map/product/pallas_call | solution.py:498
  63.4 2.8 %all-to-all-done.recv_ref = bf16[64,56,128]{2,1,0:T(8,128)(2,1)S(1)} async-done(((bf16[64,56,128]{2,1,0:T(8,128)(2,1)}), bf16[64,56,128]{2,1,0:T(8,128)(2,1)S(1)}, u32[]{:S(2)}, u32[]{:S(2)}) %all-to-all-start) | async-done | bytes 917536 | tf_op jit(solution)/shard_map/all_to_all | solution.py:594
  66.2 7.7 %all-to-all-start.1 = ((bf16[64,8,256]{2,1,0:T(8,128)(2,1)}), bf16[64,8,256]{2,1,0:T(8,128)(2,1)S(1)}, u32[]{:S(2)}, u32[]{:S(2)}) async-start(bf16[64,8,256]{2,1,0:T(8,128)(2,1)} %bitcast.8), calls=%async_computation.1 | async-start | bytes 524288 | tf_op jit(solution)/shard_map/all_to_all | solution.py:614
  73.8 0.7 collective-permute-start.7
  74.5 1.9 %unpack_smooth.1 = (bf16[1152,192]{1,0:T(8,128)(2,1)}, bf16[192,512]{1,0:T(8,128)(2,1)S(1)}) custom-call(bf16[64,56,128]{2,1,0:T(8,128)(2,1)S(1)} %all-to-all-done.recv_ref), custom_call_target="tpu_custom_call" | custom-call | flops 1000000000 | bytes 1556480 | tf_op jit(solution)/shard_map/unpack_smooth/pallas_call | solution.py:498
  76.4 0.0 collective-permute-done.7.far_ref
  76.4 10.6 %all-to-all-done.1 = bf16[64,8,256]{2,1,0:T(8,128)(2,1)S(1)} async-done(((bf16[64,8,256]{2,1,0:T(8,128)(2,1)}), bf16[64,8,256]{2,1,0:T(8,128)(2,1)S(1)}, u32[]{:S(2)}, u32[]{:S(2)}) %all-to-all-start.1) | async-done | bytes 262176 | tf_op jit(solution)/shard_map/all_to_all | solution.py:614
  87.0 1.0 %unpack_coarse.1 = f32[192,252]{1,0:T(8,128)} custom-call(s32[1]{0:T(128)} %bitcast.me_ref, bf16[192,512]{1,0:T(8,128)(2,1)S(1)} %get-tuple-element.44.pick_ref, bf16[512,256]{1,0:T(8,128)(2,1)S(1)} %bitcast.12, f32[8,256]{1,0:T(8,128)S(1)} %collective-permute-done.7.far_ref), custom_call_target="tpu_custom_call" | custom-call | bytes 660484 | tf_op jit(solution)/shard_map/unpack_coarse/pallas_call | solution.py:498
Async XLA Ops:
  0.6 0.9 %copy-start = (bf16[192,6,64]{0,2,1:T(8,128)(2,1)S(1)}, bf16[192,6,64]{0,2,1:T(8,128)(2,1)}, u32[]{:S(2)}) copy-start(bf16[192,6,64]{0,2,1:T(8,128)(2,1)} %param.4) | copy-start | bytes 442372
  1.6 0.7 copy-start.1
  3.0 13.5 %collective-permute-start = (bf16[8,384]{1,0:T(8,128)(2,1)S(1)}, bf16[8,384]{1,0:T(8,128)(2,1)S(1)}, u32[]{:S(2)}, u32[]{:S(2)}) collective-permute-start(bf16[8,384]{1,0:T(8,128)(2,1)S(1)} %get-tuple-element.34), channel_id=1, source_target_pairs={{63,64},{127,128},{191,192}} | collective-permute-start | bytes 18440 | tf_op jit(solution)/shard_map/ppermute | solution.py:555
  3.7 12.8 %collective-permute-start.1 = (bf16[192,128]{1,0:T(8,128)(2,1)S(1)}, bf16[192,128]{1,0:T(8,128)(2,1)S(1)}, u32[]{:S(2)}, u32[]{:S(2)}) collective-permute-start(bf16[192,128]{1,0:T(8,128)(2,1)S(1)} %get-tuple-element.35), channel_id=1, source_target_pairs={{1,2},{2,1},{3,4},{4,3},{5,6},{6,5},{7,8},{8,7},{9,10},{10,9},{11,... | collective-permute-start | bytes 147464 | tf_op jit(solution)/shard_map/ppermute | solution.py:556
  5.7 10.9 %collective-permute-start.2 = (bf16[192,128]{1,0:T(8,128)(2,1)S(1)}, bf16[192,128]{1,0:T(8,128)(2,1)S(1)}, u32[]{:S(2)}, u32[]{:S(2)}) collective-permute-start(bf16[192,128]{1,0:T(8,128)(2,1)S(1)} %get-tuple-element.36), channel_id=1, source_target_pairs={{0,1},{1,0},{2,3},{3,2},{4,5},{5,4},{6,7},{7,6},{8,9},{9,8},{10,11... | collective-permute-start | bytes 147464 | tf_op jit(solution)/shard_map/ppermute | solution.py:557
  12.8 3.7 %collective-permute-start.3 = (bf16[8,3328]{1,0:T(8,128)(2,1)S(1)}, bf16[8,3328]{1,0:T(8,128)(2,1)S(1)}, u32[]{:S(2)}, u32[]{:S(2)}) collective-permute-start(bf16[8,3328]{1,0:T(8,128)(2,1)S(1)} %get-tuple-element.37), channel_id=1, source_target_pairs={{64,63},{128,127},{192,191}} | collective-permute-start | bytes 159752 | tf_op jit(solution)/shard_map/ppermute | solution.py:558
  21.2 8.6 %collective-permute-start.5 = (bf16[576,128]{1,0:T(8,128)(2,1)S(1)}, bf16[576,128]{1,0:T(8,128)(2,1)S(1)}, u32[]{:S(2)}, u32[]{:S(2)}) collective-permute-start(bf16[576,128]{1,0:T(8,128)(2,1)S(1)} %get-tuple-element.40), channel_id=1, source_target_pairs={{1,2},{2,1},{3,4},{4,3},{5,6},{6,5},{7,8},{8,7},{9,10},{10,9},{11,... | collective-permute-start | bytes 442376 | tf_op jit(solution)/shard_map/ppermute | solution.py:542
  21.3 8.6 %collective-permute-start.6 = (bf16[576,128]{1,0:T(8,128)(2,1)S(1)}, bf16[576,128]{1,0:T(8,128)(2,1)S(1)}, u32[]{:S(2)}, u32[]{:S(2)}) collective-permute-start(bf16[576,128]{1,0:T(8,128)(2,1)S(1)} %get-tuple-element.41), channel_id=1, source_target_pairs={{0,1},{1,0},{2,3},{3,2},{4,5},{5,4},{6,7},{7,6},{8,9},{9,8},{10,11... | collective-permute-start | bytes 442376 | tf_op jit(solution)/shard_map/ppermute | solution.py:543
  27.4 2.4 %collective-permute-start.4 = (bf16[8,1152]{1,0:T(8,128)(2,1)S(1)}, bf16[8,1152]{1,0:T(8,128)(2,1)S(1)}, u32[]{:S(2)}, u32[]{:S(2)}) collective-permute-start(bf16[8,1152]{1,0:T(8,128)(2,1)S(1)} %get-tuple-element.39), channel_id=1, source_target_pairs={{63,64},{64,63},{127,128},{128,127},{191,192},{192,191}} | collective-permute-start | bytes 55304 | tf_op jit(solution)/shard_map/ppermute | solution.py:541
  29.8 36.3 %all-to-all-start = ((bf16[64,56,128]{2,1,0:T(8,128)(2,1)}), bf16[64,56,128]{2,1,0:T(8,128)(2,1)S(1)}, u32[]{:S(2)}, u32[]{:S(2)}) async-start(bf16[64,56,128]{2,1,0:T(8,128)(2,1)} %pack.1), calls=%async_computation | async-start | bytes 1835008 | tf_op jit(solution)/shard_map/all_to_all | solution.py:594
  66.2 20.8 %all-to-all-start.1 = ((bf16[64,8,256]{2,1,0:T(8,128)(2,1)}), bf16[64,8,256]{2,1,0:T(8,128)(2,1)S(1)}, u32[]{:S(2)}, u32[]{:S(2)}) async-start(bf16[64,8,256]{2,1,0:T(8,128)(2,1)} %bitcast.8), calls=%async_computation.1 | async-start | bytes 524288 | tf_op jit(solution)/shard_map/all_to_all | solution.py:614
  73.8 2.6 %collective-permute-start.7 = (f32[8,256]{1,0:T(8,128)S(1)}, f32[8,256]{1,0:T(8,128)S(1)}, u32[]{:S(2)}, u32[]{:S(2)}) collective-permute-start(f32[8,256]{1,0:T(8,128)S(1)} %get-tuple-element.49), channel_id=1, source_target_pairs={{63,64},{64,63},{127,128},{128,127},{191,192},{192,191}} | collective-permute-start | bytes 24584 | tf_op jit(solution)/shard_map/ppermute | solution.py:613
